TPU v7x, 256 devices: a whole 4x4x8 slice. The times are simulated.
256 devices in a mesh: row: 8 (over x, core), col: 32 (over z, y).
Axes of the slice: x: 4, y: 4, z: 8, core: 2. Of those that a mesh axis runs over, the one named last changes fastest.
Arguments:
- density: bfloat16 [256, 16, 128, 128], P(('row', 'col')), as said below
- cols: int32 [256, 16], replicated, may hold values from 0 to 255, as said below
Outputs:
- new_density: float32 [256, 16, 128, 128], P(('row', 'col'))
Inputs may be any that keep to these rules, and one draw needn't show every extreme that they name: Block row b is held by the device with row index (b) // 32 and col index q = (b) % 32. cols[b, 0] = b and a row's entries are distinct. For 1 <= t <= 7, cols[b, 2t - 1] is held by a device of col index q + t and cols[b, 2t] by one of col index q - t (modulo 32); cols[b, 15] by one of col index q + 16. The pattern is symmetric with mirrored slots: if j = cols[b, s] then cols[j, s'] = b, where s' = s for s = 0 and s = 15, s' = s + 1 for odd s below 15, and s' = s - 1 for even s above 0. density[b, s] is exactly the transpose of density[cols[b, s], s'], with s' the mirrored slot.
All inputs are finite; a program needn't handle non-finite values.
Results may differ from a plain program's by a relative error of at most 0.0093.
Values may be sent and summed in bfloat16 or wider, within the bound.
No kernel may reach another device: no remote copies, remote signals or barrier semaphores. Data moves between devices by JAX's collectives and lax.ppermute only.
A program may use at most 128 MiB of HBM per device.

v0:
```python
import jax
import jax.numpy as jnp
from jax import lax
from jax.sharding import PartitionSpec as P


def shifted(value, axis, by):
    length = lax.axis_size(axis)
    return lax.ppermute(value, axis, [(i, (i + by) % length) for i in range(length)])


def slot_offsets(slot_count, grid_cols):
    offsets = [0]
    for stride in range(1, (slot_count - 2) // 2 + 1):
        offsets = offsets + [stride, -stride]
    return offsets + [grid_cols // 2]


def mirror_slots(slot_count):
    order = [0]
    for stride in range(1, (slot_count - 2) // 2 + 1):
        order = order + [2 * stride, 2 * stride - 1]
    return order + [slot_count - 1]


def per_device(density, cols):
    rows_here = density.shape[0]
    slot_count = density.shape[1]
    grid_cols = lax.axis_size("col")
    my_row = lax.axis_index("row")
    my_col = lax.axis_index("col")
    offsets = slot_offsets(slot_count, grid_cols)
    mirror = jnp.array(mirror_slots(slot_count), jnp.int32)
    shift_ids = jnp.array(offsets, jnp.int32)
    local_ids = jnp.arange(rows_here, dtype=jnp.int32)
    slot_ids = jnp.arange(slot_count, dtype=jnp.int32)
    source_col = (my_col - shift_ids) % grid_cols
    tile_rows = (my_row * grid_cols + source_col)[:, None] * rows_here + local_ids[None, :]
    left_cols = cols[tile_rows]
    targets = left_cols[slot_ids[:, None], local_ids[None, :], slot_ids[:, None]]
    target_cols = cols[targets]
    matches = left_cols[..., :, None] == target_cols[..., None, :]
    present = jnp.any(matches, axis=-1)
    found_slot = jnp.sum(jnp.where(matches, slot_ids, 0), axis=-1)
    target_rank = targets // rows_here // grid_cols * rows_here + targets % rows_here
    present_mask = present[..., None, None]
    gathered = lax.all_gather(density, "col", axis=0, tiled=True)
    left_blocks = gathered[source_col[:, None] * rows_here + local_ids[None, :]]
    column_blocks = lax.all_gather(density, "row", axis=0, tiled=True)
    right_blocks = column_blocks[target_rank[:, :, None], found_slot]
    right_blocks = jnp.where(present_mask, right_blocks, jnp.zeros((), right_blocks.dtype))
    square_tile = jnp.einsum(
        "sltab,sltcb->slac", left_blocks, right_blocks, preferred_element_type=jnp.float32
    )
    square_half = square_tile.astype(jnp.bfloat16)
    square_panel = lax.all_gather(square_half[None], "row", axis=0, tiled=True)
    inner_row = left_cols // rows_here // grid_cols
    inner_local = left_cols % rows_here
    from_square = square_panel[inner_row, mirror[found_slot], inner_local]
    from_square = jnp.where(present_mask, from_square, jnp.zeros((), from_square.dtype))
    cube_tile = jnp.einsum(
        "sltab,sltbc->slac", left_blocks, from_square, preferred_element_type=jnp.float32
    )
    new_tiles = 3.0 * square_tile - 2.0 * cube_tile
    returned_pieces = []
    for position, stride in enumerate(offsets):
        if stride == 0:
            returned_pieces.append(new_tiles[position])
        else:
            returned_pieces.append(shifted(new_tiles[position], "col", -stride))
    return jnp.stack(returned_pieces, axis=1)


def solution(mesh):
    in_specs = (P(("row", "col"), None, None, None), P())
    out_specs = P(("row", "col"), None, None, None)
    return jax.shard_map(
        per_device, mesh=mesh, in_specs=in_specs, out_specs=out_specs, check_vma=False
    )
```

profile of v0, /device:TPU:2, one launch (start us, length us, event | category | flops | bytes accessed | tf_op | source)
XLA Modules:
  0.0 310.0 jit_solution(2974334684125972960)
XLA Ops:
  6.5 0.7 all-gather.7.cloned.1.call-update
  7.3 0.7 all-gather.5.cloned.1.call-update
  8.1 0.8 copy.11
  8.9 0.7 compare_select_fusion.6
  12.5 33.3 %all-gather.7.cloned.1.call-done = bf16[8,16,128,128]{3,2,1,0:T(8,128)(2,1)} async-done(((bf16[1,16,128,128]{3,2,1,0:T(8,128)(2,1)}), bf16[8,16,128,128]{3,2,1,0:T(8,128)(2,1)}) %all-gather.7.cloned.1.call-update) | async-done | bytes 4194320 | tf_op jit(solution)/shard_map/all_gather | solution.py:49
  45.8 12.2 %gather_fusion.4 = bf16[256,128,128]{2,1,0:T(8,128)(2,1)} fusion(bf16[8,16,128,128]{3,2,1,0:T(8,128)(2,1)} %all-gather.7.cloned.1.call-done, s32[256]{0:T(256)S(1)} %reshape.430), kind=kCustom, calls=%fused_computation.4 | custom fusion | bytes 16779264 | tf_op jit(solution)/shard_map/gather | solution.py:50
  58.0 132.1 %all-gather.5.cloned.1.call-done = bf16[32,16,128,128]{3,2,1,0:T(8,128)(2,1)} async-done(((bf16[1,16,128,128]{3,2,1,0:T(8,128)(2,1)}), bf16[32,16,128,128]{3,2,1,0:T(8,128)(2,1)}) %all-gather.5.cloned.1.call-update) | async-done | bytes 16777232 | tf_op jit(solution)/shard_map/all_gather | solution.py:47
  190.1 10.6 %gather_fusion = bf16[16,16,128,128]{3,2,1,0:T(8,128)(2,1)} fusion(bf16[32,16,128,128]{3,2,1,0:T(8,128)(2,1)} %all-gather.5.cloned.1.call-done, s32[1024]{0:T(1024)S(1)} %pad_clamp_fusion.3), kind=kCustom, calls=%fused_computation | custom fusion | bytes 16777280 | tf_op jit(solution)/shard_map/gather | solution.py:48
  200.6 9.0 %fusion.38 = (bf16[16,128,128]{2,1,0:T(8,128)(2,1)}, f32[16,128,128]{2,1,0:T(8,128)S(1)}) fusion(bf16[16,16,128,128]{3,2,1,0:T(8,128)(2,1)} %gather_fusion, bf16[16,16,128,128]{3,2,1,0:T(8,128)(2,1)} %bitcast.90, pred[16,16]{1,0:T(8,128)(4,1)S(1)} %compare_reduce_fusion), kind=kOutput, calls=%fused_computation.88 | convolution fusion | flops 1078198272 | bytes 18350336 | tf_op jit(solution)/shard_map/sltab,sltcb->slac/dot_general | solution.py:52
  209.7 1.9 gather_fusion.5
  211.8 28.7 %all-gather.9.cloned.1.call-done = bf16[128,128,128]{2,1,0:T(8,128)(2,1)} async-done(((bf16[16,128,128]{2,1,0:T(8,128)(2,1)}), bf16[128,128,128]{2,1,0:T(8,128)(2,1)}) %all-gather.9.cloned.1.call-update) | async-done | bytes 4194320 | tf_op jit(solution)/shard_map/all_gather | solution.py:56
  240.5 12.3 %gather_fusion.6 = bf16[256,128,128]{2,1,0:T(8,128)(2,1)} fusion(bf16[8,16,1,128,128]{4,3,1,0,2:T(8,128)(2,1)} %bitcast.89, s32[256]{0:T(256)S(1)} %reshape.446), kind=kCustom, calls=%fused_computation.6 | custom fusion | bytes 16780288 | tf_op jit(solution)/shard_map/gather | solution.py:59
  252.8 8.2 %fusion.17 = f32[16,128,128]{2,1,0:T(8,128)S(1)} fusion(bf16[16,16,128,128]{3,2,1,0:T(8,128)(2,1)} %gather_fusion, bf16[16,16,128,128]{3,2,1,0:T(8,128)(2,1)} %bitcast.91, pred[16,16]{1,0:T(8,128)(4,1)S(1)} %compare_reduce_fusion, f32[16,128,128]{2,1,0:T(8,128)S(1)} %get-tuple-element.23), kind=kOutput, calls=%fused_computation.18 | convolution fusion | flops 1078722560 | bytes 18874624 | tf_op jit(solution)/shard_map/sltab,sltbc->slac/dot_general | solution.py:61
  261.1 5.7 %collective-permute-start = (f32[1,128,128]{2,1,0:T(8,128)S(1)}, f32[1,128,128]{2,1,0:T(8,128)S(1)}, u32[]{:S(2)}, u32[]{:S(2)}) collective-permute-start(f32[1,128,128]{2,1,0:T(8,128)S(1)} %get-tuple-element.21), channel_id=1, source_target_pairs={{0,31},{1,0},{2,1},{3,2},{4,3},{5,4},{6,5},{7,6},{8,7},{9,8},{10,9... | collective-permute-start | bytes 196616 | tf_op jit(solution)/shard_map/ppermute | solution.py:9
  266.8 2.3 collective-permute-start.2
  269.1 1.3 collective-permute-start.3
  270.4 2.6 collective-permute-start.4
  273.7 0.8 collective-permute-done.1
  274.5 4.0 %collective-permute-start.6 = (f32[1,128,128]{2,1,0:T(8,128)S(1)}, f32[1,128,128]{2,1,0:T(8,128)S(1)}, u32[]{:S(2)}, u32[]{:S(2)}) collective-permute-start(f32[1,128,128]{2,1,0:T(8,128)S(1)} %get-tuple-element.15), channel_id=1, source_target_pairs={{0,28},{1,29},{2,30},{3,31},{4,0},{5,1},{6,2},{7,3},{8,4},{9,5},{1... | collective-permute-start | bytes 196616 | tf_op jit(solution)/shard_map/ppermute | solution.py:9
  278.6 5.1 %collective-permute-start.8 = (f32[1,128,128]{2,1,0:T(8,128)S(1)}, f32[1,128,128]{2,1,0:T(8,128)S(1)}, u32[]{:S(2)}, u32[]{:S(2)}) collective-permute-start(f32[1,128,128]{2,1,0:T(8,128)S(1)} %get-tuple-element.13), channel_id=1, source_target_pairs={{0,27},{1,28},{2,29},{3,30},{4,31},{5,0},{6,1},{7,2},{8,3},{9,4},{... | collective-permute-start | bytes 196616 | tf_op jit(solution)/shard_map/ppermute | solution.py:9
  283.8 4.2 %collective-permute-start.10 = (f32[1,128,128]{2,1,0:T(8,128)S(1)}, f32[1,128,128]{2,1,0:T(8,128)S(1)}, u32[]{:S(2)}, u32[]{:S(2)}) collective-permute-start(f32[1,128,128]{2,1,0:T(8,128)S(1)} %get-tuple-element.11), channel_id=1, source_target_pairs={{0,26},{1,27},{2,28},{3,29},{4,30},{5,31},{6,0},{7,1},{8,2},{9,3},... | collective-permute-start | bytes 196616 | tf_op jit(solution)/shard_map/ppermute | solution.py:9
  288.4 5.4 %collective-permute-start.12 = (f32[1,128,128]{2,1,0:T(8,128)S(1)}, f32[1,128,128]{2,1,0:T(8,128)S(1)}, u32[]{:S(2)}, u32[]{:S(2)}) collective-permute-start(f32[1,128,128]{2,1,0:T(8,128)S(1)} %get-tuple-element.9), channel_id=1, source_target_pairs={{0,25},{1,26},{2,27},{3,28},{4,29},{5,30},{6,31},{7,0},{8,1},{9,2}... | collective-permute-start | bytes 196616 | tf_op jit(solution)/shard_map/ppermute | solution.py:9
  294.0 3.0 collective-permute-start.14
  297.0 4.9 %collective-permute-done.13 = f32[1,128,128]{2,1,0:T(8,128)S(1)} collective-permute-done((f32[1,128,128]{2,1,0:T(8,128)S(1)}, f32[1,128,128]{2,1,0:T(8,128)S(1)}, u32[]{:S(2)}, u32[]{:S(2)}) %collective-permute-start.13) | collective-permute-done | bytes 65568 | tf_op jit(solution)/shard_map/ppermute | solution.py:9
  (72 shorter events, 6.4 us)
Async XLA Ops:
  6.5 39.3 %all-gather.7.cloned.1.call-start = ((), (), s32[]{:S(2)}) async-start(), calls=%async_computation.1 | async-start | bytes 4718592 | tf_op jit(solution)/shard_map/all_gather | solution.py:49
  7.3 182.8 %all-gather.5.cloned.1.call-start = ((), (), s32[]{:S(2)}) async-start(), calls=%async_computation | async-start | bytes 17301504 | tf_op jit(solution)/shard_map/all_gather | solution.py:47
  8.0 232.5 %all-gather.9.cloned.1.call-start = ((), (), s32[]{:S(2)}) async-start(), calls=%async_computation.2 | async-start | bytes 4718592 | tf_op jit(solution)/shard_map/all_gather | solution.py:56
  200.6 9.1 %copy-start = (s32[16]{0:T(128)S(1)}, s32[16]{0:T(128)}, u32[]{:S(2)}) copy-start(s32[16]{0:T(128)} %constant.115.clone) | copy-start | bytes 196
  261.1 12.0 %collective-permute-start = (f32[1,128,128]{2,1,0:T(8,128)S(1)}, f32[1,128,128]{2,1,0:T(8,128)S(1)}, u32[]{:S(2)}, u32[]{:S(2)}) collective-permute-start(f32[1,128,128]{2,1,0:T(8,128)S(1)} %get-tuple-element.21), channel_id=1, source_target_pairs={{0,31},{1,0},{2,1},{3,2},{4,3},{5,4},{6,5},{7,6},{8,7},{9,8},{10,9... | collective-permute-start | bytes 196616 | tf_op jit(solution)/shard_map/ppermute | solution.py:9
  266.8 7.7 %collective-permute-start.1 = (f32[1,128,128]{2,1,0:T(8,128)S(1)}, f32[1,128,128]{2,1,0:T(8,128)S(1)}, u32[]{:S(2)}, u32[]{:S(2)}) collective-permute-start(f32[1,128,128]{2,1,0:T(8,128)S(1)} %get-tuple-element.20), channel_id=1, source_target_pairs={{0,1},{1,2},{2,3},{3,4},{4,5},{5,6},{6,7},{7,8},{8,9},{9,10},{10,1... | collective-permute-start | bytes 196616 | tf_op jit(solution)/shard_map/ppermute | solution.py:9
  266.8 11.7 %collective-permute-start.2 = (f32[1,128,128]{2,1,0:T(8,128)S(1)}, f32[1,128,128]{2,1,0:T(8,128)S(1)}, u32[]{:S(2)}, u32[]{:S(2)}) collective-permute-start(f32[1,128,128]{2,1,0:T(8,128)S(1)} %get-tuple-element.19), channel_id=1, source_target_pairs={{0,30},{1,31},{2,0},{3,1},{4,2},{5,3},{6,4},{7,5},{8,6},{9,7},{10,... | collective-permute-start | bytes 196616 | tf_op jit(solution)/shard_map/ppermute | solution.py:9
  269.1 9.5 %collective-permute-start.3 = (f32[1,128,128]{2,1,0:T(8,128)S(1)}, f32[1,128,128]{2,1,0:T(8,128)S(1)}, u32[]{:S(2)}, u32[]{:S(2)}) collective-permute-start(f32[1,128,128]{2,1,0:T(8,128)S(1)} %get-tuple-element.18), channel_id=1, source_target_pairs={{0,2},{1,3},{2,4},{3,5},{4,6},{5,7},{6,8},{7,9},{8,10},{9,11},{10,... | collective-permute-start | bytes 196616 | tf_op jit(solution)/shard_map/ppermute | solution.py:9
  270.4 13.3 %collective-permute-start.4 = (f32[1,128,128]{2,1,0:T(8,128)S(1)}, f32[1,128,128]{2,1,0:T(8,128)S(1)}, u32[]{:S(2)}, u32[]{:S(2)}) collective-permute-start(f32[1,128,128]{2,1,0:T(8,128)S(1)} %get-tuple-element.17), channel_id=1, source_target_pairs={{0,29},{1,30},{2,31},{3,0},{4,1},{5,2},{6,3},{7,4},{8,5},{9,6},{10... | collective-permute-start | bytes 196616 | tf_op jit(solution)/shard_map/ppermute | solution.py:9
  273.0 10.8 %collective-permute-start.5 = (f32[1,128,128]{2,1,0:T(8,128)S(1)}, f32[1,128,128]{2,1,0:T(8,128)S(1)}, u32[]{:S(2)}, u32[]{:S(2)}) collective-permute-start(f32[1,128,128]{2,1,0:T(8,128)S(1)} %get-tuple-element.16), channel_id=1, source_target_pairs={{0,3},{1,4},{2,5},{3,6},{4,7},{5,8},{6,9},{7,10},{8,11},{9,12},{10... | collective-permute-start | bytes 196616 | tf_op jit(solution)/shard_map/ppermute | solution.py:9
  274.5 13.5 %collective-permute-start.6 = (f32[1,128,128]{2,1,0:T(8,128)S(1)}, f32[1,128,128]{2,1,0:T(8,128)S(1)}, u32[]{:S(2)}, u32[]{:S(2)}) collective-permute-start(f32[1,128,128]{2,1,0:T(8,128)S(1)} %get-tuple-element.15), channel_id=1, source_target_pairs={{0,28},{1,29},{2,30},{3,31},{4,0},{5,1},{6,2},{7,3},{8,4},{9,5},{1... | collective-permute-start | bytes 196616 | tf_op jit(solution)/shard_map/ppermute | solution.py:9
  278.5 10.0 %collective-permute-start.7 = (f32[1,128,128]{2,1,0:T(8,128)S(1)}, f32[1,128,128]{2,1,0:T(8,128)S(1)}, u32[]{:S(2)}, u32[]{:S(2)}) collective-permute-start(f32[1,128,128]{2,1,0:T(8,128)S(1)} %get-tuple-element.14), channel_id=1, source_target_pairs={{0,4},{1,5},{2,6},{3,7},{4,8},{5,9},{6,10},{7,11},{8,12},{9,13},{1... | collective-permute-start | bytes 196616 | tf_op jit(solution)/shard_map/ppermute | solution.py:9
  278.6 15.2 %collective-permute-start.8 = (f32[1,128,128]{2,1,0:T(8,128)S(1)}, f32[1,128,128]{2,1,0:T(8,128)S(1)}, u32[]{:S(2)}, u32[]{:S(2)}) collective-permute-start(f32[1,128,128]{2,1,0:T(8,128)S(1)} %get-tuple-element.13), channel_id=1, source_target_pairs={{0,27},{1,28},{2,29},{3,30},{4,31},{5,0},{6,1},{7,2},{8,3},{9,4},{... | collective-permute-start | bytes 196616 | tf_op jit(solution)/shard_map/ppermute | solution.py:9
  283.7 10.2 %collective-permute-start.9 = (f32[1,128,128]{2,1,0:T(8,128)S(1)}, f32[1,128,128]{2,1,0:T(8,128)S(1)}, u32[]{:S(2)}, u32[]{:S(2)}) collective-permute-start(f32[1,128,128]{2,1,0:T(8,128)S(1)} %get-tuple-element.12), channel_id=1, source_target_pairs={{0,5},{1,6},{2,7},{3,8},{4,9},{5,10},{6,11},{7,12},{8,13},{9,14},{... | collective-permute-start | bytes 196616 | tf_op jit(solution)/shard_map/ppermute | solution.py:9
  283.8 13.1 %collective-permute-start.10 = (f32[1,128,128]{2,1,0:T(8,128)S(1)}, f32[1,128,128]{2,1,0:T(8,128)S(1)}, u32[]{:S(2)}, u32[]{:S(2)}) collective-permute-start(f32[1,128,128]{2,1,0:T(8,128)S(1)} %get-tuple-element.11), channel_id=1, source_target_pairs={{0,26},{1,27},{2,28},{3,29},{4,30},{5,31},{6,0},{7,1},{8,2},{9,3},... | collective-permute-start | bytes 196616 | tf_op jit(solution)/shard_map/ppermute | solution.py:9
  288.0 9.0 %collective-permute-start.11 = (f32[1,128,128]{2,1,0:T(8,128)S(1)}, f32[1,128,128]{2,1,0:T(8,128)S(1)}, u32[]{:S(2)}, u32[]{:S(2)}) collective-permute-start(f32[1,128,128]{2,1,0:T(8,128)S(1)} %get-tuple-element.10), channel_id=1, source_target_pairs={{0,6},{1,7},{2,8},{3,9},{4,10},{5,11},{6,12},{7,13},{8,14},{9,15},... | collective-permute-start | bytes 196616 | tf_op jit(solution)/shard_map/ppermute | solution.py:9
  288.4 8.6 %collective-permute-start.12 = (f32[1,128,128]{2,1,0:T(8,128)S(1)}, f32[1,128,128]{2,1,0:T(8,128)S(1)}, u32[]{:S(2)}, u32[]{:S(2)}) collective-permute-start(f32[1,128,128]{2,1,0:T(8,128)S(1)} %get-tuple-element.9), channel_id=1, source_target_pairs={{0,25},{1,26},{2,27},{3,28},{4,29},{5,30},{6,31},{7,0},{8,1},{9,2}... | collective-permute-start | bytes 196616 | tf_op jit(solution)/shard_map/ppermute | solution.py:9
  293.8 8.1 %collective-permute-start.13 = (f32[1,128,128]{2,1,0:T(8,128)S(1)}, f32[1,128,128]{2,1,0:T(8,128)S(1)}, u32[]{:S(2)}, u32[]{:S(2)}) collective-permute-start(f32[1,128,128]{2,1,0:T(8,128)S(1)} %get-tuple-element.8), channel_id=1, source_target_pairs={{0,7},{1,8},{2,9},{3,10},{4,11},{5,12},{6,13},{7,14},{8,15},{9,16}... | collective-permute-start | bytes 196616 | tf_op jit(solution)/shard_map/ppermute | solution.py:9
  294.0 8.3 %collective-permute-start.14 = (f32[1,128,128]{2,1,0:T(8,128)S(1)}, f32[1,128,128]{2,1,0:T(8,128)S(1)}, u32[]{:S(2)}, u32[]{:S(2)}) collective-permute-start(f32[1,128,128]{2,1,0:T(8,128)S(1)} %get-tuple-element.7), channel_id=1, source_target_pairs={{0,16},{1,17},{2,18},{3,19},{4,20},{5,21},{6,22},{7,23},{8,24},{9,... | collective-permute-start | bytes 196616 | tf_op jit(solution)/shard_map/ppermute | solution.py:9
  301.9 1.0 copy-start.1
Sparse Core Ops, SparseCore 0:
  9.2 36.5 all-gather.6
  48.4 141.5 all-gather.4
  209.8 30.6 all-gather.8
where the time goes:
time: 314 us; the launch traced here: 310 us
  waiting for transfers between devices  202 us (64%)
  local copies, waits for them, and re-layouts  41.3 us (13%)
  starting transfers between devices  34.9 us (11%)
  matrix products  17.2 us (5%)
  between operations  13.4 us (4%)
    all_gather x1, waiting for transfers between devices, per_device(): gathered = lax.all_gather(density, 'col', axis=0, tiled=True)  132 us
    ppermute x15, starting transfers between devices, shifted(): lax.ppermute(value, axis, [(i, (i + by) % length) for i in range(length)])  34.8 us
    all_gather x1, waiting for transfers between devices, per_device(): column_blocks = lax.all_gather(density, 'row', axis=0, tiled=True)  33.3 us
    all_gather x1, waiting for transfers between devices, per_device(): square_panel = lax.all_gather(square_half[None], 'row', axis=0, tiled=True)  28.7 us
    gather x3, local copies, waits for them, and re-layouts, per_device(): from_square = square_panel[inner_row, mirror[found_slot], inner_local]  14.2 us
    gather x1, local copies, waits for them, and re-layouts, per_device(): right_blocks = column_blocks[target_rank[:, :, None], found_slot]  12.2 us
    gather x1, local copies, waits for them, and re-layouts, per_device(): left_blocks = gathered[source_col[:, None] * rows_here + local_ids[None, :]]  10.6 us
    dot_general x1, matrix products, per_device(): jnp.einsum('sltab,sltcb->slac', left_blocks, right_blocks, preferred_elem...  9 us
  transfers between devices with their start and end apart: 18, of which 6 were waited for; matrix products, arithmetic and copies ran while one was open for 6% of the time, Pallas kernels for 0%

commit v1 on v0

v1 whole, which is shorter than its diff:
```python
import functools

import jax
import jax.numpy as jnp
from jax import lax
from jax.experimental import pallas as pl
from jax.experimental.pallas import tpu as pltpu
from jax.sharding import PartitionSpec as P

SIGNS = {1: 1, 2: 1, 3: -1, 4: 1, 5: 1, 6: -1, 7: -1}


class Plan:
    def __init__(self, slot_count, grid_cols, grid_rows):
        half = (slot_count - 2) // 2
        self.slot_count, self.grid_cols, self.grid_rows = slot_count, grid_cols, grid_rows
        self.far = grid_cols // 2
        self.offsets = [0]
        for stride in range(1, half + 1):
            self.offsets += [stride, -stride]
        self.offsets.append(self.far)
        self.slot = {o: s for s, o in enumerate(self.offsets)}
        self.tiles = [0] + [SIGNS.get(d, 1) * d for d in range(1, half + 1)] + [self.far]
        self.tile = {d: t for t, d in enumerate(self.tiles)}
        near = [o for o in self.offsets if o not in (0, self.far)]
        self.left = {self.far: []}
        for d in self.tiles[1:-1]:
            self.left[d] = [a for a in near if a != d and self.near(a - d)]
        self.edges = {self.far: []}
        for a in near:
            self.edges[a] = [b for b in near if b != a and (a - b) in self.tile]
        self.moved = [o for o in self.offsets if o != 0]

    def near(self, o):
        return o in self.slot and o != self.far

    def row_id(self, rank, col):
        return rank * self.grid_cols + lax.rem(col + 2 * self.grid_cols, self.grid_cols)


def shifted(value, by):
    length = lax.axis_size("col")
    return lax.ppermute(value, "col", [(i, (i + by) % length) for i in range(length)])


def nn(a, b):
    return lax.dot_general(a, b, (((1,), (0,)), ((), ())), preferred_element_type=jnp.float32)


def nt(a, b):
    return lax.dot_general(a, b, (((1,), (1,)), ((), ())), preferred_element_type=jnp.float32)


def tn(a, b):
    return lax.dot_general(a, b, (((0,), (0,)), ((), ())), preferred_element_type=jnp.float32)


def gather_rows(block):
    length = lax.axis_size("row")
    chips = length // 2
    pieces = []
    for step in range(chips):
        if step == 0:
            same = block
        else:
            same = lax.ppermute(
                block, "row",
                [(2 * x + h, 2 * ((x + step) % chips) + h) for x in range(chips) for h in range(2)],
            )
        pieces.append(same)
    out = []
    for same in pieces:
        out += [same, lax.ppermute(same, "row", [(i, i ^ 1) for i in range(length)])]
    return out


def piece_rank(plan, my_row, index):
    chips = plan.grid_rows // 2
    x = lax.rem(my_row // 2 - index // 2 + chips, chips)
    core = lax.rem(my_row, 2)
    if index % 2:
        core = 1 - core
    return 2 * x + core


def land(plan, my_row, pieces, panel, sems):
    copies = []
    for index, piece in enumerate(pieces):
        copy = pltpu.make_async_copy(piece, panel.at[piece_rank(plan, my_row, index)], sems.at[index])
        copy.start()
        copies.append(copy)
    return copies


def square_kernel(plan, *refs):
    cols, own = refs[0], refs[1]
    n_left = len(plan.tiles) - 1
    lefts = dict(zip(plan.tiles[1:], refs[2:2 + n_left]))
    pieces = refs[2 + n_left:2 + n_left + plan.grid_rows]
    out, self_square, panel, total, sems = refs[2 + n_left + plan.grid_rows:]
    n = plan.slot_count
    my_row, my_col = lax.axis_index("row"), lax.axis_index("col")
    copies = land(plan, my_row, pieces, panel, sems)
    acc = nt(own[0], own[0])
    for s in range(1, n):
        acc = acc + nt(own[s], own[s])
    self_square[...] = acc
    out[0] = acc.astype(out.dtype)
    for copy in copies:
        copy.wait()
    for t, d in enumerate(plan.tiles):
        if d == 0:
            continue
        left = lefts[d]
        i = plan.row_id(my_row, my_col - d)
        j = cols[i * n + plan.slot[d]]
        rank = j // plan.grid_cols
        back = plan.slot[-d] if d != plan.far else plan.slot[d]
        total[...] = nt(left[0], panel[rank, back]) + tn(panel[rank, back], panel[rank, 0])
        for p, a in enumerate(plan.left[d]):
            k = cols[i * n + plan.slot[a]]
            u = plan.slot[a - d]

            @pl.when(cols[j * n + u] == k)
            def _():
                total[...] += nt(left[p + 1], panel[rank, u])

        out[t] = total[...].astype(out.dtype)


def pick_kernel(plan, *refs):
    cols, own = refs[0], refs[1]
    pieces = refs[2:2 + plan.grid_rows]
    rest = refs[2 + plan.grid_rows:]
    n_out = len(plan.moved) + 1
    outs, (panel, sems) = rest[:n_out], rest[n_out:]
    n = plan.slot_count
    my_row, my_col = lax.axis_index("row"), lax.axis_index("col")
    copies = land(plan, my_row, pieces, panel, sems)
    for copy in copies:
        copy.wait()
    for out, a in zip(outs, plan.moved):
        i = plan.row_id(my_row, my_col - a)
        k = cols[i * n + plan.slot[a]]
        out[0] = panel[k // plan.grid_cols, 0]
        p = 1
        if a in plan.tile and a != plan.far:
            out[p] = own[plan.tile[a]]
            p += 1
        for b in plan.edges[a]:
            j = cols[i * n + plan.slot[b]]
            out[p] = panel[j // plan.grid_cols, plan.tile[a - b]]
            p += 1
    i = plan.row_id(my_row, my_col)
    for p, d in enumerate(plan.tiles[1:]):
        back = plan.slot[-d] if d != plan.far else plan.slot[d]
        j = cols[i * n + back]
        outs[-1][p] = panel[j // plan.grid_cols, plan.tile[d]]


def message_size(plan, a):
    return 1 + (1 if a in plan.tile and a != plan.far else 0) + len(plan.edges[a])


def cube_kernel(plan, *refs):
    cols, own, self_square, local = refs[:4]
    arrived = dict(zip(plan.moved, refs[4:4 + len(plan.moved)]))
    out = refs[4 + len(plan.moved)]
    n = plan.slot_count
    my_row, my_col = lax.axis_index("row"), lax.axis_index("col")
    i = plan.row_id(my_row, my_col)
    s_self = self_square[...]
    acc = nn(own[0], s_self.astype(own.dtype))
    for a in plan.moved:
        t = plan.slot[a]
        diagonal = arrived[a][0]
        if a in plan.tile and a != plan.far:
            s_ia = arrived[a][1]
            acc = acc + nt(own[t], s_ia)
            cube = nn(own[0], s_ia) + nn(own[t], diagonal)
            mine = s_ia.astype(jnp.float32)
        else:
            s_ai = local[plan.tile[-a if a != plan.far else a] - 1]
            acc = acc + nn(own[t], s_ai)
            cube = nt(own[0], s_ai) + nn(own[t], diagonal)
            mine = s_ai.astype(jnp.float32).T
        out[0, t] = 3.0 * mine - 2.0 * cube
    out[0, 0] = 3.0 * s_self - 2.0 * acc
    for a in plan.moved:
        p = 2 if a in plan.tile and a != plan.far else 1
        for b in plan.edges[a]:
            k, j = cols[i * n + plan.slot[a]], cols[i * n + plan.slot[b]]

            @pl.when(cols[j * n + plan.slot[a - b]] == k)
            def _():
                edge = arrived[a][p]
                ta, tb = plan.slot[a], plan.slot[b]
                out[0, tb] += -2.0 * nt(own[ta], edge)
                out[0, ta] += -2.0 * nn(own[tb], edge)

            p += 1


VMEM = pl.BlockSpec(memory_space=pltpu.VMEM)
SMEM = pl.BlockSpec(memory_space=pltpu.SMEM)
ANY = pl.BlockSpec(memory_space=pl.ANY)
PARAMS = pltpu.CompilerParams(vmem_limit_bytes=48 << 20)


def per_device(density, cols):
    slot_count, size = density.shape[1], density.shape[2]
    plan = Plan(slot_count, lax.axis_size("col"), lax.axis_size("row"))
    own = density[0]
    table = cols.reshape(-1)
    block = (size, size)
    n_tiles = len(plan.tiles)
    lefts = []
    for d in plan.tiles[1:]:
        slots = [0] + [plan.slot[a] for a in plan.left[d]]
        message = jnp.concatenate([own[s:s + 1] for s in slots], axis=0)
        lefts.append(shifted(message, d))
    panel = gather_rows(own)
    rows = plan.grid_rows
    tiles, self_square = pl.pallas_call(
        functools.partial(square_kernel, plan),
        out_shape=[
            jax.ShapeDtypeStruct((n_tiles, *block), own.dtype),
            jax.ShapeDtypeStruct(block, jnp.float32),
        ],
        in_specs=[SMEM, VMEM] + [VMEM] * len(lefts) + [ANY] * rows,
        out_specs=[VMEM, VMEM],
        scratch_shapes=[
            pltpu.VMEM((rows, slot_count, *block), own.dtype),
            pltpu.VMEM(block, jnp.float32),
            pltpu.SemaphoreType.DMA((rows,)),
        ],
        compiler_params=PARAMS,
        name="square",
    )(table, own, *lefts, *panel)
    square_panel = gather_rows(tiles)
    picked = pl.pallas_call(
        functools.partial(pick_kernel, plan),
        out_shape=[
            jax.ShapeDtypeStruct((message_size(plan, a), *block), own.dtype) for a in plan.moved
        ] + [jax.ShapeDtypeStruct((n_tiles - 1, *block), own.dtype)],
        in_specs=[SMEM, VMEM] + [ANY] * rows,
        out_specs=[VMEM] * (len(plan.moved) + 1),
        scratch_shapes=[
            pltpu.VMEM((rows, n_tiles, *block), own.dtype),
            pltpu.SemaphoreType.DMA((rows,)),
        ],
        compiler_params=PARAMS,
        name="pick",
    )(table, tiles, *square_panel)
    arrived = [shifted(m, -a) for m, a in zip(picked, plan.moved)]
    return pl.pallas_call(
        functools.partial(cube_kernel, plan),
        out_shape=jax.ShapeDtypeStruct((1, slot_count, *block), jnp.float32),
        in_specs=[SMEM, VMEM, VMEM, VMEM] + [VMEM] * len(arrived),
        out_specs=VMEM,
        compiler_params=PARAMS,
        name="cube",
    )(table, own, self_square, picked[-1], *arrived)


def solution(mesh):
    in_specs = (P(("row", "col"), None, None, None), P())
    out_specs = P(("row", "col"), None, None, None)
    return jax.shard_map(
        per_device, mesh=mesh, in_specs=in_specs, out_specs=out_specs, check_vma=False
    )
```

time: 314 us -> 194 us (0.62)
  waiting for transfers between devices: 202 us -> 96.6 us
  starting transfers between devices: 34.9 us -> 57.3 us
  matrix products: 17.2 us -> 0 us
  local copies, waits for them, and re-layouts: 41.3 us -> 25.3 us
  between operations: 13.4 us -> 0.23 us
  Pallas kernels: 0 us -> 12.2 us
    all_gather x3 -> x0, waiting for transfers between devices: 194 us -> none  [the longest x1 132 us: per_device(): gathered = lax.all_gather(density, 'col', axis=0, tiled=True)]
    ppermute x15 -> x37, waiting for transfers between devices: 6.15 us -> 96.6 us  [the longest x23 82.1 us: shifted(): lax.ppermute(value, 'col', [(i, (i + by) % length) for i in range(length)])]
    gather x8 -> x0, local copies, waits for them, and re-layouts: 38.7 us -> none  [the longest x3 14.2 us: per_device(): from_square = square_panel[inner_row, mirror[found_slot], inner_local]]
    ppermute x15 -> x37, starting transfers between devices: 34.8 us -> 57.3 us  [the longest x23 48.9 us: shifted(): lax.ppermute(value, 'col', [(i, (i + by) % length) for i in range(length)])]
    unnamed x20 -> x64, local copies, waits for them, and re-layouts: 1.51 us -> 22.2 us
    dot_general x2 -> x0, matrix products: 17.2 us -> none  [the longest x1 9 us: per_device(): jnp.einsum('sltab,sltcb->slac', left_blocks, right_blocks, preferred_elem...]
    pallas_call x0 -> x3, Pallas kernels: none -> 12.2 us  [the longest x1 5.34 us: per_device(): pl.pallas_call(functools.partial(square_kernel, plan), out_shape=[jax.Sha...]
  transfers between devices with their start and end apart: 18 -> 37, of which waited for: 6 -> 12; matrix products, arithmetic and copies ran while one was open for 6% -> 1% of each run, Pallas kernels for 0% -> 0%
where the time goes in v1:
time: 194 us; the launch traced here: 192 us
  waiting for transfers between devices  96.6 us (50%)
  starting transfers between devices  57.3 us (30%)
  local copies, waits for them, and re-layouts  25.3 us (13%)
  Pallas kernels  12.2 us (6%)
    ppermute x23, waiting for transfers between devices, shifted(): lax.ppermute(value, 'col', [(i, (i + by) % length) for i in range(length)])  82.1 us
    ppermute x23, starting transfers between devices, shifted(): lax.ppermute(value, 'col', [(i, (i + by) % length) for i in range(length)])  48.9 us
    unnamed x64, local copies, waits for them, and re-layouts  22.2 us
    ppermute x6, waiting for transfers between devices, gather_rows(): lax.ppermute(block, 'row', [(2 * x + h, 2 * ((x + step) % chips) + h) for...  13 us
    ppermute x6, starting transfers between devices, gather_rows(): lax.ppermute(block, 'row', [(2 * x + h, 2 * ((x + step) % chips) + h) for...  7.39 us
    pallas_call x1, Pallas kernels, per_device(): pl.pallas_call(functools.partial(square_kernel, plan), out_shape=[jax.Sha...  5.34 us
    pallas_call x1, Pallas kernels, per_device(): pl.pallas_call(functools.partial(cube_kernel, plan), out_shape=jax.ShapeD...  4.91 us
  transfers between devices with their start and end apart: 37, of which 12 were waited for; matrix products, arithmetic and copies ran while one was open for 1% of the time, Pallas kernels for 0%

profile of v1, /device:TPU:2, one launch (start us, length us, event | category | flops | bytes accessed | tf_op | source)
XLA Modules:
  0.0 191.7 jit_solution(4869070717783779644)
XLA Ops:
  13.7 3.0 %collective-permute-start.4 = (bf16[9,128,128]{2,1,0:T(8,128)(2,1)S(1)}, bf16[9,128,128]{2,1,0:T(8,128)(2,1)S(1)}, u32[]{:S(2)}, u32[]{:S(2)}) collective-permute-start(bf16[9,128,128]{2,1,0:T(8,128)(2,1)S(1)} %get-tuple-element.70), channel_id=1, source_target_pairs={{0,5},{1,6},{2,7},{3,8},{4,9},{5,10},{6,11},{7,12},{8,13},{9,14},{... | collective-permute-start | bytes 884744 | tf_op jit(solution)/shard_map/ppermute | solution.py:43
  16.7 7.7 %collective-permute-start.5 = (bf16[8,128,128]{2,1,0:T(8,128)(2,1)S(1)}, bf16[8,128,128]{2,1,0:T(8,128)(2,1)S(1)}, u32[]{:S(2)}, u32[]{:S(2)}) collective-permute-start(bf16[8,128,128]{2,1,0:T(8,128)(2,1)S(1)} %get-tuple-element.48), channel_id=1, source_target_pairs={{0,26},{1,27},{2,28},{3,29},{4,30},{5,31},{6,0},{7,1},{8,2},{9,3},... | collective-permute-start | bytes 786440 | tf_op jit(solution)/shard_map/ppermute | solution.py:43
  27.6 7.3 %collective-permute-done.7.refs_9_ = bf16[1,128,128]{2,1,0:T(8,128)(2,1)S(1)} collective-permute-done((bf16[1,128,128]{2,1,0:T(8,128)(2,1)S(1)}, bf16[1,128,128]{2,1,0:T(8,128)(2,1)S(1)}, u32[]{:S(2)}, u32[]{:S(2)}) %collective-permute-start.7) | collective-permute-done | bytes 32800 | tf_op jit(solution)/shard_map/ppermute | solution.py:43
  36.6 9.3 %collective-permute-done.6.refs_8_ = bf16[7,128,128]{2,1,0:T(8,128)(2,1)S(1)} collective-permute-done((bf16[7,128,128]{2,1,0:T(8,128)(2,1)S(1)}, bf16[7,128,128]{2,1,0:T(8,128)(2,1)S(1)}, u32[]{:S(2)}, u32[]{:S(2)}) %collective-permute-start.6) | collective-permute-done | bytes 229408 | tf_op jit(solution)/shard_map/ppermute | solution.py:43
  47.8 8.8 %collective-permute-start.3 = (bf16[10,128,128]{2,1,0:T(8,128)(2,1)S(1)}, bf16[10,128,128]{2,1,0:T(8,128)(2,1)S(1)}, u32[]{:S(2)}, u32[]{:S(2)}) collective-permute-start(bf16[10,128,128]{2,1,0:T(8,128)(2,1)S(1)} %get-tuple-element.77), channel_id=1, source_target_pairs={{0,4},{1,5},{2,6},{3,7},{4,8},{5,9},{6,10},{7,11},{8,12},{9,13},{1... | collective-permute-start | bytes 983048 | tf_op jit(solution)/shard_map/ppermute | solution.py:43
  57.3 3.9 %collective-permute-done.3.refs_5_ = bf16[10,128,128]{2,1,0:T(8,128)(2,1)S(1)} collective-permute-done((bf16[10,128,128]{2,1,0:T(8,128)(2,1)S(1)}, bf16[10,128,128]{2,1,0:T(8,128)(2,1)S(1)}, u32[]{:S(2)}, u32[]{:S(2)}) %collective-permute-start.3) | collective-permute-done | bytes 327712 | tf_op jit(solution)/shard_map/ppermute | solution.py:43
  62.2 12.2 %collective-permute-done.2.refs_4_ = bf16[11,128,128]{2,1,0:T(8,128)(2,1)S(1)} collective-permute-done((bf16[11,128,128]{2,1,0:T(8,128)(2,1)S(1)}, bf16[11,128,128]{2,1,0:T(8,128)(2,1)S(1)}, u32[]{:S(2)}, u32[]{:S(2)}) %collective-permute-start.2) | collective-permute-done | bytes 360480 | tf_op jit(solution)/shard_map/ppermute | solution.py:43
  77.9 13.7 %collective-permute-done.refs_2_ = bf16[13,128,128]{2,1,0:T(8,128)(2,1)} collective-permute-done((bf16[13,128,128]{2,1,0:T(8,128)(2,1)}, bf16[13,128,128]{2,1,0:T(8,128)(2,1)}, u32[]{:S(2)}, u32[]{:S(2)}) %collective-permute-start) | collective-permute-done | bytes 426016 | tf_op jit(solution)/shard_map/ppermute | solution.py:43
  97.2 5.3 %square.1 = (bf16[9,128,128]{2,1,0:T(8,128)(2,1)S(1)}, f32[128,128]{1,0:T(8,128)S(1)}) custom-call(s32[4096]{0:T(1024)S(1)} %reshape.18.refs_0_, bf16[16,128,128]{2,1,0:T(8,128)(2,1)S(1)} %bitcast.98, bf16[13,128,128]{2,1,0:T(8,128)(2,1)} %collective-permute-done.refs_2_, bf16[12,128,128]{2,1,0:T(8,128)(2,1)S(1)} %collective-permute-done.1.refs_3_, ...), custom_call_target="tpu_custom_call" | custom-call | tf_op jit(solution)/shard_map/square/pallas_call | solution.py:224
  103.4 3.4 %collective-permute-start.18 = (bf16[9,128,128]{2,1,0:T(8,128)(2,1)S(1)}, bf16[9,128,128]{2,1,0:T(8,128)(2,1)S(1)}, u32[]{:S(2)}, u32[]{:S(2)}) collective-permute-start(bf16[9,128,128]{2,1,0:T(8,128)(2,1)S(1)} %get-tuple-element.24.refs_1_.refs_2_), channel_id=1, source_target_pairs={{0,128},{32,160},{64,192},{96,224},{128,0},{160,32},{192,64},{224,... | collective-permute-start | bytes 884744 | tf_op jit(solution)/shard_map/ppermute | solution.py:66
  106.8 5.8 %collective-permute-done.16.refs_4_ = bf16[9,128,128]{2,1,0:T(8,128)(2,1)S(1)} collective-permute-done((bf16[9,128,128]{2,1,0:T(8,128)(2,1)S(1)}, bf16[9,128,128]{2,1,0:T(8,128)(2,1)S(1)}, u32[]{:S(2)}, u32[]{:S(2)}) %collective-permute-start.16) | collective-permute-done | bytes 294944 | tf_op jit(solution)/shard_map/ppermute | solution.py:66
  112.6 2.2 %collective-permute-done.18.refs_6_ = bf16[9,128,128]{2,1,0:T(8,128)(2,1)S(1)} collective-permute-done((bf16[9,128,128]{2,1,0:T(8,128)(2,1)S(1)}, bf16[9,128,128]{2,1,0:T(8,128)(2,1)S(1)}, u32[]{:S(2)}, u32[]{:S(2)}) %collective-permute-start.18) | collective-permute-done | bytes 294944 | tf_op jit(solution)/shard_map/ppermute | solution.py:66
  114.9 4.9 %collective-permute-done.20.refs_8_ = bf16[9,128,128]{2,1,0:T(8,128)(2,1)S(1)} collective-permute-done((bf16[9,128,128]{2,1,0:T(8,128)(2,1)S(1)}, bf16[9,128,128]{2,1,0:T(8,128)(2,1)S(1)}, u32[]{:S(2)}, u32[]{:S(2)}) %collective-permute-start.20) | collective-permute-done | bytes 294944 | tf_op jit(solution)/shard_map/ppermute | solution.py:66
  119.8 1.6 collective-permute-done.21.refs_9_
  121.4 2.0 %pick.1 = (bf16[7,128,128]{2,1,0:T(8,128)(2,1)S(1)}, bf16[8,128,128]{2,1,0:T(8,128)(2,1)S(1)}, bf16[6,128,128]{2,1,0:T(8,128)(2,1)S(1)}, bf16[8,128,128]{2,1,0:T...) custom-call(s32[4096]{0:T(1024)S(1)} %reshape.18.refs_0_, ...), custom_call_target="tpu_custom_call" | custom-call | tf_op jit(solution)/shard_map/pick/pallas_call | solution.py:241
  124.8 3.2 %collective-permute-start.33 = (bf16[5,128,128]{2,1,0:T(8,128)(2,1)S(1)}, bf16[5,128,128]{2,1,0:T(8,128)(2,1)S(1)}, u32[]{:S(2)}, u32[]{:S(2)}) collective-permute-start(bf16[5,128,128]{2,1,0:T(8,128)(2,1)S(1)} %get-tuple-element.37), channel_id=1, source_target_pairs={{0,6},{1,7},{2,8},{3,9},{4,10},{5,11},{6,12},{7,13},{8,14},{9,15},... | collective-permute-start | bytes 491528 | tf_op jit(solution)/shard_map/ppermute | solution.py:43
  129.1 6.8 %collective-permute-done.36.refs_18_ = bf16[1,128,128]{2,1,0:T(8,128)(2,1)S(1)} collective-permute-done((bf16[1,128,128]{2,1,0:T(8,128)(2,1)S(1)}, bf16[1,128,128]{2,1,0:T(8,128)(2,1)S(1)}, u32[]{:S(2)}, u32[]{:S(2)}) %collective-permute-start.36) | collective-permute-done | bytes 32800 | tf_op jit(solution)/shard_map/ppermute | solution.py:43
  135.9 7.5 %collective-permute-start.24 = (bf16[6,128,128]{2,1,0:T(8,128)(2,1)S(1)}, bf16[6,128,128]{2,1,0:T(8,128)(2,1)S(1)}, u32[]{:S(2)}, u32[]{:S(2)}) collective-permute-start(bf16[6,128,128]{2,1,0:T(8,128)(2,1)S(1)} %get-tuple-element.28), channel_id=1, source_target_pairs={{0,30},{1,31},{2,0},{3,1},{4,2},{5,3},{6,4},{7,5},{8,6},{9,7},{10,... | collective-permute-start | bytes 589832 | tf_op jit(solution)/shard_map/ppermute | solution.py:43
  143.4 3.6 %collective-permute-start.26 = (bf16[6,128,128]{2,1,0:T(8,128)(2,1)S(1)}, bf16[6,128,128]{2,1,0:T(8,128)(2,1)S(1)}, u32[]{:S(2)}, u32[]{:S(2)}) collective-permute-start(bf16[6,128,128]{2,1,0:T(8,128)(2,1)S(1)} %get-tuple-element.30), channel_id=1, source_target_pairs={{0,29},{1,30},{2,31},{3,0},{4,1},{5,2},{6,3},{7,4},{8,5},{9,6},{10... | collective-permute-start | bytes 589832 | tf_op jit(solution)/shard_map/ppermute | solution.py:43
  147.4 1.7 collective-permute-start.29
  149.1 10.2 %collective-permute-done.34.refs_16_ = bf16[5,128,128]{2,1,0:T(8,128)(2,1)S(1)} collective-permute-done((bf16[5,128,128]{2,1,0:T(8,128)(2,1)S(1)}, bf16[5,128,128]{2,1,0:T(8,128)(2,1)S(1)}, u32[]{:S(2)}, u32[]{:S(2)}) %collective-permute-start.34) | collective-permute-done | bytes 163872 | tf_op jit(solution)/shard_map/ppermute | solution.py:43
  161.1 4.7 %collective-permute-start.22 = (bf16[7,128,128]{2,1,0:T(8,128)(2,1)S(1)}, bf16[7,128,128]{2,1,0:T(8,128)(2,1)S(1)}, u32[]{:S(2)}, u32[]{:S(2)}) collective-permute-start(bf16[7,128,128]{2,1,0:T(8,128)(2,1)S(1)} %get-tuple-element.26), channel_id=1, source_target_pairs={{0,31},{1,0},{2,1},{3,2},{4,3},{5,4},{6,5},{7,6},{8,7},{9,8},{10,9... | collective-permute-start | bytes 688136 | tf_op jit(solution)/shard_map/ppermute | solution.py:43
  168.0 18.8 %collective-permute-done.31.refs_13_ = bf16[6,128,128]{2,1,0:T(8,128)(2,1)S(1)} collective-permute-done((bf16[6,128,128]{2,1,0:T(8,128)(2,1)S(1)}, bf16[6,128,128]{2,1,0:T(8,128)(2,1)S(1)}, u32[]{:S(2)}, u32[]{:S(2)}) %collective-permute-start.31) | collective-permute-done | bytes 196640 | tf_op jit(solution)/shard_map/ppermute | solution.py:43
  186.8 4.9 %cube.1 = f32[1,16,128,128]{3,2,1,0:T(8,128)} custom-call(s32[4096]{0:T(1024)S(1)} %reshape.18.refs_0_, bf16[16,128,128]{2,1,0:T(8,128)(2,1)S(1)} %bitcast.100, f32[128,128]{1,0:T(8,128)S(1)} %get-tuple-element.23.refs_2_, bf16[8,128,128]{2,1,0:T(8,128)(2,1)S(1)} %get-tuple-element.25.refs_3_, bf16[7,128,128]{2,1,0:T(8,128)(2,1)S(1)} %collective-permute-done.22.refs_4_, ...), custom_call_target="tpu_custom_call" | custom-call | tf_op jit(solution)/shard_map/cube/pallas_call | solution.py:256
  (125 shorter events, 39.1 us)
Async XLA Ops:
  13.7 42.9 %collective-permute-start.4 = (bf16[9,128,128]{2,1,0:T(8,128)(2,1)S(1)}, bf16[9,128,128]{2,1,0:T(8,128)(2,1)S(1)}, u32[]{:S(2)}, u32[]{:S(2)}) collective-permute-start(bf16[9,128,128]{2,1,0:T(8,128)(2,1)S(1)} %get-tuple-element.70), channel_id=1, source_target_pairs={{0,5},{1,6},{2,7},{3,8},{4,9},{5,10},{6,11},{7,12},{8,13},{9,14},{... | collective-permute-start | bytes 884744 | tf_op jit(solution)/shard_map/ppermute | solution.py:43
  16.7 30.4 %collective-permute-start.5 = (bf16[8,128,128]{2,1,0:T(8,128)(2,1)S(1)}, bf16[8,128,128]{2,1,0:T(8,128)(2,1)S(1)}, u32[]{:S(2)}, u32[]{:S(2)}) collective-permute-start(bf16[8,128,128]{2,1,0:T(8,128)(2,1)S(1)} %get-tuple-element.48), channel_id=1, source_target_pairs={{0,26},{1,27},{2,28},{3,29},{4,30},{5,31},{6,0},{7,1},{8,2},{9,3},... | collective-permute-start | bytes 786440 | tf_op jit(solution)/shard_map/ppermute | solution.py:43
  24.4 21.5 %collective-permute-start.6 = (bf16[7,128,128]{2,1,0:T(8,128)(2,1)S(1)}, bf16[7,128,128]{2,1,0:T(8,128)(2,1)S(1)}, u32[]{:S(2)}, u32[]{:S(2)}) collective-permute-start(bf16[7,128,128]{2,1,0:T(8,128)(2,1)S(1)} %get-tuple-element.41), channel_id=1, source_target_pairs={{0,25},{1,26},{2,27},{3,28},{4,29},{5,30},{6,31},{7,0},{8,1},{9,2}... | collective-permute-start | bytes 688136 | tf_op jit(solution)/shard_map/ppermute | solution.py:43
  25.4 49.7 %collective-permute-start.9 = (bf16[16,128,128]{2,1,0:T(8,128)(2,1)S(1)}, bf16[16,128,128]{2,1,0:T(8,128)(2,1)S(1)}, u32[]{:S(2)}, u32[]{:S(2)}) collective-permute-start(bf16[16,128,128]{2,1,0:T(8,128)(2,1)S(1)} %bitcast.94), channel_id=1, source_target_pairs={{0,64},{32,96},{64,128},{96,160},{128,192},{160,224},{192,0},{224,... | collective-permute-start | bytes 1572872 | tf_op jit(solution)/shard_map/ppermute | solution.py:66
  35.5 40.1 %collective-permute-start.11 = (bf16[16,128,128]{2,1,0:T(8,128)(2,1)S(1)}, bf16[16,128,128]{2,1,0:T(8,128)(2,1)S(1)}, u32[]{:S(2)}, u32[]{:S(2)}) collective-permute-start(bf16[16,128,128]{2,1,0:T(8,128)(2,1)S(1)} %bitcast.95), channel_id=1, source_target_pairs={{0,128},{32,160},{64,192},{96,224},{128,0},{160,32},{192,64},{224,... | collective-permute-start | bytes 1572872 | tf_op jit(solution)/shard_map/ppermute | solution.py:66
  46.6 29.1 %collective-permute-start.13 = (bf16[16,128,128]{2,1,0:T(8,128)(2,1)S(1)}, bf16[16,128,128]{2,1,0:T(8,128)(2,1)}, u32[]{:S(2)}, u32[]{:S(2)}) collective-permute-start(bf16[16,128,128]{2,1,0:T(8,128)(2,1)S(1)} %bitcast.96), channel_id=1, source_target_pairs={{0,192},{32,224},{64,0},{96,32},{128,64},{160,96},{192,128},{224,1... | collective-permute-start | bytes 1572872 | tf_op jit(solution)/shard_map/ppermute | solution.py:66
  57.3 17.1 %collective-permute-start.2 = (bf16[11,128,128]{2,1,0:T(8,128)(2,1)S(1)}, bf16[11,128,128]{2,1,0:T(8,128)(2,1)S(1)}, u32[]{:S(2)}, u32[]{:S(2)}) collective-permute-start(bf16[11,128,128]{2,1,0:T(8,128)(2,1)S(1)} %get-tuple-element.80), channel_id=1, source_target_pairs={{0,29},{1,30},{2,31},{3,0},{4,1},{5,2},{6,3},{7,4},{8,5},{9,6},{10... | collective-permute-start | bytes 1081352 | tf_op jit(solution)/shard_map/ppermute | solution.py:43
  75.1 16.5 %collective-permute-start.8 = (bf16[16,128,128]{2,1,0:T(8,128)(2,1)S(1)}, bf16[16,128,128]{2,1,0:T(8,128)(2,1)S(1)}, u32[]{:S(2)}, u32[]{:S(2)}) collective-permute-start(bf16[16,128,128]{2,1,0:T(8,128)(2,1)S(1)} %bitcast.97), channel_id=1, source_target_pairs={{0,32},{32,0},{64,96},{96,64},{128,160},{160,128},{192,224},{224,1... | collective-permute-start | bytes 1572872 | tf_op jit(solution)/shard_map/ppermute | solution.py:73
  75.1 16.5 %collective-permute-start.10 = (bf16[16,128,128]{2,1,0:T(8,128)(2,1)S(1)}, bf16[16,128,128]{2,1,0:T(8,128)(2,1)S(1)}, u32[]{:S(2)}, u32[]{:S(2)}) collective-permute-start(bf16[16,128,128]{2,1,0:T(8,128)(2,1)S(1)} %collective-permute-done.9.refs_12_), channel_id=1, source_target_pairs={{0,32},{32,0},{64,96},{96,64},{128,160},{160,128},{192,224},{224,1... | collective-permute-start | bytes 1572872 | tf_op jit(solution)/shard_map/ppermute | solution.py:73
  75.6 16.0 %collective-permute-start.12 = (bf16[16,128,128]{2,1,0:T(8,128)(2,1)S(1)}, bf16[16,128,128]{2,1,0:T(8,128)(2,1)S(1)}, u32[]{:S(2)}, u32[]{:S(2)}) collective-permute-start(bf16[16,128,128]{2,1,0:T(8,128)(2,1)S(1)} %collective-permute-done.11.refs_14_), channel_id=1, source_target_pairs={{0,32},{32,0},{64,96},{96,64},{128,160},{160,128},{192,224},{224,1... | collective-permute-start | bytes 1572872 | tf_op jit(solution)/shard_map/ppermute | solution.py:73
  75.7 15.9 %collective-permute-start.14 = (bf16[16,128,128]{2,1,0:T(8,128)(2,1)}, bf16[16,128,128]{2,1,0:T(8,128)(2,1)}, u32[]{:S(2)}, u32[]{:S(2)}) collective-permute-start(bf16[16,128,128]{2,1,0:T(8,128)(2,1)} %collective-permute-done.13.refs_16_), channel_id=1, source_target_pairs={{0,32},{32,0},{64,96},{96,64},{128,160},{160,128},{192,224},{224,1... | collective-permute-start | bytes 1572872 | tf_op jit(solution)/shard_map/ppermute | solution.py:73
  123.3 23.6 %collective-permute-start.30 = (bf16[5,128,128]{2,1,0:T(8,128)(2,1)S(1)}, bf16[5,128,128]{2,1,0:T(8,128)(2,1)S(1)}, u32[]{:S(2)}, u32[]{:S(2)}) collective-permute-start(bf16[5,128,128]{2,1,0:T(8,128)(2,1)S(1)} %get-tuple-element.34), channel_id=1, source_target_pairs={{0,27},{1,28},{2,29},{3,30},{4,31},{5,0},{6,1},{7,2},{8,3},{9,4},{... | collective-permute-start | bytes 491528 | tf_op jit(solution)/shard_map/ppermute | solution.py:43
  123.4 23.6 %collective-permute-start.32 = (bf16[5,128,128]{2,1,0:T(8,128)(2,1)S(1)}, bf16[5,128,128]{2,1,0:T(8,128)(2,1)S(1)}, u32[]{:S(2)}, u32[]{:S(2)}) collective-permute-start(bf16[5,128,128]{2,1,0:T(8,128)(2,1)S(1)} %get-tuple-element.36), channel_id=1, source_target_pairs={{0,26},{1,27},{2,28},{3,29},{4,30},{5,31},{6,0},{7,1},{8,2},{9,3},... | collective-permute-start | bytes 491528 | tf_op jit(solution)/shard_map/ppermute | solution.py:43
  123.5 19.9 %collective-permute-start.35 = (bf16[4,128,128]{2,1,0:T(8,128)(2,1)S(1)}, bf16[4,128,128]{2,1,0:T(8,128)(2,1)S(1)}, u32[]{:S(2)}, u32[]{:S(2)}) collective-permute-start(bf16[4,128,128]{2,1,0:T(8,128)(2,1)S(1)} %get-tuple-element.39), channel_id=1, source_target_pairs={{0,7},{1,8},{2,9},{3,10},{4,11},{5,12},{6,13},{7,14},{8,15},{9,16}... | collective-permute-start | bytes 393224 | tf_op jit(solution)/shard_map/ppermute | solution.py:43
  124.8 22.6 %collective-permute-start.33 = (bf16[5,128,128]{2,1,0:T(8,128)(2,1)S(1)}, bf16[5,128,128]{2,1,0:T(8,128)(2,1)S(1)}, u32[]{:S(2)}, u32[]{:S(2)}) collective-permute-start(bf16[5,128,128]{2,1,0:T(8,128)(2,1)S(1)} %get-tuple-element.37), channel_id=1, source_target_pairs={{0,6},{1,7},{2,8},{3,9},{4,10},{5,11},{6,12},{7,13},{8,14},{9,15},... | collective-permute-start | bytes 491528 | tf_op jit(solution)/shard_map/ppermute | solution.py:43
  135.9 24.8 %collective-permute-start.24 = (bf16[6,128,128]{2,1,0:T(8,128)(2,1)S(1)}, bf16[6,128,128]{2,1,0:T(8,128)(2,1)S(1)}, u32[]{:S(2)}, u32[]{:S(2)}) collective-permute-start(bf16[6,128,128]{2,1,0:T(8,128)(2,1)S(1)} %get-tuple-element.28), channel_id=1, source_target_pairs={{0,30},{1,31},{2,0},{3,1},{4,2},{5,3},{6,4},{7,5},{8,6},{9,7},{10,... | collective-permute-start | bytes 589832 | tf_op jit(solution)/shard_map/ppermute | solution.py:43
  143.4 17.7 %collective-permute-start.26 = (bf16[6,128,128]{2,1,0:T(8,128)(2,1)S(1)}, bf16[6,128,128]{2,1,0:T(8,128)(2,1)S(1)}, u32[]{:S(2)}, u32[]{:S(2)}) collective-permute-start(bf16[6,128,128]{2,1,0:T(8,128)(2,1)S(1)} %get-tuple-element.30), channel_id=1, source_target_pairs={{0,29},{1,30},{2,31},{3,0},{4,1},{5,2},{6,3},{7,4},{8,5},{9,6},{10... | collective-permute-start | bytes 589832 | tf_op jit(solution)/shard_map/ppermute | solution.py:43
  147.0 18.8 %collective-permute-start.28 = (bf16[6,128,128]{2,1,0:T(8,128)(2,1)S(1)}, bf16[6,128,128]{2,1,0:T(8,128)(2,1)S(1)}, u32[]{:S(2)}, u32[]{:S(2)}) collective-permute-start(bf16[6,128,128]{2,1,0:T(8,128)(2,1)S(1)} %get-tuple-element.32), channel_id=1, source_target_pairs={{0,28},{1,29},{2,30},{3,31},{4,0},{5,1},{6,2},{7,3},{8,4},{9,5},{1... | collective-permute-start | bytes 589832 | tf_op jit(solution)/shard_map/ppermute | solution.py:43
  147.4 19.7 %collective-permute-start.29 = (bf16[6,128,128]{2,1,0:T(8,128)(2,1)S(1)}, bf16[6,128,128]{2,1,0:T(8,128)(2,1)S(1)}, u32[]{:S(2)}, u32[]{:S(2)}) collective-permute-start(bf16[6,128,128]{2,1,0:T(8,128)(2,1)S(1)} %get-tuple-element.33), channel_id=1, source_target_pairs={{0,4},{1,5},{2,6},{3,7},{4,8},{5,9},{6,10},{7,11},{8,12},{9,13},{1... | collective-permute-start | bytes 589832 | tf_op jit(solution)/shard_map/ppermute | solution.py:43
  159.4 27.4 %collective-permute-start.23 = (bf16[8,128,128]{2,1,0:T(8,128)(2,1)S(1)}, bf16[8,128,128]{2,1,0:T(8,128)(2,1)S(1)}, u32[]{:S(2)}, u32[]{:S(2)}) collective-permute-start(bf16[8,128,128]{2,1,0:T(8,128)(2,1)S(1)} %get-tuple-element.27), channel_id=1, source_target_pairs={{0,1},{1,2},{2,3},{3,4},{4,5},{5,6},{6,7},{7,8},{8,9},{9,10},{10,1... | collective-permute-start | bytes 786440 | tf_op jit(solution)/shard_map/ppermute | solution.py:43
  160.6 26.1 %collective-permute-start.25 = (bf16[8,128,128]{2,1,0:T(8,128)(2,1)S(1)}, bf16[8,128,128]{2,1,0:T(8,128)(2,1)S(1)}, u32[]{:S(2)}, u32[]{:S(2)}) collective-permute-start(bf16[8,128,128]{2,1,0:T(8,128)(2,1)S(1)} %get-tuple-element.29), channel_id=1, source_target_pairs={{0,2},{1,3},{2,4},{3,5},{4,6},{5,7},{6,8},{7,9},{8,10},{9,11},{10,... | collective-permute-start | bytes 786440 | tf_op jit(solution)/shard_map/ppermute | solution.py:43
  161.1 25.7 %collective-permute-start.22 = (bf16[7,128,128]{2,1,0:T(8,128)(2,1)S(1)}, bf16[7,128,128]{2,1,0:T(8,128)(2,1)S(1)}, u32[]{:S(2)}, u32[]{:S(2)}) collective-permute-start(bf16[7,128,128]{2,1,0:T(8,128)(2,1)S(1)} %get-tuple-element.26), channel_id=1, source_target_pairs={{0,31},{1,0},{2,1},{3,2},{4,3},{5,4},{6,5},{7,6},{8,7},{9,8},{10,9... | collective-permute-start | bytes 688136 | tf_op jit(solution)/shard_map/ppermute | solution.py:43
  165.8 20.9 %collective-permute-start.27 = (bf16[7,128,128]{2,1,0:T(8,128)(2,1)S(1)}, bf16[7,128,128]{2,1,0:T(8,128)(2,1)S(1)}, u32[]{:S(2)}, u32[]{:S(2)}) collective-permute-start(bf16[7,128,128]{2,1,0:T(8,128)(2,1)S(1)} %get-tuple-element.31), channel_id=1, source_target_pairs={{0,3},{1,4},{2,5},{3,6},{4,7},{5,8},{6,9},{7,10},{8,11},{9,12},{10... | collective-permute-start | bytes 688136 | tf_op jit(solution)/shard_map/ppermute | solution.py:43
  167.1 19.7 %collective-permute-start.31 = (bf16[6,128,128]{2,1,0:T(8,128)(2,1)S(1)}, bf16[6,128,128]{2,1,0:T(8,128)(2,1)S(1)}, u32[]{:S(2)}, u32[]{:S(2)}) collective-permute-start(bf16[6,128,128]{2,1,0:T(8,128)(2,1)S(1)} %get-tuple-element.35), channel_id=1, source_target_pairs={{0,5},{1,6},{2,7},{3,8},{4,9},{5,10},{6,11},{7,12},{8,13},{9,14},{... | collective-permute-start | bytes 589832 | tf_op jit(solution)/shard_map/ppermute | solution.py:43
  (27 other events, 167.3 us)

commit v2 on v1

--- a/solution.py
+++ b/solution.py
@@ -7,7 +7,11 @@
 from jax.experimental.pallas import tpu as pltpu
 from jax.sharding import PartitionSpec as P
 
-SIGNS = {1: 1, 2: 1, 3: -1, 4: 1, 5: 1, 6: -1, 7: -1}
+SIGNS = {1: 1, 2: -1, 3: 1, 4: 1, 5: -1, 6: 1, 7: -1}
+LEFT_ORDER = [-7, -5, 4, 3, 1, -2, 16, 6]
+BACK_ORDER = [5, 6, -7, -1, -5, -3, 4, -2, 7, -4, 3, 1, 2, 16, -6]
+LEFT_WINDOW = 4
+BACK_WINDOW = 4
 
 
 class Plan:
@@ -43,6 +47,21 @@
     return lax.ppermute(value, "col", [(i, (i + by) % length) for i in range(length)])
 
 
+def in_turn(values, sends, order, window):
+    results, last = {}, []
+    for key in order:
+        value = values[key]
+        if len(last) >= window:
+            value, _ = lax.optimization_barrier((value, last[-window]))
+        results[key] = sends[key](value)
+        last.append(results[key])
+    return results
+
+
+def ordered(preferred, keys):
+    return [k for k in preferred if k in keys] + [k for k in keys if k not in preferred]
+
+
 def nn(a, b):
     return lax.dot_general(a, b, (((1,), (0,)), ((), ())), preferred_element_type=jnp.float32)
 
@@ -92,15 +111,26 @@
     return copies
 
 
+def pack_kernel(plan, own, *outs):
+    for out, d in zip(outs, plan.tiles[1:]):
+        for p, s in enumerate([0] + [plan.slot[a] for a in plan.left[d]]):
+            out[p] = own[s]
+
+
 def square_kernel(plan, *refs):
     cols, own = refs[0], refs[1]
     n_left = len(plan.tiles) - 1
-    lefts = dict(zip(plan.tiles[1:], refs[2:2 + n_left]))
     pieces = refs[2 + n_left:2 + n_left + plan.grid_rows]
-    out, self_square, panel, total, sems = refs[2 + n_left + plan.grid_rows:]
+    rest = refs[2 + n_left + plan.grid_rows:]
+    out, far_out, self_square, panel, total, sems, left_sems = rest[:7]
+    lefts = dict(zip(plan.tiles[1:], rest[7:]))
     n = plan.slot_count
     my_row, my_col = lax.axis_index("row"), lax.axis_index("col")
     copies = land(plan, my_row, pieces, panel, sems)
+    for t in range(n_left):
+        copy = pltpu.make_async_copy(refs[2 + t], rest[7 + t], left_sems.at[t])
+        copy.start()
+        copies.append(copy)
     acc = nt(own[0], own[0])
     for s in range(1, n):
         acc = acc + nt(own[s], own[s])
@@ -125,13 +155,16 @@
             def _():
                 total[...] += nt(left[p + 1], panel[rank, u])
 
-        out[t] = total[...].astype(out.dtype)
+        if d == plan.far:
+            far_out[0] = total[...].astype(out.dtype)
+        else:
+            out[t] = total[...].astype(out.dtype)
 
 
 def pick_kernel(plan, *refs):
-    cols, own = refs[0], refs[1]
-    pieces = refs[2:2 + plan.grid_rows]
-    rest = refs[2 + plan.grid_rows:]
+    cols, own, far = refs[0], refs[1], refs[2]
+    pieces = refs[3:3 + plan.grid_rows]
+    rest = refs[3 + plan.grid_rows:]
     n_out = len(plan.moved) + 1
     outs, (panel, sems) = rest[:n_out], rest[n_out:]
     n = plan.slot_count
@@ -144,7 +177,9 @@
         k = cols[i * n + plan.slot[a]]
         out[0] = panel[k // plan.grid_cols, 0]
         p = 1
-        if a in plan.tile and a != plan.far:
+        if a == plan.far:
+            out[p] = far[0]
+        elif a in plan.tile:
             out[p] = own[plan.tile[a]]
             p += 1
         for b in plan.edges[a]:
@@ -152,14 +187,13 @@
             out[p] = panel[j // plan.grid_cols, plan.tile[a - b]]
             p += 1
     i = plan.row_id(my_row, my_col)
-    for p, d in enumerate(plan.tiles[1:]):
-        back = plan.slot[-d] if d != plan.far else plan.slot[d]
-        j = cols[i * n + back]
+    for p, d in enumerate(plan.tiles[1:-1]):
+        j = cols[i * n + plan.slot[-d]]
         outs[-1][p] = panel[j // plan.grid_cols, plan.tile[d]]
 
 
 def message_size(plan, a):
-    return 1 + (1 if a in plan.tile and a != plan.far else 0) + len(plan.edges[a])
+    return 1 + (1 if a in plan.tile else 0) + len(plan.edges[a])
 
 
 def cube_kernel(plan, *refs):
@@ -174,20 +208,20 @@
     for a in plan.moved:
         t = plan.slot[a]
         diagonal = arrived[a][0]
-        if a in plan.tile and a != plan.far:
+        if a in plan.tile:
             s_ia = arrived[a][1]
             acc = acc + nt(own[t], s_ia)
             cube = nn(own[0], s_ia) + nn(own[t], diagonal)
             mine = s_ia.astype(jnp.float32)
         else:
-            s_ai = local[plan.tile[-a if a != plan.far else a] - 1]
+            s_ai = local[plan.tile[-a] - 1]
             acc = acc + nn(own[t], s_ai)
             cube = nt(own[0], s_ai) + nn(own[t], diagonal)
             mine = s_ai.astype(jnp.float32).T
         out[0, t] = 3.0 * mine - 2.0 * cube
     out[0, 0] = 3.0 * s_self - 2.0 * acc
     for a in plan.moved:
-        p = 2 if a in plan.tile and a != plan.far else 1
+        p = 2 if a in plan.tile else 1
         for b in plan.edges[a]:
             k, j = cols[i * n + plan.slot[a]], cols[i * n + plan.slot[b]]
 
@@ -204,7 +238,7 @@
 VMEM = pl.BlockSpec(memory_space=pltpu.VMEM)
 SMEM = pl.BlockSpec(memory_space=pltpu.SMEM)
 ANY = pl.BlockSpec(memory_space=pl.ANY)
-PARAMS = pltpu.CompilerParams(vmem_limit_bytes=48 << 20)
+SMALL = pltpu.CompilerParams(vmem_limit_bytes=24 << 20)
 
 
 def per_device(density, cols):
@@ -213,54 +247,66 @@
     own = density[0]
     table = cols.reshape(-1)
     block = (size, size)
-    n_tiles = len(plan.tiles)
-    lefts = []
-    for d in plan.tiles[1:]:
-        slots = [0] + [plan.slot[a] for a in plan.left[d]]
-        message = jnp.concatenate([own[s:s + 1] for s in slots], axis=0)
-        lefts.append(shifted(message, d))
+    rows, tiles = plan.grid_rows, plan.tiles
+    sizes = {d: 1 + len(plan.left[d]) for d in tiles[1:]}
     panel = gather_rows(own)
-    rows = plan.grid_rows
-    tiles, self_square = pl.pallas_call(
+    packed = pl.pallas_call(
+        functools.partial(pack_kernel, plan),
+        out_shape=[jax.ShapeDtypeStruct((sizes[d], *block), own.dtype) for d in tiles[1:]],
+        in_specs=[VMEM],
+        out_specs=[VMEM] * len(sizes),
+        compiler_params=SMALL,
+        name="pack",
+    )(own)
+    sends = {d: functools.partial(shifted, by=d) for d in tiles[1:]}
+    lefts = in_turn(
+        dict(zip(tiles[1:], packed)), sends, ordered(LEFT_ORDER, tiles[1:]), LEFT_WINDOW
+    )
+    squares, far_square, self_square = pl.pallas_call(
         functools.partial(square_kernel, plan),
         out_shape=[
-            jax.ShapeDtypeStruct((n_tiles, *block), own.dtype),
+            jax.ShapeDtypeStruct((len(tiles) - 1, *block), own.dtype),
+            jax.ShapeDtypeStruct((1, *block), own.dtype),
             jax.ShapeDtypeStruct(block, jnp.float32),
         ],
-        in_specs=[SMEM, VMEM] + [VMEM] * len(lefts) + [ANY] * rows,
-        out_specs=[VMEM, VMEM],
+        in_specs=[SMEM, VMEM] + [ANY] * len(lefts) + [ANY] * rows,
+        out_specs=[VMEM, VMEM, VMEM],
         scratch_shapes=[
             pltpu.VMEM((rows, slot_count, *block), own.dtype),
             pltpu.VMEM(block, jnp.float32),
             pltpu.SemaphoreType.DMA((rows,)),
-        ],
-        compiler_params=PARAMS,
+            pltpu.SemaphoreType.DMA((len(lefts),)),
+        ] + [pltpu.VMEM((sizes[d], *block), own.dtype) for d in tiles[1:]],
+        compiler_params=SMALL,
         name="square",
-    )(table, own, *lefts, *panel)
-    square_panel = gather_rows(tiles)
+    )(table, own, *[lefts[d] for d in tiles[1:]], *panel)
+    square_panel = gather_rows(squares)
     picked = pl.pallas_call(
         functools.partial(pick_kernel, plan),
         out_shape=[
             jax.ShapeDtypeStruct((message_size(plan, a), *block), own.dtype) for a in plan.moved
-        ] + [jax.ShapeDtypeStruct((n_tiles - 1, *block), own.dtype)],
-        in_specs=[SMEM, VMEM] + [ANY] * rows,
+        ] + [jax.ShapeDtypeStruct((len(tiles) - 2, *block), own.dtype)],
+        in_specs=[SMEM, VMEM, VMEM] + [ANY] * rows,
         out_specs=[VMEM] * (len(plan.moved) + 1),
         scratch_shapes=[
-            pltpu.VMEM((rows, n_tiles, *block), own.dtype),
+            pltpu.VMEM((rows, len(tiles) - 1, *block), own.dtype),
             pltpu.SemaphoreType.DMA((rows,)),
         ],
-        compiler_params=PARAMS,
+        compiler_params=SMALL,
         name="pick",
-    )(table, tiles, *square_panel)
-    arrived = [shifted(m, -a) for m, a in zip(picked, plan.moved)]
+    )(table, squares, far_square, *square_panel)
+    sends = {a: functools.partial(shifted, by=-a) for a in plan.moved}
+    arrived = in_turn(
+        dict(zip(plan.moved, picked)), sends, ordered(BACK_ORDER, plan.moved), BACK_WINDOW
+    )
     return pl.pallas_call(
         functools.partial(cube_kernel, plan),
         out_shape=jax.ShapeDtypeStruct((1, slot_count, *block), jnp.float32),
         in_specs=[SMEM, VMEM, VMEM, VMEM] + [VMEM] * len(arrived),
         out_specs=VMEM,
-        compiler_params=PARAMS,
+        compiler_params=SMALL,
         name="cube",
-    )(table, own, self_square, picked[-1], *arrived)
+    )(table, own, self_square, picked[-1], *[arrived[a] for a in plan.moved])
 
 
 def solution(mesh):

time: 194 us -> 176 us (0.907)
  local copies, waits for them, and re-layouts: 25.3 us -> 13.2 us
  starting transfers between devices: 57.3 us -> 51.4 us
    unnamed x64 -> x29, local copies, waits for them, and re-layouts: 22.2 us -> 12.2 us
    ppermute x6, waiting for transfers between devices: 13 us -> 21.1 us  [gather_rows(): lax.ppermute(block, 'row', [(2 * x + h, 2 * ((x + step) % chips) + h) for...]
    ppermute x23, waiting for transfers between devices: 82.1 us -> 74.8 us  [shifted(): lax.ppermute(value, 'col', [(i, (i + by) % length) for i in range(length)])]
    ppermute x23, starting transfers between devices: 48.9 us -> 43.2 us  [shifted(): lax.ppermute(value, 'col', [(i, (i + by) % length) for i in range(length)])]
    concatenate x6 -> x0, local copies, waits for them, and re-layouts: 2.14 us -> none  [per_device(): message = jnp.concatenate([own[s:s + 1] for s in slots], axis=0)]
  transfers between devices with their start and end apart: 37 -> 37, of which waited for: 12 -> 19; matrix products, arithmetic and copies ran while one was open for 1% -> 1% of each run, Pallas kernels for 0% -> 0%
where the time goes in v2:
time: 176 us; the launch traced here: 175 us
  waiting for transfers between devices  97.3 us (55%)
  starting transfers between devices  51.4 us (29%)
  Pallas kernels  13.4 us (8%)
  local copies, waits for them, and re-layouts  13.2 us (8%)
    ppermute x23, waiting for transfers between devices, shifted(): lax.ppermute(value, 'col', [(i, (i + by) % length) for i in range(length)])  74.8 us
    ppermute x23, starting transfers between devices, shifted(): lax.ppermute(value, 'col', [(i, (i + by) % length) for i in range(length)])  43.2 us
    ppermute x6, waiting for transfers between devices, gather_rows(): lax.ppermute(block, 'row', [(2 * x + h, 2 * ((x + step) % chips) + h) for...  21.1 us
    unnamed x29, local copies, waits for them, and re-layouts  12.2 us
    ppermute x6, starting transfers between devices, gather_rows(): lax.ppermute(block, 'row', [(2 * x + h, 2 * ((x + step) % chips) + h) for...  8.17 us
    pallas_call x1, Pallas kernels, per_device(): pl.pallas_call(functools.partial(square_kernel, plan), out_shape=[jax.Sha...  6.09 us
    pallas_call x1, Pallas kernels, per_device(): pl.pallas_call(functools.partial(cube_kernel, plan), out_shape=jax.ShapeD...  4.62 us
  transfers between devices with their start and end apart: 37, of which 19 were waited for; matrix products, arithmetic and copies ran while one was open for 1% of the time, Pallas kernels for 0%

profile of v2, /device:TPU:2, one launch (start us, length us, event | category | flops | bytes accessed | tf_op | source)
XLA Modules:
  0.0 175.5 jit_solution(66715704103190112)
XLA Ops:
  2.2 8.8 %collective-permute-start.2 = (bf16[9,128,128]{2,1,0:T(8,128)(2,1)S(1)}, bf16[9,128,128]{2,1,0:T(8,128)(2,1)S(1)}, u32[]{:S(2)}, u32[]{:S(2)}) collective-permute-start(bf16[9,128,128]{2,1,0:T(8,128)(2,1)S(1)} %get-tuple-element.51), channel_id=1, source_target_pairs={{0,27},{1,28},{2,29},{3,30},{4,31},{5,0},{6,1},{7,2},{8,3},{9,4},{... | collective-permute-start | bytes 884744 | tf_op jit(solution)/shard_map/ppermute | solution.py:47
  12.0 4.9 %collective-permute-start.4 = (bf16[11,128,128]{2,1,0:T(8,128)(2,1)S(1)}, bf16[11,128,128]{2,1,0:T(8,128)(2,1)S(1)}, u32[]{:S(2)}, u32[]{:S(2)}) collective-permute-start(bf16[11,128,128]{2,1,0:T(8,128)(2,1)S(1)} %get-tuple-element.53), channel_id=1, source_target_pairs={{0,3},{1,4},{2,5},{3,6},{4,7},{5,8},{6,9},{7,10},{8,11},{9,12},{10... | collective-permute-start | bytes 1081352 | tf_op jit(solution)/shard_map/ppermute | solution.py:47
  18.4 15.0 %collective-permute-done.refs_8_ = bf16[7,128,128]{2,1,0:T(8,128)(2,1)S(1)} collective-permute-done((bf16[7,128,128]{2,1,0:T(8,128)(2,1)S(1)}, bf16[7,128,128]{2,1,0:T(8,128)(2,1)S(1)}, u32[]{:S(2)}, u32[]{:S(2)}) %collective-permute-start) | collective-permute-done | bytes 229408 | tf_op jit(solution)/shard_map/ppermute | solution.py:47
  40.4 7.3 %collective-permute-done.7.refs_9_ = bf16[1,128,128]{2,1,0:T(8,128)(2,1)S(1)} collective-permute-done((bf16[1,128,128]{2,1,0:T(8,128)(2,1)S(1)}, bf16[1,128,128]{2,1,0:T(8,128)(2,1)S(1)}, u32[]{:S(2)}, u32[]{:S(2)}) %collective-permute-start.7) | collective-permute-done | bytes 32800 | tf_op jit(solution)/shard_map/ppermute | solution.py:47
  50.5 6.5 %collective-permute-done.13.refs_16_ = bf16[16,128,128]{2,1,0:T(8,128)(2,1)S(1)} collective-permute-done((bf16[16,128,128]{2,1,0:T(8,128)(2,1)S(1)}, bf16[16,128,128]{2,1,0:T(8,128)(2,1)S(1)}, u32[]{:S(2)}, u32[]{:S(2)}) %collective-permute-start.13) | collective-permute-done | bytes 524320 | tf_op jit(solution)/shard_map/ppermute | solution.py:85
  58.2 4.9 %collective-permute-done.6.refs_7_ = bf16[8,128,128]{2,1,0:T(8,128)(2,1)S(1)} collective-permute-done((bf16[8,128,128]{2,1,0:T(8,128)(2,1)S(1)}, bf16[8,128,128]{2,1,0:T(8,128)(2,1)S(1)}, u32[]{:S(2)}, u32[]{:S(2)}) %collective-permute-start.6) | collective-permute-done | bytes 262176 | tf_op jit(solution)/shard_map/ppermute | solution.py:47
  66.6 12.0 %collective-permute-done.1.refs_2_ = bf16[13,128,128]{2,1,0:T(8,128)(2,1)} collective-permute-done((bf16[13,128,128]{2,1,0:T(8,128)(2,1)}, bf16[13,128,128]{2,1,0:T(8,128)(2,1)}, u32[]{:S(2)}, u32[]{:S(2)}) %collective-permute-start.1) | collective-permute-done | bytes 426016 | tf_op jit(solution)/shard_map/ppermute | solution.py:47
  78.6 4.7 %collective-permute-done.3.refs_3_ = bf16[12,128,128]{2,1,0:T(8,128)(2,1)S(1)} collective-permute-done((bf16[12,128,128]{2,1,0:T(8,128)(2,1)}, bf16[12,128,128]{2,1,0:T(8,128)(2,1)S(1)}, u32[]{:S(2)}, u32[]{:S(2)}) %collective-permute-start.3) | collective-permute-done | bytes 393248 | tf_op jit(solution)/shard_map/ppermute | solution.py:47
  88.9 6.1 %square.1 = (bf16[8,128,128]{2,1,0:T(8,128)(2,1)S(1)}, bf16[1,128,128]{2,1,0:T(8,128)(2,1)S(1)}, f32[128,128]{1,0:T(8,128)S(1)}) custom-call(s32[4096]{0:T(1024)S(1)} %reshape.3.refs_0_, bf16[16,128,128]{2,1,0:T(8,128)(2,1)S(1)} %bitcast.6, bf16[13,128,128]{2,1,0:T(8,128)(2,1)} %collective-permute-done.1.refs_2_, ...), custom_call_target="tpu_custom_call" | custom-call | tf_op jit(solution)/shard_map/square/pallas_call | solution.py:265
  95.3 2.3 %collective-permute-start.18 = (bf16[8,128,128]{2,1,0:T(8,128)(2,1)S(1)}, bf16[8,128,128]{2,1,0:T(8,128)(2,1)S(1)}, u32[]{:S(2)}, u32[]{:S(2)}) collective-permute-start(bf16[8,128,128]{2,1,0:T(8,128)(2,1)S(1)} %get-tuple-element.60.refs_1_.refs_3_), channel_id=1, source_target_pairs={{0,128},{32,160},{64,192},{96,224},{128,0},{160,32},{192,64},{224,... | collective-permute-start | bytes 786440 | tf_op jit(solution)/shard_map/ppermute | solution.py:85
  98.1 6.2 %collective-permute-done.16.refs_5_ = bf16[8,128,128]{2,1,0:T(8,128)(2,1)S(1)} collective-permute-done((bf16[8,128,128]{2,1,0:T(8,128)(2,1)S(1)}, bf16[8,128,128]{2,1,0:T(8,128)(2,1)S(1)}, u32[]{:S(2)}, u32[]{:S(2)}) %collective-permute-start.16) | collective-permute-done | bytes 262176 | tf_op jit(solution)/shard_map/ppermute | solution.py:85
  106.0 4.5 %collective-permute-done.20.refs_9_ = bf16[8,128,128]{2,1,0:T(8,128)(2,1)S(1)} collective-permute-done((bf16[8,128,128]{2,1,0:T(8,128)(2,1)S(1)}, bf16[8,128,128]{2,1,0:T(8,128)(2,1)S(1)}, u32[]{:S(2)}, u32[]{:S(2)}) %collective-permute-start.20) | collective-permute-done | bytes 262176 | tf_op jit(solution)/shard_map/ppermute | solution.py:85
  116.2 6.3 %collective-permute-start.32 = (bf16[5,128,128]{2,1,0:T(8,128)(2,1)S(1)}, bf16[5,128,128]{2,1,0:T(8,128)(2,1)S(1)}, u32[]{:S(2)}, u32[]{:S(2)}) collective-permute-start(bf16[5,128,128]{2,1,0:T(8,128)(2,1)S(1)} %get-tuple-element.81), channel_id=1, source_target_pairs={{0,26},{1,27},{2,28},{3,29},{4,30},{5,31},{6,0},{7,1},{8,2},{9,3},... | collective-permute-start | bytes 491528 | tf_op jit(solution)/shard_map/ppermute | solution.py:47
  124.5 3.3 %collective-permute-start.30 = (bf16[6,128,128]{2,1,0:T(8,128)(2,1)S(1)}, bf16[6,128,128]{2,1,0:T(8,128)(2,1)S(1)}, u32[]{:S(2)}, u32[]{:S(2)}) collective-permute-start(bf16[6,128,128]{2,1,0:T(8,128)(2,1)S(1)} %get-tuple-element.78), channel_id=1, source_target_pairs={{0,28},{1,29},{2,30},{3,31},{4,0},{5,1},{6,2},{7,3},{8,4},{9,5},{1... | collective-permute-start | bytes 589832 | tf_op jit(solution)/shard_map/ppermute | solution.py:47
  127.8 3.0 %collective-permute-done.25.refs_12_ = bf16[6,128,128]{2,1,0:T(8,128)(2,1)S(1)} collective-permute-done((bf16[6,128,128]{2,1,0:T(8,128)(2,1)S(1)}, bf16[6,128,128]{2,1,0:T(8,128)(2,1)S(1)}, u32[]{:S(2)}, u32[]{:S(2)}) %collective-permute-start.25) | collective-permute-done | bytes 196640 | tf_op jit(solution)/shard_map/ppermute | solution.py:47
  131.9 5.2 %collective-permute-start.23 = (bf16[7,128,128]{2,1,0:T(8,128)(2,1)S(1)}, bf16[7,128,128]{2,1,0:T(8,128)(2,1)S(1)}, u32[]{:S(2)}, u32[]{:S(2)}) collective-permute-start(bf16[7,128,128]{2,1,0:T(8,128)(2,1)S(1)} %get-tuple-element.66), channel_id=1, source_target_pairs={{0,2},{1,3},{2,4},{3,5},{4,6},{5,7},{6,8},{7,9},{8,10},{9,11},{10,... | collective-permute-start | bytes 688136 | tf_op jit(solution)/shard_map/ppermute | solution.py:47
  137.2 5.0 %collective-permute-done.26.refs_13_ = bf16[5,128,128]{2,1,0:T(8,128)(2,1)S(1)} collective-permute-done((bf16[5,128,128]{2,1,0:T(8,128)(2,1)S(1)}, bf16[5,128,128]{2,1,0:T(8,128)(2,1)S(1)}, u32[]{:S(2)}, u32[]{:S(2)}) %collective-permute-start.26) | collective-permute-done | bytes 163872 | tf_op jit(solution)/shard_map/ppermute | solution.py:47
  144.3 2.2 %collective-permute-start.34 = (bf16[6,128,128]{2,1,0:T(8,128)(2,1)S(1)}, bf16[6,128,128]{2,1,0:T(8,128)(2,1)S(1)}, u32[]{:S(2)}, u32[]{:S(2)}) collective-permute-start(bf16[6,128,128]{2,1,0:T(8,128)(2,1)S(1)} %get-tuple-element.84), channel_id=1, source_target_pairs={{0,4},{1,5},{2,6},{3,7},{4,8},{5,9},{6,10},{7,11},{8,12},{9,13},{1... | collective-permute-start | bytes 589832 | tf_op jit(solution)/shard_map/ppermute | solution.py:47
  146.6 4.5 %collective-permute-done.23.refs_7_ = bf16[7,128,128]{2,1,0:T(8,128)(2,1)S(1)} collective-permute-done((bf16[7,128,128]{2,1,0:T(8,128)(2,1)S(1)}, bf16[7,128,128]{2,1,0:T(8,128)(2,1)S(1)}, u32[]{:S(2)}, u32[]{:S(2)}) %collective-permute-start.23) | collective-permute-done | bytes 229408 | tf_op jit(solution)/shard_map/ppermute | solution.py:47
  151.8 3.1 %collective-permute-start.28 = (bf16[7,128,128]{2,1,0:T(8,128)(2,1)S(1)}, bf16[7,128,128]{2,1,0:T(8,128)(2,1)S(1)}, u32[]{:S(2)}, u32[]{:S(2)}) collective-permute-start(bf16[7,128,128]{2,1,0:T(8,128)(2,1)S(1)} %get-tuple-element.74), channel_id=1, source_target_pairs={{0,30},{1,31},{2,0},{3,1},{4,2},{5,3},{6,4},{7,5},{8,6},{9,7},{10,... | collective-permute-start | bytes 688136 | tf_op jit(solution)/shard_map/ppermute | solution.py:47
  154.9 5.4 %collective-permute-done.31.refs_8_ = bf16[6,128,128]{2,1,0:T(8,128)(2,1)S(1)} collective-permute-done((bf16[6,128,128]{2,1,0:T(8,128)(2,1)S(1)}, bf16[6,128,128]{2,1,0:T(8,128)(2,1)S(1)}, u32[]{:S(2)}, u32[]{:S(2)}) %collective-permute-start.31) | collective-permute-done | bytes 196640 | tf_op jit(solution)/shard_map/ppermute | solution.py:47
  160.3 8.2 %collective-permute-done.36.refs_18_ = bf16[2,128,128]{2,1,0:T(8,128)(2,1)S(1)} collective-permute-done((bf16[2,128,128]{2,1,0:T(8,128)(2,1)S(1)}, bf16[2,128,128]{2,1,0:T(8,128)(2,1)S(1)}, u32[]{:S(2)}, u32[]{:S(2)}) %collective-permute-start.36) | collective-permute-done | bytes 65568 | tf_op jit(solution)/shard_map/ppermute | solution.py:47
  168.5 2.4 %collective-permute-done.35.refs_15_ = bf16[5,128,128]{2,1,0:T(8,128)(2,1)S(1)} collective-permute-done((bf16[5,128,128]{2,1,0:T(8,128)(2,1)S(1)}, bf16[5,128,128]{2,1,0:T(8,128)(2,1)S(1)}, u32[]{:S(2)}, u32[]{:S(2)}) %collective-permute-start.35) | collective-permute-done | bytes 163872 | tf_op jit(solution)/shard_map/ppermute | solution.py:47
  170.9 4.6 %cube.1 = f32[1,16,128,128]{3,2,1,0:T(8,128)} custom-call(s32[4096]{0:T(1024)S(1)} %reshape.3.refs_0_, bf16[16,128,128]{2,1,0:T(8,128)(2,1)S(1)} %bitcast.8, f32[128,128]{1,0:T(8,128)S(1)} %get-tuple-element.59.refs_2_, bf16[7,128,128]{2,1,0:T(8,128)(2,1)S(1)} %get-tuple-element.62.refs_3_, bf16[7,128,128]{2,1,0:T(8,128)(2,1)S(1)} %collective-permute-done.24.refs_4_, ...), custom_call_target="tpu_custom_call" | custom-call | tf_op jit(solution)/shard_map/cube/pallas_call | solution.py:302
  (84 shorter events, 38.9 us)
Async XLA Ops:
  2.2 34.0 %collective-permute-start.2 = (bf16[9,128,128]{2,1,0:T(8,128)(2,1)S(1)}, bf16[9,128,128]{2,1,0:T(8,128)(2,1)S(1)}, u32[]{:S(2)}, u32[]{:S(2)}) collective-permute-start(bf16[9,128,128]{2,1,0:T(8,128)(2,1)S(1)} %get-tuple-element.51), channel_id=1, source_target_pairs={{0,27},{1,28},{2,29},{3,30},{4,31},{5,0},{6,1},{7,2},{8,3},{9,4},{... | collective-permute-start | bytes 884744 | tf_op jit(solution)/shard_map/ppermute | solution.py:47
  11.0 27.4 %collective-permute-start.5 = (bf16[10,128,128]{2,1,0:T(8,128)(2,1)S(1)}, bf16[10,128,128]{2,1,0:T(8,128)(2,1)S(1)}, u32[]{:S(2)}, u32[]{:S(2)}) collective-permute-start(bf16[10,128,128]{2,1,0:T(8,128)(2,1)S(1)} %get-tuple-element.54), channel_id=1, source_target_pairs={{0,4},{1,5},{2,6},{3,7},{4,8},{5,9},{6,10},{7,11},{8,12},{9,13},{1... | collective-permute-start | bytes 983048 | tf_op jit(solution)/shard_map/ppermute | solution.py:47
  12.0 21.4 %collective-permute-start = (bf16[7,128,128]{2,1,0:T(8,128)(2,1)S(1)}, bf16[7,128,128]{2,1,0:T(8,128)(2,1)S(1)}, u32[]{:S(2)}, u32[]{:S(2)}) collective-permute-start(bf16[7,128,128]{2,1,0:T(8,128)(2,1)S(1)} %get-tuple-element.48), channel_id=1, source_target_pairs={{0,25},{1,26},{2,27},{3,28},{4,29},{5,30},{6,31},{7,0},{8,1},{9,2}... | collective-permute-start | bytes 688136 | tf_op jit(solution)/shard_map/ppermute | solution.py:47
  12.0 27.2 %collective-permute-start.4 = (bf16[11,128,128]{2,1,0:T(8,128)(2,1)S(1)}, bf16[11,128,128]{2,1,0:T(8,128)(2,1)S(1)}, u32[]{:S(2)}, u32[]{:S(2)}) collective-permute-start(bf16[11,128,128]{2,1,0:T(8,128)(2,1)S(1)} %get-tuple-element.53), channel_id=1, source_target_pairs={{0,3},{1,4},{2,5},{3,6},{4,7},{5,8},{6,9},{7,10},{8,11},{9,12},{10... | collective-permute-start | bytes 1081352 | tf_op jit(solution)/shard_map/ppermute | solution.py:47
  16.9 31.4 %collective-permute-start.9 = (bf16[16,128,128]{2,1,0:T(8,128)(2,1)S(1)}, bf16[16,128,128]{2,1,0:T(8,128)(2,1)S(1)}, u32[]{:S(2)}, u32[]{:S(2)}) collective-permute-start(bf16[16,128,128]{2,1,0:T(8,128)(2,1)S(1)} %bitcast.2), channel_id=1, source_target_pairs={{0,64},{32,96},{64,128},{96,160},{128,192},{160,224},{192,0},{224,... | collective-permute-start | bytes 1572872 | tf_op jit(solution)/shard_map/ppermute | solution.py:85
  34.1 16.4 %collective-permute-start.11 = (bf16[16,128,128]{2,1,0:T(8,128)(2,1)S(1)}, bf16[16,128,128]{2,1,0:T(8,128)(2,1)S(1)}, u32[]{:S(2)}, u32[]{:S(2)}) collective-permute-start(bf16[16,128,128]{2,1,0:T(8,128)(2,1)S(1)} %bitcast.3), channel_id=1, source_target_pairs={{0,128},{32,160},{64,192},{96,224},{128,0},{160,32},{192,64},{224,... | collective-permute-start | bytes 1572872 | tf_op jit(solution)/shard_map/ppermute | solution.py:85
  36.9 20.1 %collective-permute-start.13 = (bf16[16,128,128]{2,1,0:T(8,128)(2,1)S(1)}, bf16[16,128,128]{2,1,0:T(8,128)(2,1)S(1)}, u32[]{:S(2)}, u32[]{:S(2)}) collective-permute-start(bf16[16,128,128]{2,1,0:T(8,128)(2,1)S(1)} %bitcast.4), channel_id=1, source_target_pairs={{0,192},{32,224},{64,0},{96,32},{128,64},{160,96},{192,128},{224,1... | collective-permute-start | bytes 1572872 | tf_op jit(solution)/shard_map/ppermute | solution.py:85
  39.1 17.9 %collective-permute-start.8 = (bf16[16,128,128]{2,1,0:T(8,128)(2,1)S(1)}, bf16[16,128,128]{2,1,0:T(8,128)(2,1)S(1)}, u32[]{:S(2)}, u32[]{:S(2)}) collective-permute-start(bf16[16,128,128]{2,1,0:T(8,128)(2,1)S(1)} %bitcast.5), channel_id=1, source_target_pairs={{0,32},{32,0},{64,96},{96,64},{128,160},{160,128},{192,224},{224,1... | collective-permute-start | bytes 1572872 | tf_op jit(solution)/shard_map/ppermute | solution.py:92
  48.3 14.8 %collective-permute-start.6 = (bf16[8,128,128]{2,1,0:T(8,128)(2,1)S(1)}, bf16[8,128,128]{2,1,0:T(8,128)(2,1)S(1)}, u32[]{:S(2)}, u32[]{:S(2)}) collective-permute-start(bf16[8,128,128]{2,1,0:T(8,128)(2,1)S(1)} %get-tuple-element.56), channel_id=1, source_target_pairs={{0,6},{1,7},{2,8},{3,9},{4,10},{5,11},{6,12},{7,13},{8,14},{9,15},... | collective-permute-start | bytes 786440 | tf_op jit(solution)/shard_map/ppermute | solution.py:47
  48.3 35.0 %collective-permute-start.10 = (bf16[16,128,128]{2,1,0:T(8,128)(2,1)S(1)}, bf16[16,128,128]{2,1,0:T(8,128)(2,1)S(1)}, u32[]{:S(2)}, u32[]{:S(2)}) collective-permute-start(bf16[16,128,128]{2,1,0:T(8,128)(2,1)S(1)} %collective-permute-done.9.refs_12_), channel_id=1, source_target_pairs={{0,32},{32,0},{64,96},{96,64},{128,160},{160,128},{192,224},{224,1... | collective-permute-start | bytes 1572872 | tf_op jit(solution)/shard_map/ppermute | solution.py:92
  50.5 32.8 %collective-permute-start.12 = (bf16[16,128,128]{2,1,0:T(8,128)(2,1)S(1)}, bf16[16,128,128]{2,1,0:T(8,128)(2,1)}, u32[]{:S(2)}, u32[]{:S(2)}) collective-permute-start(bf16[16,128,128]{2,1,0:T(8,128)(2,1)S(1)} %collective-permute-done.11.refs_14_), channel_id=1, source_target_pairs={{0,32},{32,0},{64,96},{96,64},{128,160},{160,128},{192,224},{224,1... | collective-permute-start | bytes 1572872 | tf_op jit(solution)/shard_map/ppermute | solution.py:92
  57.0 26.3 %collective-permute-start.14 = (bf16[16,128,128]{2,1,0:T(8,128)(2,1)S(1)}, bf16[16,128,128]{2,1,0:T(8,128)(2,1)}, u32[]{:S(2)}, u32[]{:S(2)}) collective-permute-start(bf16[16,128,128]{2,1,0:T(8,128)(2,1)S(1)} %collective-permute-done.13.refs_16_), channel_id=1, source_target_pairs={{0,32},{32,0},{64,96},{96,64},{128,160},{160,128},{192,224},{224,1... | collective-permute-start | bytes 1572872 | tf_op jit(solution)/shard_map/ppermute | solution.py:92
  57.0 21.6 %collective-permute-start.1 = (bf16[13,128,128]{2,1,0:T(8,128)(2,1)}, bf16[13,128,128]{2,1,0:T(8,128)(2,1)}, u32[]{:S(2)}, u32[]{:S(2)}) collective-permute-start(bf16[13,128,128]{2,1,0:T(8,128)(2,1)} %get-tuple-element.49), channel_id=1, source_target_pairs={{0,1},{1,2},{2,3},{3,4},{4,5},{5,6},{6,7},{7,8},{8,9},{9,10},{10,1... | collective-permute-start | bytes 1277960 | tf_op jit(solution)/shard_map/ppermute | solution.py:47
  63.8 19.5 %collective-permute-start.3 = (bf16[12,128,128]{2,1,0:T(8,128)(2,1)}, bf16[12,128,128]{2,1,0:T(8,128)(2,1)S(1)}, u32[]{:S(2)}, u32[]{:S(2)}) collective-permute-start(bf16[12,128,128]{2,1,0:T(8,128)(2,1)} %get-tuple-element.52), channel_id=1, source_target_pairs={{0,30},{1,31},{2,0},{3,1},{4,2},{5,3},{6,4},{7,5},{8,6},{9,7},{10,... | collective-permute-start | bytes 1179656 | tf_op jit(solution)/shard_map/ppermute | solution.py:47
  113.6 17.2 %collective-permute-start.25 = (bf16[6,128,128]{2,1,0:T(8,128)(2,1)S(1)}, bf16[6,128,128]{2,1,0:T(8,128)(2,1)S(1)}, u32[]{:S(2)}, u32[]{:S(2)}) collective-permute-start(bf16[6,128,128]{2,1,0:T(8,128)(2,1)S(1)} %get-tuple-element.71), channel_id=1, source_target_pairs={{0,27},{1,28},{2,29},{3,30},{4,31},{5,0},{6,1},{7,2},{8,3},{9,4},{... | collective-permute-start | bytes 589832 | tf_op jit(solution)/shard_map/ppermute | solution.py:47
  113.7 18.3 %collective-permute-start.22 = (bf16[8,128,128]{2,1,0:T(8,128)(2,1)S(1)}, bf16[8,128,128]{2,1,0:T(8,128)(2,1)S(1)}, u32[]{:S(2)}, u32[]{:S(2)}) collective-permute-start(bf16[8,128,128]{2,1,0:T(8,128)(2,1)S(1)} %get-tuple-element.65), channel_id=1, source_target_pairs={{0,1},{1,2},{2,3},{3,4},{4,5},{5,6},{6,7},{7,8},{8,9},{9,10},{10,1... | collective-permute-start | bytes 786440 | tf_op jit(solution)/shard_map/ppermute | solution.py:47
  116.2 14.6 %collective-permute-start.32 = (bf16[5,128,128]{2,1,0:T(8,128)(2,1)S(1)}, bf16[5,128,128]{2,1,0:T(8,128)(2,1)S(1)}, u32[]{:S(2)}, u32[]{:S(2)}) collective-permute-start(bf16[5,128,128]{2,1,0:T(8,128)(2,1)S(1)} %get-tuple-element.81), channel_id=1, source_target_pairs={{0,26},{1,27},{2,28},{3,29},{4,30},{5,31},{6,0},{7,1},{8,2},{9,3},... | collective-permute-start | bytes 491528 | tf_op jit(solution)/shard_map/ppermute | solution.py:47
  124.5 17.7 %collective-permute-start.30 = (bf16[6,128,128]{2,1,0:T(8,128)(2,1)S(1)}, bf16[6,128,128]{2,1,0:T(8,128)(2,1)S(1)}, u32[]{:S(2)}, u32[]{:S(2)}) collective-permute-start(bf16[6,128,128]{2,1,0:T(8,128)(2,1)S(1)} %get-tuple-element.78), channel_id=1, source_target_pairs={{0,28},{1,29},{2,30},{3,31},{4,0},{5,1},{6,2},{7,3},{8,4},{9,5},{1... | collective-permute-start | bytes 589832 | tf_op jit(solution)/shard_map/ppermute | solution.py:47
  130.8 13.5 %collective-permute-start.33 = (bf16[7,128,128]{2,1,0:T(8,128)(2,1)S(1)}, bf16[7,128,128]{2,1,0:T(8,128)(2,1)S(1)}, u32[]{:S(2)}, u32[]{:S(2)}) collective-permute-start(bf16[7,128,128]{2,1,0:T(8,128)(2,1)S(1)} %get-tuple-element.82), channel_id=1, source_target_pairs={{0,3},{1,4},{2,5},{3,6},{4,7},{5,8},{6,9},{7,10},{8,11},{9,12},{10... | collective-permute-start | bytes 688136 | tf_op jit(solution)/shard_map/ppermute | solution.py:47
  131.9 19.1 %collective-permute-start.23 = (bf16[7,128,128]{2,1,0:T(8,128)(2,1)S(1)}, bf16[7,128,128]{2,1,0:T(8,128)(2,1)S(1)}, u32[]{:S(2)}, u32[]{:S(2)}) collective-permute-start(bf16[7,128,128]{2,1,0:T(8,128)(2,1)S(1)} %get-tuple-element.66), channel_id=1, source_target_pairs={{0,2},{1,3},{2,4},{3,5},{4,6},{5,7},{6,8},{7,9},{8,10},{9,11},{10,... | collective-permute-start | bytes 688136 | tf_op jit(solution)/shard_map/ppermute | solution.py:47
  142.2 18.1 %collective-permute-start.31 = (bf16[6,128,128]{2,1,0:T(8,128)(2,1)S(1)}, bf16[6,128,128]{2,1,0:T(8,128)(2,1)S(1)}, u32[]{:S(2)}, u32[]{:S(2)}) collective-permute-start(bf16[6,128,128]{2,1,0:T(8,128)(2,1)S(1)} %get-tuple-element.79), channel_id=1, source_target_pairs={{0,29},{1,30},{2,31},{3,0},{4,1},{5,2},{6,3},{7,4},{8,5},{9,6},{10... | collective-permute-start | bytes 589832 | tf_op jit(solution)/shard_map/ppermute | solution.py:47
  144.3 16.0 %collective-permute-start.34 = (bf16[6,128,128]{2,1,0:T(8,128)(2,1)S(1)}, bf16[6,128,128]{2,1,0:T(8,128)(2,1)S(1)}, u32[]{:S(2)}, u32[]{:S(2)}) collective-permute-start(bf16[6,128,128]{2,1,0:T(8,128)(2,1)S(1)} %get-tuple-element.84), channel_id=1, source_target_pairs={{0,4},{1,5},{2,6},{3,7},{4,8},{5,9},{6,10},{7,11},{8,12},{9,13},{1... | collective-permute-start | bytes 589832 | tf_op jit(solution)/shard_map/ppermute | solution.py:47
  151.1 19.8 %collective-permute-start.24 = (bf16[7,128,128]{2,1,0:T(8,128)(2,1)S(1)}, bf16[7,128,128]{2,1,0:T(8,128)(2,1)S(1)}, u32[]{:S(2)}, u32[]{:S(2)}) collective-permute-start(bf16[7,128,128]{2,1,0:T(8,128)(2,1)S(1)} %get-tuple-element.67), channel_id=1, source_target_pairs={{0,31},{1,0},{2,1},{3,2},{4,3},{5,4},{6,5},{7,6},{8,7},{9,8},{10,9... | collective-permute-start | bytes 688136 | tf_op jit(solution)/shard_map/ppermute | solution.py:47
  151.8 19.0 %collective-permute-start.28 = (bf16[7,128,128]{2,1,0:T(8,128)(2,1)S(1)}, bf16[7,128,128]{2,1,0:T(8,128)(2,1)S(1)}, u32[]{:S(2)}, u32[]{:S(2)}) collective-permute-start(bf16[7,128,128]{2,1,0:T(8,128)(2,1)S(1)} %get-tuple-element.74), channel_id=1, source_target_pairs={{0,30},{1,31},{2,0},{3,1},{4,2},{5,3},{6,4},{7,5},{8,6},{9,7},{10,... | collective-permute-start | bytes 688136 | tf_op jit(solution)/shard_map/ppermute | solution.py:47
  (27 other events, 207.7 us)

commit v3 on v2

--- a/solution.py
+++ b/solution.py
@@ -7,10 +7,9 @@
 from jax.experimental.pallas import tpu as pltpu
 from jax.sharding import PartitionSpec as P
 
-SIGNS = {1: 1, 2: -1, 3: 1, 4: 1, 5: -1, 6: 1, 7: -1}
-LEFT_ORDER = [-7, -5, 4, 3, 1, -2, 16, 6]
-BACK_ORDER = [5, 6, -7, -1, -5, -3, 4, -2, 7, -4, 3, 1, 2, 16, -6]
-LEFT_WINDOW = 4
+SIGNS = {1: 1, 2: 1, 3: -1, 4: 1, 5: -1, 6: -1, 7: 1}
+PARENTS = {2: 1, -3: 1, -6: -5, 7: 4}
+BACK_ORDER = [1, -1, 4, -4, 2, 5, -5, -2, 3, -3, 6, -6, 7, -7, 16]
 BACK_WINDOW = 4
 
 
@@ -30,10 +29,21 @@
         self.left = {self.far: []}
         for d in self.tiles[1:-1]:
             self.left[d] = [a for a in near if a != d and self.near(a - d)]
+        self.children = {p: [d for d in self.tiles if self.parent(d) == p] for p in self.tiles}
+        self.carried = {}
+        for d in self.tiles[1:]:
+            wanted = {0} | set(self.left[d])
+            for child in self.children[d]:
+                wanted |= {0} | set(self.left[child])
+            self.carried[d] = [a for a in self.offsets if a in wanted]
         self.edges = {self.far: []}
         for a in near:
             self.edges[a] = [b for b in near if b != a and (a - b) in self.tile]
         self.moved = [o for o in self.offsets if o != 0]
+
+    def parent(self, d):
+        p = PARENTS.get(d, 0)
+        return p if d != 0 and p in self.tiles else (0 if d != 0 else None)
 
     def near(self, o):
         return o in self.slot and o != self.far
@@ -74,22 +84,27 @@
     return lax.dot_general(a, b, (((0,), (0,)), ((), ())), preferred_element_type=jnp.float32)
 
 
-def gather_rows(block):
+def from_chip(block, step):
     length = lax.axis_size("row")
     chips = length // 2
-    pieces = []
-    for step in range(chips):
-        if step == 0:
-            same = block
-        else:
-            same = lax.ppermute(
-                block, "row",
-                [(2 * x + h, 2 * ((x + step) % chips) + h) for x in range(chips) for h in range(2)],
-            )
-        pieces.append(same)
+    pairs = [(2 * x + h, 2 * ((x + step) % chips) + h) for x in range(chips) for h in range(2)]
+    return lax.ppermute(block, "row", pairs)
+
+
+def from_core(block):
+    return lax.ppermute(block, "row", [(i, i ^ 1) for i in range(lax.axis_size("row"))])
+
+
+def gather_rows(block):
+    chips = lax.axis_size("row") // 2
+    same = [block] + [None] * (chips - 1)
+    same[1], same[chips - 1] = from_chip(block, 1), from_chip(block, chips - 1)
+    for step in range(2, chips - 1):
+        held, _ = lax.optimization_barrier((block, same[step - 1]))
+        same[step] = from_chip(held, step)
     out = []
-    for same in pieces:
-        out += [same, lax.ppermute(same, "row", [(i, i ^ 1) for i in range(length)])]
+    for piece in same:
+        out += [piece, from_core(piece)]
     return out
 
 
@@ -111,10 +126,21 @@
     return copies
 
 
-def pack_kernel(plan, own, *outs):
-    for out, d in zip(outs, plan.tiles[1:]):
-        for p, s in enumerate([0] + [plan.slot[a] for a in plan.left[d]]):
-            out[p] = own[s]
+def pack_kernel(choices, source, *outs):
+    for out, choice in zip(outs, choices):
+        for p, s in enumerate(choice):
+            out[p] = source[s]
+
+
+def pack(source, choices):
+    return pl.pallas_call(
+        functools.partial(pack_kernel, choices),
+        out_shape=[jax.ShapeDtypeStruct((len(c), *source.shape[1:]), source.dtype) for c in choices],
+        in_specs=[VMEM],
+        out_specs=[VMEM] * len(choices),
+        compiler_params=SMALL,
+        name="pack",
+    )(source)
 
 
 def square_kernel(plan, *refs):
@@ -146,14 +172,15 @@
         j = cols[i * n + plan.slot[d]]
         rank = j // plan.grid_cols
         back = plan.slot[-d] if d != plan.far else plan.slot[d]
-        total[...] = nt(left[0], panel[rank, back]) + tn(panel[rank, back], panel[rank, 0])
-        for p, a in enumerate(plan.left[d]):
+        total[...] = nt(left[plan.carried[d].index(0)], panel[rank, back]) + tn(panel[rank, back], panel[rank, 0])
+        for a in plan.left[d]:
+            p = plan.carried[d].index(a)
             k = cols[i * n + plan.slot[a]]
             u = plan.slot[a - d]
 
             @pl.when(cols[j * n + u] == k)
             def _():
-                total[...] += nt(left[p + 1], panel[rank, u])
+                total[...] += nt(left[p], panel[rank, u])
 
         if d == plan.far:
             far_out[0] = total[...].astype(out.dtype)
@@ -238,7 +265,7 @@
 VMEM = pl.BlockSpec(memory_space=pltpu.VMEM)
 SMEM = pl.BlockSpec(memory_space=pltpu.SMEM)
 ANY = pl.BlockSpec(memory_space=pl.ANY)
-SMALL = pltpu.CompilerParams(vmem_limit_bytes=24 << 20)
+SMALL = pltpu.CompilerParams(vmem_limit_bytes=12 << 20)
 
 
 def per_device(density, cols):
@@ -248,20 +275,19 @@
     table = cols.reshape(-1)
     block = (size, size)
     rows, tiles = plan.grid_rows, plan.tiles
-    sizes = {d: 1 + len(plan.left[d]) for d in tiles[1:]}
+    sizes = {d: len(plan.carried[d]) for d in tiles[1:]}
     panel = gather_rows(own)
-    packed = pl.pallas_call(
-        functools.partial(pack_kernel, plan),
-        out_shape=[jax.ShapeDtypeStruct((sizes[d], *block), own.dtype) for d in tiles[1:]],
-        in_specs=[VMEM],
-        out_specs=[VMEM] * len(sizes),
-        compiler_params=SMALL,
-        name="pack",
-    )(own)
-    sends = {d: functools.partial(shifted, by=d) for d in tiles[1:]}
-    lefts = in_turn(
-        dict(zip(tiles[1:], packed)), sends, ordered(LEFT_ORDER, tiles[1:]), LEFT_WINDOW
-    )
+    lefts = {}
+
+    def hand_on(source, at, held):
+        children = plan.children[at]
+        choices = [[held.index(a) for a in plan.carried[d]] for d in children]
+        for d, message in zip(children, pack(source, choices)):
+            lefts[d] = shifted(message, d - at)
+
+    hand_on(own, 0, plan.offsets)
+    for d in [d for d in tiles[1:] if plan.children[d]]:
+        hand_on(lefts[d], d, plan.carried[d])
     squares, far_square, self_square = pl.pallas_call(
         functools.partial(square_kernel, plan),
         out_shape=[

time: 176 us -> 155 us (0.88)
  the two profiles are of different devices: /device:TPU:2 before, /device:TPU:16 now
where the time goes in v3:
time: 155 us; the launch traced here: 154 us
  starting transfers between devices  82.8 us (53%)
  waiting for transfers between devices  52.3 us (34%)
  Pallas kernels  14.4 us (9%)
  local copies, waits for them, and re-layouts  4.73 us (3%)
    ppermute x23, starting transfers between devices, shifted(): lax.ppermute(value, 'col', [(i, (i + by) % length) for i in range(length)])  70.3 us
    ppermute x23, waiting for transfers between devices, shifted(): lax.ppermute(value, 'col', [(i, (i + by) % length) for i in range(length)])  36.8 us
    ppermute x6, waiting for transfers between devices, from_chip(): return lax.ppermute(block, 'row', pairs)  14 us
    ppermute x6, starting transfers between devices, from_chip(): return lax.ppermute(block, 'row', pairs)  11.4 us
    pallas_call x1, Pallas kernels, per_device(): pl.pallas_call(functools.partial(square_kernel, plan), out_shape=[jax.Sha...  6.01 us
    pallas_call x1, Pallas kernels, per_device(): pl.pallas_call(functools.partial(cube_kernel, plan), out_shape=jax.ShapeD...  4.67 us
    unnamed x11, local copies, waits for them, and re-layouts  3.73 us
  transfers between devices with their start and end apart: 37, of which 12 were waited for; matrix products, arithmetic and copies ran while one was open for 1% of the time, Pallas kernels for 1%

profile of v3, /device:TPU:16, one launch (start us, length us, event | category | flops | bytes accessed | tf_op | source)
XLA Modules:
  0.0 154.4 jit_solution(15741473542165150306)
XLA Ops:
  2.7 5.8 %collective-permute-start.4 = (bf16[10,128,128]{2,1,0:T(8,128)(2,1)S(1)}, bf16[10,128,128]{2,1,0:T(8,128)(2,1)S(1)}, u32[]{:S(2)}, u32[]{:S(2)}) collective-permute-start(bf16[10,128,128]{2,1,0:T(8,128)(2,1)S(1)} %get-tuple-element.47), channel_id=1, source_target_pairs={{0,27},{1,28},{2,29},{3,30},{4,31},{5,0},{6,1},{7,2},{8,3},{9,4},{... | collective-permute-start | bytes 983048 | tf_op jit(solution)/shard_map/ppermute | solution.py:57
  15.1 2.8 %collective-permute-done.7.refs_9_ = bf16[1,128,128]{2,1,0:T(8,128)(2,1)S(1)} collective-permute-done((bf16[1,128,128]{2,1,0:T(8,128)(2,1)S(1)}, bf16[1,128,128]{2,1,0:T(8,128)(2,1)S(1)}, u32[]{:S(2)}, u32[]{:S(2)}) %collective-permute-start.7) | collective-permute-done | bytes 32800 | tf_op jit(solution)/shard_map/ppermute | solution.py:57
  18.5 2.7 %collective-permute-start.11 = (bf16[16,128,128]{2,1,0:T(8,128)(2,1)}, bf16[16,128,128]{2,1,0:T(8,128)(2,1)S(1)}, u32[]{:S(2)}, u32[]{:S(2)}) collective-permute-start(bf16[16,128,128]{2,1,0:T(8,128)(2,1)} %bitcast.source.refs_1_.refs_10_), channel_id=1, source_target_pairs={{0,128},{32,160},{64,192},{96,224},{128,0},{160,32},{192,64},{224,... | collective-permute-start | bytes 1572872 | tf_op jit(solution)/shard_map/ppermute | solution.py:91
  21.3 2.2 %collective-permute-start.3 = (bf16[11,128,128]{2,1,0:T(8,128)(2,1)S(1)}, bf16[11,128,128]{2,1,0:T(8,128)(2,1)S(1)}, u32[]{:S(2)}, u32[]{:S(2)}) collective-permute-start(bf16[11,128,128]{2,1,0:T(8,128)(2,1)S(1)} %get-tuple-element.46), channel_id=1, source_target_pairs={{0,4},{1,5},{2,6},{3,7},{4,8},{5,9},{6,10},{7,11},{8,12},{9,13},{1... | collective-permute-start | bytes 1081352 | tf_op jit(solution)/shard_map/ppermute | solution.py:57
  23.4 8.7 %collective-permute-done.3.source.refs_5_ = bf16[11,128,128]{2,1,0:T(8,128)(2,1)S(1)} collective-permute-done((bf16[11,128,128]{2,1,0:T(8,128)(2,1)S(1)}, bf16[11,128,128]{2,1,0:T(8,128)(2,1)S(1)}, u32[]{:S(2)}, u32[]{:S(2)}) %collective-permute-start.3) | collective-permute-done | bytes 360480 | tf_op jit(solution)/shard_map/ppermute | solution.py:57
  32.7 7.0 %collective-permute-start.6 = (bf16[7,128,128]{2,1,0:T(8,128)(2,1)S(1)}, bf16[7,128,128]{2,1,0:T(8,128)(2,1)S(1)}, u32[]{:S(2)}, u32[]{:S(2)}) collective-permute-start(bf16[7,128,128]{2,1,0:T(8,128)(2,1)S(1)} %pack.7), channel_id=1, source_target_pairs={{0,3},{1,4},{2,5},{3,6},{4,7},{5,8},{6,9},{7,10},{8,11},{9,12},{10... | collective-permute-start | bytes 688136 | tf_op jit(solution)/shard_map/ppermute | solution.py:57
  41.3 5.5 %collective-permute-done.5.refs_7_ = bf16[8,128,128]{2,1,0:T(8,128)(2,1)S(1)} collective-permute-done((bf16[8,128,128]{2,1,0:T(8,128)(2,1)S(1)}, bf16[8,128,128]{2,1,0:T(8,128)(2,1)S(1)}, u32[]{:S(2)}, u32[]{:S(2)}) %collective-permute-start.5) | collective-permute-done | bytes 262176 | tf_op jit(solution)/shard_map/ppermute | solution.py:57
  49.1 2.8 %collective-permute-start.2 = (bf16[11,128,128]{2,1,0:T(8,128)(2,1)}, bf16[11,128,128]{2,1,0:T(8,128)(2,1)}, u32[]{:S(2)}, u32[]{:S(2)}) collective-permute-start(bf16[11,128,128]{2,1,0:T(8,128)(2,1)} %get-tuple-element.45), channel_id=1, source_target_pairs={{0,28},{1,29},{2,30},{3,31},{4,0},{5,1},{6,2},{7,3},{8,4},{9,5},{1... | collective-permute-start | bytes 1081352 | tf_op jit(solution)/shard_map/ppermute | solution.py:57
  53.6 3.5 %collective-permute-done.2.refs_4_ = bf16[11,128,128]{2,1,0:T(8,128)(2,1)} collective-permute-done((bf16[11,128,128]{2,1,0:T(8,128)(2,1)}, bf16[11,128,128]{2,1,0:T(8,128)(2,1)}, u32[]{:S(2)}, u32[]{:S(2)}) %collective-permute-start.2) | collective-permute-done | bytes 360480 | tf_op jit(solution)/shard_map/ppermute | solution.py:57
  58.9 6.0 %square.1 = (bf16[8,128,128]{2,1,0:T(8,128)(2,1)S(1)}, bf16[1,128,128]{2,1,0:T(8,128)(2,1)S(1)}, f32[128,128]{1,0:T(8,128)S(1)}) custom-call(s32[4096]{0:T(1024)S(1)} %reshape.3.refs_0_, bf16[16,128,128]{2,1,0:T(8,128)(2,1)} %bitcast.source.refs_1_.refs_10_, bf16[15,128,128]{2,1,0:T(8,128)(2,1)S(1)} %collective-permute-done.source.refs_2_, ...), custom_call_target="tpu_custom_call" | custom-call | tf_op jit(solution)/shard_map/square/pallas_call | solution.py:291
  68.2 6.9 %collective-permute-done.16.refs_5_ = bf16[8,128,128]{2,1,0:T(8,128)(2,1)S(1)} collective-permute-done((bf16[8,128,128]{2,1,0:T(8,128)(2,1)S(1)}, bf16[8,128,128]{2,1,0:T(8,128)(2,1)S(1)}, u32[]{:S(2)}, u32[]{:S(2)}) %collective-permute-start.16) | collective-permute-done | bytes 262176 | tf_op jit(solution)/shard_map/ppermute | solution.py:91
  77.8 5.2 %collective-permute-done.18.refs_7_ = bf16[8,128,128]{2,1,0:T(8,128)(2,1)S(1)} collective-permute-done((bf16[8,128,128]{2,1,0:T(8,128)(2,1)S(1)}, bf16[8,128,128]{2,1,0:T(8,128)(2,1)S(1)}, u32[]{:S(2)}, u32[]{:S(2)}) %collective-permute-start.18) | collective-permute-done | bytes 262176 | tf_op jit(solution)/shard_map/ppermute | solution.py:91
  88.2 4.6 %collective-permute-start.30 = (bf16[6,128,128]{2,1,0:T(8,128)(2,1)S(1)}, bf16[6,128,128]{2,1,0:T(8,128)(2,1)S(1)}, u32[]{:S(2)}, u32[]{:S(2)}) collective-permute-start(bf16[6,128,128]{2,1,0:T(8,128)(2,1)S(1)} %get-tuple-element.68), channel_id=1, source_target_pairs={{0,28},{1,29},{2,30},{3,31},{4,0},{5,1},{6,2},{7,3},{8,4},{9,5},{1... | collective-permute-start | bytes 589832 | tf_op jit(solution)/shard_map/ppermute | solution.py:57
  94.5 3.1 %collective-permute-start.24 = (bf16[7,128,128]{2,1,0:T(8,128)(2,1)S(1)}, bf16[7,128,128]{2,1,0:T(8,128)(2,1)S(1)}, u32[]{:S(2)}, u32[]{:S(2)}) collective-permute-start(bf16[7,128,128]{2,1,0:T(8,128)(2,1)S(1)} %get-tuple-element.58), channel_id=1, source_target_pairs={{0,30},{1,31},{2,0},{3,1},{4,2},{5,3},{6,4},{7,5},{8,6},{9,7},{10,... | collective-permute-start | bytes 688136 | tf_op jit(solution)/shard_map/ppermute | solution.py:57
  97.7 7.2 %collective-permute-start.28 = (bf16[5,128,128]{2,1,0:T(8,128)(2,1)S(1)}, bf16[5,128,128]{2,1,0:T(8,128)(2,1)S(1)}, u32[]{:S(2)}, u32[]{:S(2)}) collective-permute-start(bf16[5,128,128]{2,1,0:T(8,128)(2,1)S(1)} %get-tuple-element.66), channel_id=1, source_target_pairs={{0,27},{1,28},{2,29},{3,30},{4,31},{5,0},{6,1},{7,2},{8,3},{9,4},{... | collective-permute-start | bytes 491528 | tf_op jit(solution)/shard_map/ppermute | solution.py:57
  107.7 4.5 %collective-permute-start.29 = (bf16[7,128,128]{2,1,0:T(8,128)(2,1)S(1)}, bf16[7,128,128]{2,1,0:T(8,128)(2,1)S(1)}, u32[]{:S(2)}, u32[]{:S(2)}) collective-permute-start(bf16[7,128,128]{2,1,0:T(8,128)(2,1)S(1)} %get-tuple-element.67), channel_id=1, source_target_pairs={{0,3},{1,4},{2,5},{3,6},{4,7},{5,8},{6,9},{7,10},{8,11},{9,12},{10... | collective-permute-start | bytes 688136 | tf_op jit(solution)/shard_map/ppermute | solution.py:57
  112.2 4.5 %collective-permute-start.27 = (bf16[6,128,128]{2,1,0:T(8,128)(2,1)S(1)}, bf16[6,128,128]{2,1,0:T(8,128)(2,1)S(1)}, u32[]{:S(2)}, u32[]{:S(2)}) collective-permute-start(bf16[6,128,128]{2,1,0:T(8,128)(2,1)S(1)} %get-tuple-element.63), channel_id=1, source_target_pairs={{0,29},{1,30},{2,31},{3,0},{4,1},{5,2},{6,3},{7,4},{8,5},{9,6},{10... | collective-permute-start | bytes 589832 | tf_op jit(solution)/shard_map/ppermute | solution.py:57
  116.7 3.3 %collective-permute-start.32 = (bf16[5,128,128]{2,1,0:T(8,128)(2,1)S(1)}, bf16[5,128,128]{2,1,0:T(8,128)(2,1)S(1)}, u32[]{:S(2)}, u32[]{:S(2)}) collective-permute-start(bf16[5,128,128]{2,1,0:T(8,128)(2,1)S(1)} %get-tuple-element.72), channel_id=1, source_target_pairs={{0,26},{1,27},{2,28},{3,29},{4,30},{5,31},{6,0},{7,1},{8,2},{9,3},... | collective-permute-start | bytes 491528 | tf_op jit(solution)/shard_map/ppermute | solution.py:57
  119.9 4.8 %collective-permute-start.33 = (bf16[5,128,128]{2,1,0:T(8,128)(2,1)S(1)}, bf16[5,128,128]{2,1,0:T(8,128)(2,1)S(1)}, u32[]{:S(2)}, u32[]{:S(2)}) collective-permute-start(bf16[5,128,128]{2,1,0:T(8,128)(2,1)S(1)} %get-tuple-element.74), channel_id=1, source_target_pairs={{0,6},{1,7},{2,8},{3,9},{4,10},{5,11},{6,12},{7,13},{8,14},{9,15},... | collective-permute-start | bytes 491528 | tf_op jit(solution)/shard_map/ppermute | solution.py:57
  124.7 7.2 %collective-permute-start.34 = (bf16[5,128,128]{2,1,0:T(8,128)(2,1)S(1)}, bf16[5,128,128]{2,1,0:T(8,128)(2,1)S(1)}, u32[]{:S(2)}, u32[]{:S(2)}) collective-permute-start(bf16[5,128,128]{2,1,0:T(8,128)(2,1)S(1)} %get-tuple-element.76), channel_id=1, source_target_pairs={{0,25},{1,26},{2,27},{3,28},{4,29},{5,30},{6,31},{7,0},{8,1},{9,2}... | collective-permute-start | bytes 491528 | tf_op jit(solution)/shard_map/ppermute | solution.py:57
  134.1 7.5 %collective-permute-done.32.refs_14_ = bf16[5,128,128]{2,1,0:T(8,128)(2,1)S(1)} collective-permute-done((bf16[5,128,128]{2,1,0:T(8,128)(2,1)S(1)}, bf16[5,128,128]{2,1,0:T(8,128)(2,1)S(1)}, u32[]{:S(2)}, u32[]{:S(2)}) %collective-permute-start.32) | collective-permute-done | bytes 163872 | tf_op jit(solution)/shard_map/ppermute | solution.py:57
  141.6 3.0 %collective-permute-start.36 = (bf16[2,128,128]{2,1,0:T(8,128)(2,1)S(1)}, bf16[2,128,128]{2,1,0:T(8,128)(2,1)S(1)}, u32[]{:S(2)}, u32[]{:S(2)}) collective-permute-start(bf16[2,128,128]{2,1,0:T(8,128)(2,1)S(1)} %get-tuple-element.80), channel_id=1, source_target_pairs={{0,16},{1,17},{2,18},{3,19},{4,20},{5,21},{6,22},{7,23},{8,24},{9,... | collective-permute-start | bytes 196616 | tf_op jit(solution)/shard_map/ppermute | solution.py:57
  144.6 5.2 %collective-permute-done.36.refs_18_ = bf16[2,128,128]{2,1,0:T(8,128)(2,1)S(1)} collective-permute-done((bf16[2,128,128]{2,1,0:T(8,128)(2,1)S(1)}, bf16[2,128,128]{2,1,0:T(8,128)(2,1)S(1)}, u32[]{:S(2)}, u32[]{:S(2)}) %collective-permute-start.36) | collective-permute-done | bytes 65568 | tf_op jit(solution)/shard_map/ppermute | solution.py:57
  149.8 4.7 %cube.1 = f32[1,16,128,128]{3,2,1,0:T(8,128)} custom-call(s32[4096]{0:T(1024)S(1)} %reshape.3.refs_0_, bf16[16,128,128]{2,1,0:T(8,128)(2,1)} %bitcast.source.refs_1_.refs_10_, f32[128,128]{1,0:T(8,128)S(1)} %get-tuple-element.50.refs_2_, bf16[7,128,128]{2,1,0:T(8,128)(2,1)S(1)} %get-tuple-element.54.refs_3_, ...), custom_call_target="tpu_custom_call" | custom-call | tf_op jit(solution)/shard_map/cube/pallas_call | solution.py:328
  (69 shorter events, 35.5 us)
Async XLA Ops:
  0.0 15.1 %collective-permute-start.9 = (bf16[16,128,128]{2,1,0:T(8,128)(2,1)}, bf16[16,128,128]{2,1,0:T(8,128)(2,1)S(1)}, u32[]{:S(2)}, u32[]{:S(2)}) collective-permute-start(bf16[16,128,128]{2,1,0:T(8,128)(2,1)} %bitcast.source.refs_1_.refs_10_), channel_id=1, source_target_pairs={{0,64},{32,96},{64,128},{96,160},{128,192},{160,224},{192,0},{224,... | collective-permute-start | bytes 1572872 | tf_op jit(solution)/shard_map/ppermute | solution.py:91
  2.7 18.6 %collective-permute-start.4 = (bf16[10,128,128]{2,1,0:T(8,128)(2,1)S(1)}, bf16[10,128,128]{2,1,0:T(8,128)(2,1)S(1)}, u32[]{:S(2)}, u32[]{:S(2)}) collective-permute-start(bf16[10,128,128]{2,1,0:T(8,128)(2,1)S(1)} %get-tuple-element.47), channel_id=1, source_target_pairs={{0,27},{1,28},{2,29},{3,30},{4,31},{5,0},{6,1},{7,2},{8,3},{9,4},{... | collective-permute-start | bytes 983048 | tf_op jit(solution)/shard_map/ppermute | solution.py:57
  8.5 24.1 %collective-permute-start = (bf16[15,128,128]{2,1,0:T(8,128)(2,1)S(1)}, bf16[15,128,128]{2,1,0:T(8,128)(2,1)S(1)}, u32[]{:S(2)}, u32[]{:S(2)}) collective-permute-start(bf16[15,128,128]{2,1,0:T(8,128)(2,1)S(1)} %get-tuple-element.43), channel_id=1, source_target_pairs={{0,1},{1,2},{2,3},{3,4},{4,5},{5,6},{6,7},{7,8},{8,9},{9,10},{10,1... | collective-permute-start | bytes 1474568 | tf_op jit(solution)/shard_map/ppermute | solution.py:57
  11.5 28.2 %collective-permute-start.13 = (bf16[16,128,128]{2,1,0:T(8,128)(2,1)}, bf16[16,128,128]{2,1,0:T(8,128)(2,1)S(1)}, u32[]{:S(2)}, u32[]{:S(2)}) collective-permute-start(bf16[16,128,128]{2,1,0:T(8,128)(2,1)} %bitcast.source.refs_1_.refs_10_), channel_id=1, source_target_pairs={{0,192},{32,224},{64,0},{96,32},{128,64},{160,96},{192,128},{224,1... | collective-permute-start | bytes 1572872 | tf_op jit(solution)/shard_map/ppermute | solution.py:91
  15.1 24.6 %collective-permute-start.8 = (bf16[16,128,128]{2,1,0:T(8,128)(2,1)}, bf16[16,128,128]{2,1,0:T(8,128)(2,1)S(1)}, u32[]{:S(2)}, u32[]{:S(2)}) collective-permute-start(bf16[16,128,128]{2,1,0:T(8,128)(2,1)} %bitcast.source.refs_1_.refs_10_), channel_id=1, source_target_pairs={{0,32},{32,0},{64,96},{96,64},{128,160},{160,128},{192,224},{224,1... | collective-permute-start | bytes 1572872 | tf_op jit(solution)/shard_map/ppermute | solution.py:95
  18.5 21.7 %collective-permute-start.11 = (bf16[16,128,128]{2,1,0:T(8,128)(2,1)}, bf16[16,128,128]{2,1,0:T(8,128)(2,1)S(1)}, u32[]{:S(2)}, u32[]{:S(2)}) collective-permute-start(bf16[16,128,128]{2,1,0:T(8,128)(2,1)} %bitcast.source.refs_1_.refs_10_), channel_id=1, source_target_pairs={{0,128},{32,160},{64,192},{96,224},{128,0},{160,32},{192,64},{224,... | collective-permute-start | bytes 1572872 | tf_op jit(solution)/shard_map/ppermute | solution.py:91
  32.2 14.6 %collective-permute-start.5 = (bf16[8,128,128]{2,1,0:T(8,128)(2,1)S(1)}, bf16[8,128,128]{2,1,0:T(8,128)(2,1)S(1)}, u32[]{:S(2)}, u32[]{:S(2)}) collective-permute-start(bf16[8,128,128]{2,1,0:T(8,128)(2,1)S(1)} %pack.6), channel_id=1, source_target_pairs={{0,31},{1,0},{2,1},{3,2},{4,3},{5,4},{6,5},{7,6},{8,7},{9,8},{10,9... | collective-permute-start | bytes 786440 | tf_op jit(solution)/shard_map/ppermute | solution.py:57
  32.7 15.8 %collective-permute-start.6 = (bf16[7,128,128]{2,1,0:T(8,128)(2,1)S(1)}, bf16[7,128,128]{2,1,0:T(8,128)(2,1)S(1)}, u32[]{:S(2)}, u32[]{:S(2)}) collective-permute-start(bf16[7,128,128]{2,1,0:T(8,128)(2,1)S(1)} %pack.7), channel_id=1, source_target_pairs={{0,3},{1,4},{2,5},{3,6},{4,7},{5,8},{6,9},{7,10},{8,11},{9,12},{10... | collective-permute-start | bytes 688136 | tf_op jit(solution)/shard_map/ppermute | solution.py:57
  39.7 17.4 %collective-permute-start.10 = (bf16[16,128,128]{2,1,0:T(8,128)(2,1)S(1)}, bf16[16,128,128]{2,1,0:T(8,128)(2,1)}, u32[]{:S(2)}, u32[]{:S(2)}) collective-permute-start(bf16[16,128,128]{2,1,0:T(8,128)(2,1)S(1)} %collective-permute-done.9.refs_12_), channel_id=1, source_target_pairs={{0,32},{32,0},{64,96},{96,64},{128,160},{160,128},{192,224},{224,1... | collective-permute-start | bytes 1572872 | tf_op jit(solution)/shard_map/ppermute | solution.py:95
  39.7 17.4 %collective-permute-start.14 = (bf16[16,128,128]{2,1,0:T(8,128)(2,1)S(1)}, bf16[16,128,128]{2,1,0:T(8,128)(2,1)}, u32[]{:S(2)}, u32[]{:S(2)}) collective-permute-start(bf16[16,128,128]{2,1,0:T(8,128)(2,1)S(1)} %collective-permute-done.13.refs_16_), channel_id=1, source_target_pairs={{0,32},{32,0},{64,96},{96,64},{128,160},{160,128},{192,224},{224,1... | collective-permute-start | bytes 1572872 | tf_op jit(solution)/shard_map/ppermute | solution.py:95
  40.2 16.9 %collective-permute-start.12 = (bf16[16,128,128]{2,1,0:T(8,128)(2,1)S(1)}, bf16[16,128,128]{2,1,0:T(8,128)(2,1)}, u32[]{:S(2)}, u32[]{:S(2)}) collective-permute-start(bf16[16,128,128]{2,1,0:T(8,128)(2,1)S(1)} %collective-permute-done.11.refs_14_), channel_id=1, source_target_pairs={{0,32},{32,0},{64,96},{96,64},{128,160},{160,128},{192,224},{224,1... | collective-permute-start | bytes 1572872 | tf_op jit(solution)/shard_map/ppermute | solution.py:95
  66.3 11.4 %collective-permute-start.20 = (bf16[8,128,128]{2,1,0:T(8,128)(2,1)S(1)}, bf16[8,128,128]{2,1,0:T(8,128)(2,1)S(1)}, u32[]{:S(2)}, u32[]{:S(2)}) collective-permute-start(bf16[8,128,128]{2,1,0:T(8,128)(2,1)S(1)} %get-tuple-element.53.refs_1_.refs_3_), channel_id=1, source_target_pairs={{0,192},{32,224},{64,0},{96,32},{128,64},{160,96},{192,128},{224,1... | collective-permute-start | bytes 786440 | tf_op jit(solution)/shard_map/ppermute | solution.py:91
  86.2 11.5 %collective-permute-start.23 = (bf16[7,128,128]{2,1,0:T(8,128)(2,1)S(1)}, bf16[7,128,128]{2,1,0:T(8,128)(2,1)S(1)}, u32[]{:S(2)}, u32[]{:S(2)}) collective-permute-start(bf16[7,128,128]{2,1,0:T(8,128)(2,1)S(1)} %get-tuple-element.56), channel_id=1, source_target_pairs={{0,1},{1,2},{2,3},{3,4},{4,5},{5,6},{6,7},{7,8},{8,9},{9,10},{10,1... | collective-permute-start | bytes 688136 | tf_op jit(solution)/shard_map/ppermute | solution.py:57
  88.2 16.6 %collective-permute-start.30 = (bf16[6,128,128]{2,1,0:T(8,128)(2,1)S(1)}, bf16[6,128,128]{2,1,0:T(8,128)(2,1)S(1)}, u32[]{:S(2)}, u32[]{:S(2)}) collective-permute-start(bf16[6,128,128]{2,1,0:T(8,128)(2,1)S(1)} %get-tuple-element.68), channel_id=1, source_target_pairs={{0,28},{1,29},{2,30},{3,31},{4,0},{5,1},{6,2},{7,3},{8,4},{9,5},{1... | collective-permute-start | bytes 589832 | tf_op jit(solution)/shard_map/ppermute | solution.py:57
  92.8 12.0 %collective-permute-start.25 = (bf16[6,128,128]{2,1,0:T(8,128)(2,1)S(1)}, bf16[6,128,128]{2,1,0:T(8,128)(2,1)S(1)}, u32[]{:S(2)}, u32[]{:S(2)}) collective-permute-start(bf16[6,128,128]{2,1,0:T(8,128)(2,1)S(1)} %get-tuple-element.60), channel_id=1, source_target_pairs={{0,4},{1,5},{2,6},{3,7},{4,8},{5,9},{6,10},{7,11},{8,12},{9,13},{1... | collective-permute-start | bytes 589832 | tf_op jit(solution)/shard_map/ppermute | solution.py:57
  94.5 17.6 %collective-permute-start.24 = (bf16[7,128,128]{2,1,0:T(8,128)(2,1)S(1)}, bf16[7,128,128]{2,1,0:T(8,128)(2,1)S(1)}, u32[]{:S(2)}, u32[]{:S(2)}) collective-permute-start(bf16[7,128,128]{2,1,0:T(8,128)(2,1)S(1)} %get-tuple-element.58), channel_id=1, source_target_pairs={{0,30},{1,31},{2,0},{3,1},{4,2},{5,3},{6,4},{7,5},{8,6},{9,7},{10,... | collective-permute-start | bytes 688136 | tf_op jit(solution)/shard_map/ppermute | solution.py:57
  104.8 11.8 %collective-permute-start.31 = (bf16[6,128,128]{2,1,0:T(8,128)(2,1)S(1)}, bf16[6,128,128]{2,1,0:T(8,128)(2,1)S(1)}, u32[]{:S(2)}, u32[]{:S(2)}) collective-permute-start(bf16[6,128,128]{2,1,0:T(8,128)(2,1)S(1)} %get-tuple-element.70), channel_id=1, source_target_pairs={{0,5},{1,6},{2,7},{3,8},{4,9},{5,10},{6,11},{7,12},{8,13},{9,14},{... | collective-permute-start | bytes 589832 | tf_op jit(solution)/shard_map/ppermute | solution.py:57
  104.8 15.1 %collective-permute-start.26 = (bf16[7,128,128]{2,1,0:T(8,128)(2,1)S(1)}, bf16[7,128,128]{2,1,0:T(8,128)(2,1)S(1)}, u32[]{:S(2)}, u32[]{:S(2)}) collective-permute-start(bf16[7,128,128]{2,1,0:T(8,128)(2,1)S(1)} %get-tuple-element.61), channel_id=1, source_target_pairs={{0,2},{1,3},{2,4},{3,5},{4,6},{5,7},{6,8},{7,9},{8,10},{9,11},{10,... | collective-permute-start | bytes 688136 | tf_op jit(solution)/shard_map/ppermute | solution.py:57
  107.7 24.3 %collective-permute-start.29 = (bf16[7,128,128]{2,1,0:T(8,128)(2,1)S(1)}, bf16[7,128,128]{2,1,0:T(8,128)(2,1)S(1)}, u32[]{:S(2)}, u32[]{:S(2)}) collective-permute-start(bf16[7,128,128]{2,1,0:T(8,128)(2,1)S(1)} %get-tuple-element.67), channel_id=1, source_target_pairs={{0,3},{1,4},{2,5},{3,6},{4,7},{5,8},{6,9},{7,10},{8,11},{9,12},{10... | collective-permute-start | bytes 688136 | tf_op jit(solution)/shard_map/ppermute | solution.py:57
  112.2 12.6 %collective-permute-start.27 = (bf16[6,128,128]{2,1,0:T(8,128)(2,1)S(1)}, bf16[6,128,128]{2,1,0:T(8,128)(2,1)S(1)}, u32[]{:S(2)}, u32[]{:S(2)}) collective-permute-start(bf16[6,128,128]{2,1,0:T(8,128)(2,1)S(1)} %get-tuple-element.63), channel_id=1, source_target_pairs={{0,29},{1,30},{2,31},{3,0},{4,1},{5,2},{6,3},{7,4},{8,5},{9,6},{10... | collective-permute-start | bytes 589832 | tf_op jit(solution)/shard_map/ppermute | solution.py:57
  116.7 24.9 %collective-permute-start.32 = (bf16[5,128,128]{2,1,0:T(8,128)(2,1)S(1)}, bf16[5,128,128]{2,1,0:T(8,128)(2,1)S(1)}, u32[]{:S(2)}, u32[]{:S(2)}) collective-permute-start(bf16[5,128,128]{2,1,0:T(8,128)(2,1)S(1)} %get-tuple-element.72), channel_id=1, source_target_pairs={{0,26},{1,27},{2,28},{3,29},{4,30},{5,31},{6,0},{7,1},{8,2},{9,3},... | collective-permute-start | bytes 491528 | tf_op jit(solution)/shard_map/ppermute | solution.py:57
  119.9 24.6 %collective-permute-start.33 = (bf16[5,128,128]{2,1,0:T(8,128)(2,1)S(1)}, bf16[5,128,128]{2,1,0:T(8,128)(2,1)S(1)}, u32[]{:S(2)}, u32[]{:S(2)}) collective-permute-start(bf16[5,128,128]{2,1,0:T(8,128)(2,1)S(1)} %get-tuple-element.74), channel_id=1, source_target_pairs={{0,6},{1,7},{2,8},{3,9},{4,10},{5,11},{6,12},{7,13},{8,14},{9,15},... | collective-permute-start | bytes 491528 | tf_op jit(solution)/shard_map/ppermute | solution.py:57
  124.7 25.1 %collective-permute-start.34 = (bf16[5,128,128]{2,1,0:T(8,128)(2,1)S(1)}, bf16[5,128,128]{2,1,0:T(8,128)(2,1)S(1)}, u32[]{:S(2)}, u32[]{:S(2)}) collective-permute-start(bf16[5,128,128]{2,1,0:T(8,128)(2,1)S(1)} %get-tuple-element.76), channel_id=1, source_target_pairs={{0,25},{1,26},{2,27},{3,28},{4,29},{5,30},{6,31},{7,0},{8,1},{9,2}... | collective-permute-start | bytes 491528 | tf_op jit(solution)/shard_map/ppermute | solution.py:57
  131.9 17.8 %collective-permute-start.35 = (bf16[4,128,128]{2,1,0:T(8,128)(2,1)S(1)}, bf16[4,128,128]{2,1,0:T(8,128)(2,1)S(1)}, u32[]{:S(2)}, u32[]{:S(2)}) collective-permute-start(bf16[4,128,128]{2,1,0:T(8,128)(2,1)S(1)} %get-tuple-element.78), channel_id=1, source_target_pairs={{0,7},{1,8},{2,9},{3,10},{4,11},{5,12},{6,13},{7,14},{8,15},{9,16}... | collective-permute-start | bytes 393224 | tf_op jit(solution)/shard_map/ppermute | solution.py:57
  (18 other events, 122.4 us)

commit v4 on v0

v4 whole, which is shorter than its diff:
```python
import functools

import jax
import jax.numpy as jnp
from jax import lax
from jax.experimental import pallas as pl
from jax.experimental.pallas import tpu as pltpu
from jax.sharding import PartitionSpec as P

SIGNS = {1: 1, 2: 1, 3: -1, 4: 1, 5: -1, 6: -1, 7: 1}
ROUNDS = [[(1, 5), (-1, -5), (3, 7), (-3, -7)], [(2, 6), (-2, -6)]]
STEP = 4
LONG = {4: [4, 5, 3, 6], -4: [-4, -3, -5, -2], 8: [7], -8: [-7, -6]}
SHORT = [1, -1, 2]


class Plan:
    def __init__(self, slot_count, grid_cols, grid_rows):
        half = (slot_count - 2) // 2
        self.slot_count, self.grid_cols, self.grid_rows = slot_count, grid_cols, grid_rows
        self.far = grid_cols // 2
        self.offsets = [0]
        for stride in range(1, half + 1):
            self.offsets += [stride, -stride]
        self.offsets.append(self.far)
        self.slot = {o: s for s, o in enumerate(self.offsets)}
        self.moved = self.offsets[1:]
        near = self.offsets[1:-1]
        self.kept = [0] + [SIGNS.get(d, 1) * d for d in range(1, half + 1)]
        self.place = {d: p for p, d in enumerate(self.kept)}
        self.edges = {self.far: []}
        for a in near:
            self.edges[a] = [b for b in near if b != a and (a - b) in self.place]
        self.size = {a: 1 + len(self.edges[a]) for a in self.moved}
        self.bundles, self.onward = {}, []
        for number, pairs in enumerate(ROUNDS):
            legs = {STEP: [], -STEP: []}
            if number == 0:
                legs = {STEP: [STEP], -STEP: [-STEP]}
            for f, a in pairs:
                self.bundles[f] = [f, a]
                legs[a - f].append(a)
            self.onward.append(legs)
        self.long = {e: [a for a in LONG[e] if a in self.slot] for e in LONG}
        relayed = [a for e in LONG for a in self.long[e]]
        self.short = {f: [f] + [a for e in LONG for a in self.long[e] if a - e == f] for f in SHORT}
        self.alone = [a for a in self.moved if a not in relayed and a not in SHORT]

    def back(self, a):
        return self.slot[a if a == self.far else -a]

    def row_id(self, rank, col):
        return rank * self.grid_cols + lax.rem(col + 2 * self.grid_cols, self.grid_cols)


def shifted(value, by):
    length = lax.axis_size("col")
    return lax.ppermute(value, "col", [(i, (i + by) % length) for i in range(length)])


def after(value, *others):
    return lax.optimization_barrier((value, *others))[0]


def nn(a, b):
    return lax.dot_general(a, b, (((1,), (0,)), ((), ())), preferred_element_type=jnp.float32)


def nt(a, b):
    return lax.dot_general(a, b, (((1,), (1,)), ((), ())), preferred_element_type=jnp.float32)


def from_chip(block, step):
    length = lax.axis_size("row")
    chips = length // 2
    pairs = [(2 * x + h, 2 * ((x + step) % chips) + h) for x in range(chips) for h in range(2)]
    return lax.ppermute(block, "row", pairs)


def from_core(block):
    return lax.ppermute(block, "row", [(i, i ^ 1) for i in range(lax.axis_size("row"))])


def gather_rows(block):
    chips = lax.axis_size("row") // 2
    same = [block] + [None] * (chips - 1)
    same[1], same[chips - 1] = from_chip(block, 1), from_chip(block, chips - 1)
    for step in range(2, chips - 1):
        held, _ = lax.optimization_barrier((block, same[step - 1]))
        same[step] = from_chip(held, step)
    out = []
    for piece in same:
        out += [piece, from_core(piece)]
    return out


def piece_rank(plan, my_row, index):
    chips = plan.grid_rows // 2
    x = lax.rem(my_row // 2 - index // 2 + chips, chips)
    core = lax.rem(my_row, 2)
    if index % 2:
        core = 1 - core
    return 2 * x + core


def land(plan, my_row, pieces, panel, sems):
    copies = []
    for index, piece in enumerate(pieces):
        copy = pltpu.make_async_copy(piece, panel.at[piece_rank(plan, my_row, index)], sems.at[index])
        copy.start()
        copies.append(copy)
    return copies


def keep_kernel(plan, own, out):
    for p, d in enumerate(plan.kept):
        out[p] = own[plan.slot[-d]]


def pick_kernel(plan, *refs):
    cols, pieces = refs[0], refs[1:1 + plan.grid_rows]
    outs, (panel, sems) = refs[1 + plan.grid_rows:-2], refs[-2:]
    n = plan.slot_count
    my_row, my_col = lax.axis_index("row"), lax.axis_index("col")
    for copy in land(plan, my_row, pieces, panel, sems):
        copy.wait()
    for out, group in zip(outs, pick_groups(plan)):
        at = 0
        for a in group:
            i = plan.row_id(my_row, my_col - a)
            rank = cols[i * n + plan.slot[a]] // plan.grid_cols
            out[at] = panel[rank, 0]
            for p, b in enumerate(plan.edges[a]):
                out[at + p + 1] = panel[rank, plan.place[a - b]]
            at += plan.size[a]


def pick_groups(plan):
    return list(plan.bundles.values()) + [[STEP], [-STEP], [plan.far]]


def total_size(plan, group):
    return sum(plan.size[a] for a in group)


def start_of(plan, group, a):
    return total_size(plan, group[:group.index(a)])


def onward_kernel(plan, number, held, *refs):
    outs = refs[len(held):]
    for out, group in zip(outs, plan.onward[number].values()):
        at = 0
        for a in group:
            source = [a in h for h in held].index(True)
            first = start_of(plan, held[source], a)
            for p in range(plan.size[a]):
                out[at + p] = refs[source][first + p]
            at += plan.size[a]


class Part:
    def __init__(self, ref, first):
        self.ref, self.first = ref, first

    def __getitem__(self, p):
        return self.ref[self.first + p]


def product_kernel(plan, held, *refs):
    cols, own = refs[:2]
    arrived = {}
    for ref, group in zip(refs[2:2 + len(held)], held):
        for a in group:
            arrived[a] = Part(ref, start_of(plan, group, a))
    away, self_new, total, half = refs[2 + len(held):]
    n = plan.slot_count
    i = plan.row_id(lax.axis_index("row"), lax.axis_index("col"))

    def add_edges(left, scale):
        for a in plan.moved:
            for p, b in enumerate(plan.edges[a]):
                ta, tb = plan.slot[a], plan.slot[b]
                k, j = cols[i * n + ta], cols[i * n + tb]

                @pl.when(cols[k * n + plan.slot[b - a]] == j)
                def _():
                    edge = arrived[a][p + 1]
                    total[tb] += scale * nn(left[ta], edge)
                    total[ta] += scale * nt(left[tb], edge)

    acc = nt(own[0], own[0])
    for s in range(1, n):
        acc = acc + nt(own[s], own[s])
    total[0] = acc
    half[0] = acc.astype(half.dtype)
    for a in plan.moved:
        t = plan.slot[a]
        total[t] = nn(own[0], own[t]) + nn(own[t], arrived[a][0])
    add_edges(own, 1.0)
    for t in range(1, n):
        half[t] = total[t].astype(half.dtype)
    acc = nt(own[0], half[0])
    for s in range(1, n):
        acc = acc + nt(own[s], half[s])
    self_new[...] = 3.0 * total[0] - 2.0 * acc
    for a in plan.moved:
        t = plan.slot[a]
        cube = nn(half[0], own[t]) + nn(half[t], arrived[a][0])
        total[t] = 3.0 * total[t] - 2.0 * cube
    add_edges(half, -2.0)
    for t in range(1, n):
        away[t - 1] = total[t].astype(away.dtype)


def home_kernel(plan, *refs):
    cols, pieces, outs = refs[0], refs[1:1 + plan.grid_rows], refs[1 + plan.grid_rows:]
    n = plan.slot_count
    my_row, my_col = lax.axis_index("row"), lax.axis_index("col")
    for out, group in zip(outs, home_groups(plan)):
        for p, a in enumerate(group):
            i = plan.row_id(my_row, my_col - a)
            rank = cols[i * n + plan.slot[a]] // plan.grid_cols
            for index, piece in enumerate(pieces):

                @pl.when(rank == piece_rank(plan, my_row, index))
                def _():
                    out[p] = piece[plan.back(a) - 1]


def home_groups(plan):
    return [plan.long[e] for e in LONG] + [SHORT] + [[a] for a in plan.alone]


def relay_kernel(plan, *refs):
    longs, near = dict(zip(LONG, refs)), refs[len(LONG)]
    for out, f in zip(refs[len(LONG) + 1:], SHORT):
        out[0] = near[SHORT.index(f)]
        for p, a in enumerate(plan.short[f][1:]):
            e = a - f
            out[p + 1] = longs[e][plan.long[e].index(a)]


def finish_kernel(where, self_new, *refs):
    out = refs[-1]
    out[0, 0] = self_new[...]
    for t, (source, p) in where.items():
        out[0, t] = refs[source][p].astype(jnp.float32).T


VMEM = pl.BlockSpec(memory_space=pltpu.VMEM)
SMEM = pl.BlockSpec(memory_space=pltpu.SMEM)
ANY = pl.BlockSpec(memory_space=pl.ANY)
SMALL = pltpu.CompilerParams(vmem_limit_bytes=12 << 20)


def call(kernel, name, args, specs, outs, scratch=()):
    return pl.pallas_call(
        kernel,
        out_shape=[jax.ShapeDtypeStruct(shape, dtype) for shape, dtype in outs],
        in_specs=specs,
        out_specs=[VMEM] * len(outs),
        scratch_shapes=list(scratch),
        compiler_params=SMALL,
        name=name,
    )(*args)


def per_device(density, cols):
    slot_count, block = density.shape[1], density.shape[2:]
    plan = Plan(slot_count, lax.axis_size("col"), lax.axis_size("row"))
    own, dtype, rows = density[0], density.dtype, plan.grid_rows
    table = cols.reshape(-1)
    n_moved = len(plan.moved)

    def panel_scratch(blocks):
        return [pltpu.VMEM((rows, blocks, *block), dtype), pltpu.SemaphoreType.DMA((rows,))]

    n_kept = len(plan.kept)
    (kept,) = call(
        functools.partial(keep_kernel, plan), "keep", [own], [VMEM], [((n_kept, *block), dtype)]
    )
    groups = pick_groups(plan)
    picked = call(
        functools.partial(pick_kernel, plan), "pick",
        [table, *gather_rows(kept)], [SMEM] + [ANY] * rows,
        [((total_size(plan, g), *block), dtype) for g in groups],
        panel_scratch(n_kept),
    )
    *bundles, up, down, far = picked
    far = shifted(far, -plan.far)
    came, held, last = [], [], []
    for number, pairs in enumerate(ROUNDS):
        arrays, contents = [], []
        for index, (f, a) in enumerate(pairs):
            message = bundles[list(plan.bundles).index(f)]
            if last:
                message = after(message, last[index], far)
            arrays.append(shifted(message, -f))
            contents.append(plan.bundles[f])
        last = arrays
        came, held = came + arrays, held + contents
        if number == 0:
            arrays, contents = arrays + [up, down], contents + [[STEP], [-STEP]]
        legs = plan.onward[number]
        joined = call(
            functools.partial(onward_kernel, plan, number, contents), "onward",
            arrays, [VMEM] * len(arrays),
            [((total_size(plan, g), *block), dtype) for g in legs.values()],
        )
        came += [shifted(m, -e) for m, e in zip(joined, legs)]
        held += list(legs.values())
    came.append(far)
    held = [[f for f in g] for g in held] + [[plan.far]]
    away, self_new = call(
        functools.partial(product_kernel, plan, held), "product",
        [table, own, *came], [SMEM] + [VMEM] * (1 + len(came)),
        [((n_moved, *block), dtype), (block, jnp.float32)],
        [pltpu.VMEM((slot_count, *block), jnp.float32), pltpu.VMEM((slot_count, *block), dtype)],
    )
    groups = home_groups(plan)
    homing = call(
        functools.partial(home_kernel, plan), "home",
        [table, *gather_rows(away)], [SMEM] + [VMEM] * rows,
        [((len(g), *block), dtype) for g in groups],
    )
    n_long = len(LONG)
    longs = [shifted(m, -e) for m, e in zip(homing, LONG)]
    alone = [shifted(m, -a) for m, a in zip(homing[n_long + 1:], plan.alone)]
    longs = list(lax.optimization_barrier((*longs, *alone)))
    longs, alone = longs[:n_long], longs[n_long:]
    relayed = call(
        functools.partial(relay_kernel, plan), "relay",
        [*longs, homing[n_long]], [VMEM] * (n_long + 1),
        [((len(plan.short[f]), *block), dtype) for f in SHORT],
    )
    shorts = [shifted(m, -f) for m, f in zip(relayed, SHORT)]
    came = longs + alone + shorts
    where = {}
    for source, e in enumerate(LONG):
        if e in plan.long[e]:
            where[plan.slot[e]] = (source, plan.long[e].index(e))
    for source, a in enumerate(plan.alone):
        where[plan.slot[a]] = (n_long + source, 0)
    for source, f in enumerate(SHORT):
        for p, a in enumerate(plan.short[f]):
            where[plan.slot[a]] = (n_long + len(alone) + source, p)
    (new,) = call(
        functools.partial(finish_kernel, where), "finish",
        [self_new, *came], [VMEM] * (1 + len(came)),
        [((1, slot_count, *block), jnp.float32)],
    )
    return new


def solution(mesh):
    in_specs = (P(("row", "col"), None, None, None), P())
    out_specs = P(("row", "col"), None, None, None)
    return jax.shard_map(
        per_device, mesh=mesh, in_specs=in_specs, out_specs=out_specs, check_vma=False
    )
```

time: 314 us -> 142 us (0.45); the launches traced: 310 us -> 143 us
  waiting for transfers between devices: 202 us -> 82.3 us
  local copies, waits for them, and re-layouts: 41.3 us -> 1.25 us
  matrix products: 17.2 us -> 0 us
  between operations: 13.4 us -> 0.16 us
  starting transfers between devices: 34.9 us -> 48.1 us
  Pallas kernels: 0 us -> 11.3 us
    all_gather x3 -> x0, waiting for transfers between devices: 194 us -> none  [the longest x1 132 us: per_device(): gathered = lax.all_gather(density, 'col', axis=0, tiled=True)]
    ppermute x15 -> x33, waiting for transfers between devices: 6.15 us -> 82.3 us  [the longest x19 49 us: shifted(): lax.ppermute(value, 'col', [(i, (i + by) % length) for i in range(length)])]
    gather x8 -> x0, local copies, waits for them, and re-layouts: 38.7 us -> none  [the longest x3 14.2 us: per_device(): from_square = square_panel[inner_row, mirror[found_slot], inner_local]]
    dot_general x2 -> x0, matrix products: 17.2 us -> none  [the longest x1 9 us: per_device(): jnp.einsum('sltab,sltcb->slac', left_blocks, right_blocks, preferred_elem...]
    ppermute x15 -> x33, starting transfers between devices: 34.8 us -> 48.1 us  [the longest x19 37.2 us: shifted(): lax.ppermute(value, 'col', [(i, (i + by) % length) for i in range(length)])]
    pallas_call x0 -> x8, Pallas kernels: none -> 11.3 us  [call(): pl.pallas_call(kernel, out_shape=[jax.ShapeDtypeStruct(shape, dtype) for...]
  transfers between devices with their start and end apart: 18 -> 33, of which waited for: 6 -> 15; matrix products, arithmetic and copies ran while one was open for 6% -> 0% of each run, Pallas kernels for 0% -> 0%
where the time goes in v4:
time: 142 us; the launch traced here: 143 us
  waiting for transfers between devices  82.3 us (58%)
  starting transfers between devices  48.1 us (34%)
  Pallas kernels  11.3 us (8%)
    ppermute x19, waiting for transfers between devices, shifted(): lax.ppermute(value, 'col', [(i, (i + by) % length) for i in range(length)])  49 us
    ppermute x19, starting transfers between devices, shifted(): lax.ppermute(value, 'col', [(i, (i + by) % length) for i in range(length)])  37.2 us
    ppermute x6, waiting for transfers between devices, from_chip(): return lax.ppermute(block, 'row', pairs)  30.2 us
    pallas_call x8, Pallas kernels, call(): pl.pallas_call(kernel, out_shape=[jax.ShapeDtypeStruct(shape, dtype) for...  11.3 us
    ppermute x6, starting transfers between devices, from_chip(): return lax.ppermute(block, 'row', pairs)  9.88 us
    ppermute x8, waiting for transfers between devices, from_core(): lax.ppermute(block, 'row', [(i, i ^ 1) for i in range(lax.axis_size('row'...  3.15 us
  transfers between devices with their start and end apart: 33, of which 15 were waited for; matrix products, arithmetic and copies ran while one was open for 0% of the time, Pallas kernels for 0%

profile of v4, /device:TPU:2, one launch (start us, length us, event | category | flops | bytes accessed | tf_op | source)
XLA Modules:
  0.0 143.1 jit_solution(15005866646265422512)
XLA Ops:
  3.5 5.7 %collective-permute-done.1.refs_3_ = bf16[8,128,128]{2,1,0:T(8,128)(2,1)S(1)} collective-permute-done((bf16[8,128,128]{2,1,0:T(8,128)(2,1)S(1)}, bf16[8,128,128]{2,1,0:T(8,128)(2,1)S(1)}, u32[]{:S(2)}, u32[]{:S(2)}) %collective-permute-start.1) | collective-permute-done | bytes 262176 | tf_op jit(solution)/shard_map/ppermute | solution.py:77
  9.2 2.1 %collective-permute-start.3 = (bf16[8,128,128]{2,1,0:T(8,128)(2,1)S(1)}, bf16[8,128,128]{2,1,0:T(8,128)(2,1)S(1)}, u32[]{:S(2)}, u32[]{:S(2)}) collective-permute-start(bf16[8,128,128]{2,1,0:T(8,128)(2,1)S(1)} %keep.1.refs_1_), channel_id=1, source_target_pairs={{0,128},{32,160},{64,192},{96,224},{128,0},{160,32},{192,64},{224,... | collective-permute-start | bytes 786440 | tf_op jit(solution)/shard_map/ppermute | solution.py:77
  11.8 5.7 %collective-permute-done.3.refs_5_ = bf16[8,128,128]{2,1,0:T(8,128)(2,1)S(1)} collective-permute-done((bf16[8,128,128]{2,1,0:T(8,128)(2,1)S(1)}, bf16[8,128,128]{2,1,0:T(8,128)(2,1)S(1)}, u32[]{:S(2)}, u32[]{:S(2)}) %collective-permute-start.3) | collective-permute-done | bytes 262176 | tf_op jit(solution)/shard_map/ppermute | solution.py:77
  20.4 8.7 %collective-permute-start.7 = (bf16[12,128,128]{2,1,0:T(8,128)(2,1)S(1)}, bf16[12,128,128]{2,1,0:T(8,128)(2,1)S(1)}, u32[]{:S(2)}, u32[]{:S(2)}) collective-permute-start(bf16[12,128,128]{2,1,0:T(8,128)(2,1)S(1)} %get-tuple-element.39), channel_id=1, source_target_pairs={{0,31},{1,0},{2,1},{3,2},{4,3},{5,4},{6,5},{7,6},{8,7},{9,8},{10,9... | collective-permute-start | bytes 1179656 | tf_op jit(solution)/shard_map/ppermute | solution.py:58
  29.6 2.6 %collective-permute-start.10 = (bf16[10,128,128]{2,1,0:T(8,128)(2,1)S(1)}, bf16[10,128,128]{2,1,0:T(8,128)(2,1)S(1)}, u32[]{:S(2)}, u32[]{:S(2)}) collective-permute-start(bf16[10,128,128]{2,1,0:T(8,128)(2,1)S(1)} %get-tuple-element.42), channel_id=1, source_target_pairs={{0,3},{1,4},{2,5},{3,6},{4,7},{5,8},{6,9},{7,10},{8,11},{9,12},{10... | collective-permute-start | bytes 983048 | tf_op jit(solution)/shard_map/ppermute | solution.py:58
  32.3 2.8 %collective-permute-start.13 = (bf16[1,128,128]{2,1,0:T(8,128)(2,1)S(1)}, bf16[1,128,128]{2,1,0:T(8,128)(2,1)S(1)}, u32[]{:S(2)}, u32[]{:S(2)}) collective-permute-start(bf16[1,128,128]{2,1,0:T(8,128)(2,1)S(1)} %get-tuple-element.48), channel_id=1, source_target_pairs={{0,16},{1,17},{2,18},{3,19},{4,20},{5,21},{6,22},{7,23},{8,24},{9,... | collective-permute-start | bytes 98312 | tf_op jit(solution)/shard_map/ppermute | solution.py:58
  35.1 5.0 %collective-permute-done.13.refs_12_ = bf16[1,128,128]{2,1,0:T(8,128)(2,1)S(1)} collective-permute-done((bf16[1,128,128]{2,1,0:T(8,128)(2,1)S(1)}, bf16[1,128,128]{2,1,0:T(8,128)(2,1)S(1)}, u32[]{:S(2)}, u32[]{:S(2)}) %collective-permute-start.13) | collective-permute-done | bytes 32800 | tf_op jit(solution)/shard_map/ppermute | solution.py:58
  40.1 5.2 %collective-permute-start.14 = (bf16[11,128,128]{2,1,0:T(8,128)(2,1)S(1)}, bf16[11,128,128]{2,1,0:T(8,128)(2,1)S(1)}, u32[]{:S(2)}, u32[]{:S(2)}) collective-permute-start(bf16[11,128,128]{2,1,0:T(8,128)(2,1)S(1)} %get-tuple-element.49), channel_id=1, source_target_pairs={{0,30},{1,31},{2,0},{3,1},{4,2},{5,3},{6,4},{7,5},{8,6},{9,7},{10,... | collective-permute-start | bytes 1081352 | tf_op jit(solution)/shard_map/ppermute | solution.py:58
  46.0 17.6 %collective-permute-done.9.refs_2_.refs_4_ = bf16[10,128,128]{2,1,0:T(8,128)(2,1)S(1)} collective-permute-done((bf16[10,128,128]{2,1,0:T(8,128)(2,1)S(1)}, bf16[10,128,128]{2,1,0:T(8,128)(2,1)S(1)}, u32[]{:S(2)}, u32[]{:S(2)}) %collective-permute-start.9) | collective-permute-done | bytes 327712 | tf_op jit(solution)/shard_map/ppermute | solution.py:58
  63.8 3.2 %collective-permute-start.11 = (bf16[14,128,128]{2,1,0:T(8,128)(2,1)S(1)}, bf16[14,128,128]{2,1,0:T(8,128)(2,1)S(1)}, u32[]{:S(2)}, u32[]{:S(2)}) collective-permute-start(bf16[14,128,128]{2,1,0:T(8,128)(2,1)S(1)} %get-tuple-element.45), channel_id=1, source_target_pairs={{0,28},{1,29},{2,30},{3,31},{4,0},{5,1},{6,2},{7,3},{8,4},{9,5},{1... | collective-permute-start | bytes 1376264 | tf_op jit(solution)/shard_map/ppermute | solution.py:58
  67.3 2.0 %collective-permute-start.17 = (bf16[4,128,128]{2,1,0:T(8,128)(2,1)S(1)}, bf16[4,128,128]{2,1,0:T(8,128)(2,1)S(1)}, u32[]{:S(2)}, u32[]{:S(2)}) collective-permute-start(bf16[4,128,128]{2,1,0:T(8,128)(2,1)S(1)} %get-tuple-element.53), channel_id=1, source_target_pairs={{0,4},{1,5},{2,6},{3,7},{4,8},{5,9},{6,10},{7,11},{8,12},{9,13},{1... | collective-permute-start | bytes 393224 | tf_op jit(solution)/shard_map/ppermute | solution.py:58
  69.3 8.1 %collective-permute-done.11.refs_6_ = bf16[14,128,128]{2,1,0:T(8,128)(2,1)S(1)} collective-permute-done((bf16[14,128,128]{2,1,0:T(8,128)(2,1)S(1)}, bf16[14,128,128]{2,1,0:T(8,128)(2,1)S(1)}, u32[]{:S(2)}, u32[]{:S(2)}) %collective-permute-start.11) | collective-permute-done | bytes 458784 | tf_op jit(solution)/shard_map/ppermute | solution.py:58
  77.4 2.5 %collective-permute-done.17.refs_11_ = bf16[4,128,128]{2,1,0:T(8,128)(2,1)S(1)} collective-permute-done((bf16[4,128,128]{2,1,0:T(8,128)(2,1)S(1)}, bf16[4,128,128]{2,1,0:T(8,128)(2,1)S(1)}, u32[]{:S(2)}, u32[]{:S(2)}) %collective-permute-start.17) | collective-permute-done | bytes 131104 | tf_op jit(solution)/shard_map/ppermute | solution.py:58
  79.9 7.0 %product.1 = (bf16[15,128,128]{2,1,0:T(8,128)(2,1)S(1)}, f32[128,128]{1,0:T(8,128)S(1)}) custom-call(s32[4096]{0:T(1024)S(1)} %reshape.3.refs_0_, bf16[16,128,128]{2,1,0:T(8,128)(2,1)S(1)} %bitcast.2, bf16[12,128,128]{2,1,0:T(8,128)(2,1)S(1)} %collective-permute-done.7.refs_0_.refs_2_, bf16[12,128,128]{2,1,0:T(8,128)(2,1)S(1)} %collective-permute-done.8.refs_1_.refs_3_, ...), custom_call_target="tpu_custom_call" | custom-call | tf_op jit(solution)/shard_map/product/pallas_call | solution.py:258
  87.9 2.9 %collective-permute-start.23 = (bf16[15,128,128]{2,1,0:T(8,128)(2,1)S(1)}, bf16[15,128,128]{2,1,0:T(8,128)(2,1)S(1)}, u32[]{:S(2)}, u32[]{:S(2)}) collective-permute-start(bf16[15,128,128]{2,1,0:T(8,128)(2,1)S(1)} %get-tuple-element.56.refs_1_), channel_id=1, source_target_pairs={{0,192},{32,224},{64,0},{96,32},{128,64},{160,96},{192,128},{224,1... | collective-permute-start | bytes 1474568 | tf_op jit(solution)/shard_map/ppermute | solution.py:77
  90.8 8.4 %collective-permute-done.19.refs_3_ = bf16[15,128,128]{2,1,0:T(8,128)(2,1)S(1)} collective-permute-done((bf16[15,128,128]{2,1,0:T(8,128)(2,1)S(1)}, bf16[15,128,128]{2,1,0:T(8,128)(2,1)S(1)}, u32[]{:S(2)}, u32[]{:S(2)}) %collective-permute-start.19) | collective-permute-done | bytes 491552 | tf_op jit(solution)/shard_map/ppermute | solution.py:77
  101.2 10.3 %collective-permute-done.21.refs_5_ = bf16[15,128,128]{2,1,0:T(8,128)(2,1)S(1)} collective-permute-done((bf16[15,128,128]{2,1,0:T(8,128)(2,1)S(1)}, bf16[15,128,128]{2,1,0:T(8,128)(2,1)S(1)}, u32[]{:S(2)}, u32[]{:S(2)}) %collective-permute-start.21) | collective-permute-done | bytes 491552 | tf_op jit(solution)/shard_map/ppermute | solution.py:77
  111.5 1.8 %collective-permute-done.22.refs_6_ = bf16[15,128,128]{2,1,0:T(8,128)(2,1)S(1)} collective-permute-done((bf16[15,128,128]{2,1,0:T(8,128)(2,1)S(1)}, bf16[15,128,128]{2,1,0:T(8,128)(2,1)S(1)}, u32[]{:S(2)}, u32[]{:S(2)}) %collective-permute-start.22) | collective-permute-done | bytes 491552 | tf_op jit(solution)/shard_map/ppermute | solution.py:81
  115.1 4.8 %collective-permute-start.25 = (bf16[4,128,128]{2,1,0:T(8,128)(2,1)S(1)}, bf16[4,128,128]{2,1,0:T(8,128)(2,1)S(1)}, u32[]{:S(2)}, u32[]{:S(2)}) collective-permute-start(bf16[4,128,128]{2,1,0:T(8,128)(2,1)S(1)} %get-tuple-element.57), channel_id=1, source_target_pairs={{0,28},{1,29},{2,30},{3,31},{4,0},{5,1},{6,2},{7,3},{8,4},{9,5},{1... | collective-permute-start | bytes 393224 | tf_op jit(solution)/shard_map/ppermute | solution.py:58
  119.9 4.1 %collective-permute-start.27 = (bf16[1,128,128]{2,1,0:T(8,128)(2,1)S(1)}, bf16[1,128,128]{2,1,0:T(8,128)(2,1)S(1)}, u32[]{:S(2)}, u32[]{:S(2)}) collective-permute-start(bf16[1,128,128]{2,1,0:T(8,128)(2,1)S(1)} %get-tuple-element.59), channel_id=1, source_target_pairs={{0,24},{1,25},{2,26},{3,27},{4,28},{5,29},{6,30},{7,31},{8,0},{9,1... | collective-permute-start | bytes 98312 | tf_op jit(solution)/shard_map/ppermute | solution.py:58
  125.9 6.1 %collective-permute-done.29.refs_4_ = bf16[1,128,128]{2,1,0:T(8,128)(2,1)S(1)} collective-permute-done((bf16[1,128,128]{2,1,0:T(8,128)(2,1)S(1)}, bf16[1,128,128]{2,1,0:T(8,128)(2,1)S(1)}, u32[]{:S(2)}, u32[]{:S(2)}) %collective-permute-start.29) | collective-permute-done | bytes 32800 | tf_op jit(solution)/shard_map/ppermute | solution.py:58
  132.1 2.0 %collective-permute-start.31 = (bf16[4,128,128]{2,1,0:T(8,128)(2,1)S(1)}, bf16[4,128,128]{2,1,0:T(8,128)(2,1)S(1)}, u32[]{:S(2)}, u32[]{:S(2)}) collective-permute-start(bf16[4,128,128]{2,1,0:T(8,128)(2,1)S(1)} %get-tuple-element.69), channel_id=1, source_target_pairs={{0,1},{1,2},{2,3},{3,4},{4,5},{5,6},{6,7},{7,8},{8,9},{9,10},{10,1... | collective-permute-start | bytes 393224 | tf_op jit(solution)/shard_map/ppermute | solution.py:58
  134.2 4.2 %collective-permute-done.30.refs_5_ = bf16[4,128,128]{2,1,0:T(8,128)(2,1)S(1)} collective-permute-done((bf16[4,128,128]{2,1,0:T(8,128)(2,1)S(1)}, bf16[4,128,128]{2,1,0:T(8,128)(2,1)S(1)}, u32[]{:S(2)}, u32[]{:S(2)}) %collective-permute-start.30) | collective-permute-done | bytes 131104 | tf_op jit(solution)/shard_map/ppermute | solution.py:58
  138.3 3.3 %collective-permute-done.31.refs_6_ = bf16[4,128,128]{2,1,0:T(8,128)(2,1)S(1)} collective-permute-done((bf16[4,128,128]{2,1,0:T(8,128)(2,1)S(1)}, bf16[4,128,128]{2,1,0:T(8,128)(2,1)S(1)}, u32[]{:S(2)}, u32[]{:S(2)}) %collective-permute-start.31) | collective-permute-done | bytes 131104 | tf_op jit(solution)/shard_map/ppermute | solution.py:58
  (58 shorter events, 16.5 us)
Async XLA Ops:
  1.1 8.1 %collective-permute-start.1 = (bf16[8,128,128]{2,1,0:T(8,128)(2,1)S(1)}, bf16[8,128,128]{2,1,0:T(8,128)(2,1)S(1)}, u32[]{:S(2)}, u32[]{:S(2)}) collective-permute-start(bf16[8,128,128]{2,1,0:T(8,128)(2,1)S(1)} %keep.1.refs_1_), channel_id=1, source_target_pairs={{0,64},{32,96},{64,128},{96,160},{128,192},{160,224},{192,0},{224,... | collective-permute-start | bytes 786440 | tf_op jit(solution)/shard_map/ppermute | solution.py:77
  2.6 9.2 %collective-permute-start.5 = (bf16[8,128,128]{2,1,0:T(8,128)(2,1)S(1)}, bf16[8,128,128]{2,1,0:T(8,128)(2,1)S(1)}, u32[]{:S(2)}, u32[]{:S(2)}) collective-permute-start(bf16[8,128,128]{2,1,0:T(8,128)(2,1)S(1)} %keep.1.refs_1_), channel_id=1, source_target_pairs={{0,192},{32,224},{64,0},{96,32},{128,64},{160,96},{192,128},{224,1... | collective-permute-start | bytes 786440 | tf_op jit(solution)/shard_map/ppermute | solution.py:77
  9.2 8.4 %collective-permute-start.3 = (bf16[8,128,128]{2,1,0:T(8,128)(2,1)S(1)}, bf16[8,128,128]{2,1,0:T(8,128)(2,1)S(1)}, u32[]{:S(2)}, u32[]{:S(2)}) collective-permute-start(bf16[8,128,128]{2,1,0:T(8,128)(2,1)S(1)} %keep.1.refs_1_), channel_id=1, source_target_pairs={{0,128},{32,160},{64,192},{96,224},{128,0},{160,32},{192,64},{224,... | collective-permute-start | bytes 786440 | tf_op jit(solution)/shard_map/ppermute | solution.py:77
  20.4 19.8 %collective-permute-start.7 = (bf16[12,128,128]{2,1,0:T(8,128)(2,1)S(1)}, bf16[12,128,128]{2,1,0:T(8,128)(2,1)S(1)}, u32[]{:S(2)}, u32[]{:S(2)}) collective-permute-start(bf16[12,128,128]{2,1,0:T(8,128)(2,1)S(1)} %get-tuple-element.39), channel_id=1, source_target_pairs={{0,31},{1,0},{2,1},{3,2},{4,3},{5,4},{6,5},{7,6},{8,7},{9,8},{10,9... | collective-permute-start | bytes 1179656 | tf_op jit(solution)/shard_map/ppermute | solution.py:58
  29.0 16.3 %collective-permute-start.8 = (bf16[12,128,128]{2,1,0:T(8,128)(2,1)S(1)}, bf16[12,128,128]{2,1,0:T(8,128)(2,1)S(1)}, u32[]{:S(2)}, u32[]{:S(2)}) collective-permute-start(bf16[12,128,128]{2,1,0:T(8,128)(2,1)S(1)} %get-tuple-element.40), channel_id=1, source_target_pairs={{0,1},{1,2},{2,3},{3,4},{4,5},{5,6},{6,7},{7,8},{8,9},{9,10},{10,1... | collective-permute-start | bytes 1179656 | tf_op jit(solution)/shard_map/ppermute | solution.py:58
  29.0 34.6 %collective-permute-start.9 = (bf16[10,128,128]{2,1,0:T(8,128)(2,1)S(1)}, bf16[10,128,128]{2,1,0:T(8,128)(2,1)S(1)}, u32[]{:S(2)}, u32[]{:S(2)}) collective-permute-start(bf16[10,128,128]{2,1,0:T(8,128)(2,1)S(1)} %get-tuple-element.41), channel_id=1, source_target_pairs={{0,29},{1,30},{2,31},{3,0},{4,1},{5,2},{6,3},{7,4},{8,5},{9,6},{10... | collective-permute-start | bytes 983048 | tf_op jit(solution)/shard_map/ppermute | solution.py:58
  29.6 34.0 %collective-permute-start.10 = (bf16[10,128,128]{2,1,0:T(8,128)(2,1)S(1)}, bf16[10,128,128]{2,1,0:T(8,128)(2,1)S(1)}, u32[]{:S(2)}, u32[]{:S(2)}) collective-permute-start(bf16[10,128,128]{2,1,0:T(8,128)(2,1)S(1)} %get-tuple-element.42), channel_id=1, source_target_pairs={{0,3},{1,4},{2,5},{3,6},{4,7},{5,8},{6,9},{7,10},{8,11},{9,12},{10... | collective-permute-start | bytes 983048 | tf_op jit(solution)/shard_map/ppermute | solution.py:58
  40.1 26.9 %collective-permute-start.14 = (bf16[11,128,128]{2,1,0:T(8,128)(2,1)S(1)}, bf16[11,128,128]{2,1,0:T(8,128)(2,1)S(1)}, u32[]{:S(2)}, u32[]{:S(2)}) collective-permute-start(bf16[11,128,128]{2,1,0:T(8,128)(2,1)S(1)} %get-tuple-element.49), channel_id=1, source_target_pairs={{0,30},{1,31},{2,0},{3,1},{4,2},{5,3},{6,4},{7,5},{8,6},{9,7},{10,... | collective-permute-start | bytes 1081352 | tf_op jit(solution)/shard_map/ppermute | solution.py:58
  45.4 21.6 %collective-permute-start.15 = (bf16[11,128,128]{2,1,0:T(8,128)(2,1)S(1)}, bf16[11,128,128]{2,1,0:T(8,128)(2,1)S(1)}, u32[]{:S(2)}, u32[]{:S(2)}) collective-permute-start(bf16[11,128,128]{2,1,0:T(8,128)(2,1)S(1)} %get-tuple-element.51), channel_id=1, source_target_pairs={{0,2},{1,3},{2,4},{3,5},{4,6},{5,7},{6,8},{7,9},{8,10},{9,11},{10,... | collective-permute-start | bytes 1081352 | tf_op jit(solution)/shard_map/ppermute | solution.py:58
  63.7 16.2 %collective-permute-start.12 = (bf16[15,128,128]{2,1,0:T(8,128)(2,1)S(1)}, bf16[15,128,128]{2,1,0:T(8,128)(2,1)S(1)}, u32[]{:S(2)}, u32[]{:S(2)}) collective-permute-start(bf16[15,128,128]{2,1,0:T(8,128)(2,1)S(1)} %get-tuple-element.46), channel_id=1, source_target_pairs={{0,4},{1,5},{2,6},{3,7},{4,8},{5,9},{6,10},{7,11},{8,12},{9,13},{1... | collective-permute-start | bytes 1474568 | tf_op jit(solution)/shard_map/ppermute | solution.py:58
  63.8 13.6 %collective-permute-start.11 = (bf16[14,128,128]{2,1,0:T(8,128)(2,1)S(1)}, bf16[14,128,128]{2,1,0:T(8,128)(2,1)S(1)}, u32[]{:S(2)}, u32[]{:S(2)}) collective-permute-start(bf16[14,128,128]{2,1,0:T(8,128)(2,1)S(1)} %get-tuple-element.45), channel_id=1, source_target_pairs={{0,28},{1,29},{2,30},{3,31},{4,0},{5,1},{6,2},{7,3},{8,4},{9,5},{1... | collective-permute-start | bytes 1376264 | tf_op jit(solution)/shard_map/ppermute | solution.py:58
  67.0 12.9 %collective-permute-start.16 = (bf16[5,128,128]{2,1,0:T(8,128)(2,1)S(1)}, bf16[5,128,128]{2,1,0:T(8,128)(2,1)S(1)}, u32[]{:S(2)}, u32[]{:S(2)}) collective-permute-start(bf16[5,128,128]{2,1,0:T(8,128)(2,1)S(1)} %get-tuple-element.52), channel_id=1, source_target_pairs={{0,28},{1,29},{2,30},{3,31},{4,0},{5,1},{6,2},{7,3},{8,4},{9,5},{1... | collective-permute-start | bytes 491528 | tf_op jit(solution)/shard_map/ppermute | solution.py:58
  67.3 12.6 %collective-permute-start.17 = (bf16[4,128,128]{2,1,0:T(8,128)(2,1)S(1)}, bf16[4,128,128]{2,1,0:T(8,128)(2,1)S(1)}, u32[]{:S(2)}, u32[]{:S(2)}) collective-permute-start(bf16[4,128,128]{2,1,0:T(8,128)(2,1)S(1)} %get-tuple-element.53), channel_id=1, source_target_pairs={{0,4},{1,5},{2,6},{3,7},{4,8},{5,9},{6,10},{7,11},{8,12},{9,13},{1... | collective-permute-start | bytes 393224 | tf_op jit(solution)/shard_map/ppermute | solution.py:58
  86.9 12.3 %collective-permute-start.19 = (bf16[15,128,128]{2,1,0:T(8,128)(2,1)S(1)}, bf16[15,128,128]{2,1,0:T(8,128)(2,1)S(1)}, u32[]{:S(2)}, u32[]{:S(2)}) collective-permute-start(bf16[15,128,128]{2,1,0:T(8,128)(2,1)S(1)} %get-tuple-element.56.refs_1_), channel_id=1, source_target_pairs={{0,64},{32,96},{64,128},{96,160},{128,192},{160,224},{192,0},{224,... | collective-permute-start | bytes 1474568 | tf_op jit(solution)/shard_map/ppermute | solution.py:77
  87.9 13.3 %collective-permute-start.23 = (bf16[15,128,128]{2,1,0:T(8,128)(2,1)S(1)}, bf16[15,128,128]{2,1,0:T(8,128)(2,1)S(1)}, u32[]{:S(2)}, u32[]{:S(2)}) collective-permute-start(bf16[15,128,128]{2,1,0:T(8,128)(2,1)S(1)} %get-tuple-element.56.refs_1_), channel_id=1, source_target_pairs={{0,192},{32,224},{64,0},{96,32},{128,64},{160,96},{192,128},{224,1... | collective-permute-start | bytes 1474568 | tf_op jit(solution)/shard_map/ppermute | solution.py:77
  99.2 12.3 %collective-permute-start.21 = (bf16[15,128,128]{2,1,0:T(8,128)(2,1)S(1)}, bf16[15,128,128]{2,1,0:T(8,128)(2,1)S(1)}, u32[]{:S(2)}, u32[]{:S(2)}) collective-permute-start(bf16[15,128,128]{2,1,0:T(8,128)(2,1)S(1)} %get-tuple-element.56.refs_1_), channel_id=1, source_target_pairs={{0,128},{32,160},{64,192},{96,224},{128,0},{160,32},{192,64},{224,... | collective-permute-start | bytes 1474568 | tf_op jit(solution)/shard_map/ppermute | solution.py:77
  100.7 10.8 %collective-permute-start.18 = (bf16[15,128,128]{2,1,0:T(8,128)(2,1)S(1)}, bf16[15,128,128]{2,1,0:T(8,128)(2,1)S(1)}, u32[]{:S(2)}, u32[]{:S(2)}) collective-permute-start(bf16[15,128,128]{2,1,0:T(8,128)(2,1)S(1)} %get-tuple-element.56.refs_1_), channel_id=1, source_target_pairs={{0,32},{32,0},{64,96},{96,64},{128,160},{160,128},{192,224},{224,1... | collective-permute-start | bytes 1474568 | tf_op jit(solution)/shard_map/ppermute | solution.py:81
  100.7 10.8 %collective-permute-start.20 = (bf16[15,128,128]{2,1,0:T(8,128)(2,1)S(1)}, bf16[15,128,128]{2,1,0:T(8,128)(2,1)S(1)}, u32[]{:S(2)}, u32[]{:S(2)}) collective-permute-start(bf16[15,128,128]{2,1,0:T(8,128)(2,1)S(1)} %collective-permute-done.19.refs_3_), channel_id=1, source_target_pairs={{0,32},{32,0},{64,96},{96,64},{128,160},{160,128},{192,224},{224,1... | collective-permute-start | bytes 1474568 | tf_op jit(solution)/shard_map/ppermute | solution.py:81
  101.2 10.3 %collective-permute-start.24 = (bf16[15,128,128]{2,1,0:T(8,128)(2,1)S(1)}, bf16[15,128,128]{2,1,0:T(8,128)(2,1)S(1)}, u32[]{:S(2)}, u32[]{:S(2)}) collective-permute-start(bf16[15,128,128]{2,1,0:T(8,128)(2,1)S(1)} %collective-permute-done.23.refs_7_), channel_id=1, source_target_pairs={{0,32},{32,0},{64,96},{96,64},{128,160},{160,128},{192,224},{224,1... | collective-permute-start | bytes 1474568 | tf_op jit(solution)/shard_map/ppermute | solution.py:81
  115.1 16.9 %collective-permute-start.25 = (bf16[4,128,128]{2,1,0:T(8,128)(2,1)S(1)}, bf16[4,128,128]{2,1,0:T(8,128)(2,1)S(1)}, u32[]{:S(2)}, u32[]{:S(2)}) collective-permute-start(bf16[4,128,128]{2,1,0:T(8,128)(2,1)S(1)} %get-tuple-element.57), channel_id=1, source_target_pairs={{0,28},{1,29},{2,30},{3,31},{4,0},{5,1},{6,2},{7,3},{8,4},{9,5},{1... | collective-permute-start | bytes 393224 | tf_op jit(solution)/shard_map/ppermute | solution.py:58
  119.9 12.1 %collective-permute-start.26 = (bf16[4,128,128]{2,1,0:T(8,128)(2,1)S(1)}, bf16[4,128,128]{2,1,0:T(8,128)(2,1)S(1)}, u32[]{:S(2)}, u32[]{:S(2)}) collective-permute-start(bf16[4,128,128]{2,1,0:T(8,128)(2,1)S(1)} %get-tuple-element.58), channel_id=1, source_target_pairs={{0,4},{1,5},{2,6},{3,7},{4,8},{5,9},{6,10},{7,11},{8,12},{9,13},{1... | collective-permute-start | bytes 393224 | tf_op jit(solution)/shard_map/ppermute | solution.py:58
  119.9 12.1 %collective-permute-start.28 = (bf16[2,128,128]{2,1,0:T(8,128)(2,1)S(1)}, bf16[2,128,128]{2,1,0:T(8,128)(2,1)S(1)}, u32[]{:S(2)}, u32[]{:S(2)}) collective-permute-start(bf16[2,128,128]{2,1,0:T(8,128)(2,1)S(1)} %get-tuple-element.60), channel_id=1, source_target_pairs={{0,8},{1,9},{2,10},{3,11},{4,12},{5,13},{6,14},{7,15},{8,16},{9,17... | collective-permute-start | bytes 196616 | tf_op jit(solution)/shard_map/ppermute | solution.py:58
  124.0 8.0 %collective-permute-start.29 = (bf16[1,128,128]{2,1,0:T(8,128)(2,1)S(1)}, bf16[1,128,128]{2,1,0:T(8,128)(2,1)S(1)}, u32[]{:S(2)}, u32[]{:S(2)}) collective-permute-start(bf16[1,128,128]{2,1,0:T(8,128)(2,1)S(1)} %get-tuple-element.61), channel_id=1, source_target_pairs={{0,16},{1,17},{2,18},{3,19},{4,20},{5,21},{6,22},{7,23},{8,24},{9,... | collective-permute-start | bytes 98312 | tf_op jit(solution)/shard_map/ppermute | solution.py:58
  132.1 9.5 %collective-permute-start.31 = (bf16[4,128,128]{2,1,0:T(8,128)(2,1)S(1)}, bf16[4,128,128]{2,1,0:T(8,128)(2,1)S(1)}, u32[]{:S(2)}, u32[]{:S(2)}) collective-permute-start(bf16[4,128,128]{2,1,0:T(8,128)(2,1)S(1)} %get-tuple-element.69), channel_id=1, source_target_pairs={{0,1},{1,2},{2,3},{3,4},{4,5},{5,6},{6,7},{7,8},{8,9},{9,10},{10,1... | collective-permute-start | bytes 393224 | tf_op jit(solution)/shard_map/ppermute | solution.py:58
  (12 other events, 84.0 us)

commit v5 on v4

--- a/solution.py
+++ b/solution.py
@@ -8,8 +8,8 @@
 from jax.sharding import PartitionSpec as P
 
 SIGNS = {1: 1, 2: 1, 3: -1, 4: 1, 5: -1, 6: -1, 7: 1}
-ROUNDS = [[(1, 5), (-1, -5), (3, 7), (-3, -7)], [(2, 6), (-2, -6)]]
-STEP = 4
+FIRST = {1: [1, 5], -1: [-1, -5], 2: [2, 6], -2: [-2, -6], 4: [4, 7], -4: [-4, -7]}
+THEN = [({4: [5], -4: [-5]}, (1, -1)), ({3: [3, 7], -3: [-3, -7]}, (4, -4)), ({4: [6], -4: [-6]}, (2, -2))]
 LONG = {4: [4, 5, 3, 6], -4: [-4, -3, -5, -2], 8: [7], -8: [-7, -6]}
 SHORT = [1, -1, 2]
 
@@ -31,23 +31,13 @@
         self.edges = {self.far: []}
         for a in near:
             self.edges[a] = [b for b in near if b != a and (a - b) in self.place]
-        self.size = {a: 1 + len(self.edges[a]) for a in self.moved}
-        self.bundles, self.onward = {}, []
-        for number, pairs in enumerate(ROUNDS):
-            legs = {STEP: [], -STEP: []}
-            if number == 0:
-                legs = {STEP: [STEP], -STEP: [-STEP]}
-            for f, a in pairs:
-                self.bundles[f] = [f, a]
-                legs[a - f].append(a)
-            self.onward.append(legs)
+        self.size = {a: 1 + len(self.edges[a]) for a in near}
+        self.size[self.far] = 2
+        self.near_moved = near
         self.long = {e: [a for a in LONG[e] if a in self.slot] for e in LONG}
         relayed = [a for e in LONG for a in self.long[e]]
         self.short = {f: [f] + [a for e in LONG for a in self.long[e] if a - e == f] for f in SHORT}
-        self.alone = [a for a in self.moved if a not in relayed and a not in SHORT]
-
-    def back(self, a):
-        return self.slot[a if a == self.far else -a]
+        self.alone = [a for a in near if a not in relayed and a not in SHORT]
 
     def row_id(self, rank, col):
         return rank * self.grid_cols + lax.rem(col + 2 * self.grid_cols, self.grid_cols)
@@ -115,6 +105,10 @@
 def keep_kernel(plan, own, out):
     for p, d in enumerate(plan.kept):
         out[p] = own[plan.slot[-d]]
+    square = nt(own[0], own[0])
+    for s in range(1, plan.slot_count):
+        square = square + nt(own[s], own[s])
+    out[len(plan.kept)] = square.astype(out.dtype)
 
 
 def pick_kernel(plan, *refs):
@@ -130,13 +124,15 @@
             i = plan.row_id(my_row, my_col - a)
             rank = cols[i * n + plan.slot[a]] // plan.grid_cols
             out[at] = panel[rank, 0]
+            if a == plan.far:
+                out[at + 1] = panel[rank, len(plan.kept)]
             for p, b in enumerate(plan.edges[a]):
                 out[at + p + 1] = panel[rank, plan.place[a - b]]
             at += plan.size[a]
 
 
 def pick_groups(plan):
-    return list(plan.bundles.values()) + [[STEP], [-STEP], [plan.far]]
+    return [[plan.far]] + list(FIRST.values()) + [[3], [-3]]
 
 
 def total_size(plan, group):
@@ -147,9 +143,8 @@
     return total_size(plan, group[:group.index(a)])
 
 
-def onward_kernel(plan, number, held, *refs):
-    outs = refs[len(held):]
-    for out, group in zip(outs, plan.onward[number].values()):
+def join_kernel(plan, held, groups, *refs):
+    for out, group in zip(refs[len(held):], groups):
         at = 0
         for a in group:
             source = [a in h for h in held].index(True)
@@ -157,6 +152,15 @@
             for p in range(plan.size[a]):
                 out[at + p] = refs[source][first + p]
             at += plan.size[a]
+
+
+def join(plan, arrays, held, groups):
+    block, dtype = arrays[0].shape[1:], arrays[0].dtype
+    return call(
+        functools.partial(join_kernel, plan, held, groups), "join",
+        arrays, [VMEM] * len(arrays),
+        [((total_size(plan, g), *block), dtype) for g in groups],
+    )
 
 
 class Part:
@@ -203,13 +207,17 @@
     acc = nt(own[0], half[0])
     for s in range(1, n):
         acc = acc + nt(own[s], half[s])
-    self_new[...] = 3.0 * total[0] - 2.0 * acc
-    for a in plan.moved:
+    self_new[0] = 3.0 * total[0] - 2.0 * acc
+    t = plan.slot[plan.far]
+    cube = nn(own[0], half[t]) + nn(own[t], arrived[plan.far][1])
+    self_new[1] = 3.0 * total[t] - 2.0 * cube
+    for a in plan.near_moved:
         t = plan.slot[a]
         cube = nn(half[0], own[t]) + nn(half[t], arrived[a][0])
         total[t] = 3.0 * total[t] - 2.0 * cube
     add_edges(half, -2.0)
-    for t in range(1, n):
+    for a in plan.near_moved:
+        t = plan.slot[a]
         away[t - 1] = total[t].astype(away.dtype)
 
 
@@ -225,7 +233,7 @@
 
                 @pl.when(rank == piece_rank(plan, my_row, index))
                 def _():
-                    out[p] = piece[plan.back(a) - 1]
+                    out[p] = piece[plan.slot[-a] - 1]
 
 
 def home_groups(plan):
@@ -243,7 +251,8 @@
 
 def finish_kernel(where, self_new, *refs):
     out = refs[-1]
-    out[0, 0] = self_new[...]
+    out[0, 0] = self_new[0]
+    out[0, out.shape[1] - 1] = self_new[1]
     for t, (source, p) in where.items():
         out[0, t] = refs[source][p].astype(jnp.float32).T
 
@@ -271,51 +280,46 @@
     plan = Plan(slot_count, lax.axis_size("col"), lax.axis_size("row"))
     own, dtype, rows = density[0], density.dtype, plan.grid_rows
     table = cols.reshape(-1)
-    n_moved = len(plan.moved)
 
     def panel_scratch(blocks):
         return [pltpu.VMEM((rows, blocks, *block), dtype), pltpu.SemaphoreType.DMA((rows,))]
 
-    n_kept = len(plan.kept)
+    n_kept = len(plan.kept) + 1
     (kept,) = call(
         functools.partial(keep_kernel, plan), "keep", [own], [VMEM], [((n_kept, *block), dtype)]
     )
     groups = pick_groups(plan)
-    picked = call(
+    far, *first, three, minus_three = call(
         functools.partial(pick_kernel, plan), "pick",
         [table, *gather_rows(kept)], [SMEM] + [ANY] * rows,
         [((total_size(plan, g), *block), dtype) for g in groups],
         panel_scratch(n_kept),
     )
-    *bundles, up, down, far = picked
     far = shifted(far, -plan.far)
-    came, held, last = [], [], []
-    for number, pairs in enumerate(ROUNDS):
-        arrays, contents = [], []
-        for index, (f, a) in enumerate(pairs):
-            message = bundles[list(plan.bundles).index(f)]
-            if last:
-                message = after(message, last[index], far)
-            arrays.append(shifted(message, -f))
-            contents.append(plan.bundles[f])
-        last = arrays
-        came, held = came + arrays, held + contents
-        if number == 0:
-            arrays, contents = arrays + [up, down], contents + [[STEP], [-STEP]]
-        legs = plan.onward[number]
-        joined = call(
-            functools.partial(onward_kernel, plan, number, contents), "onward",
-            arrays, [VMEM] * len(arrays),
-            [((total_size(plan, g), *block), dtype) for g in legs.values()],
-        )
-        came += [shifted(m, -e) for m, e in zip(joined, legs)]
-        held += list(legs.values())
-    came.append(far)
-    held = [[f for f in g] for g in held] + [[plan.far]]
+    came = {}
+    for f, message in zip(FIRST, first):
+        if abs(f) == 4:
+            message = after(message, far)
+        came[f] = shifted(message, -f)
+    waiting = {4: (three, [3]), -4: (minus_three, [-3])}
+    second, held = [], list(FIRST.values())
+    for bundles, sources in THEN:
+        arrays, contents = [came[f] for f in sources], [FIRST[f] for f in sources]
+        if 4 in sources:
+            arrays[0] = after(arrays[0], came[2], came[-2])
+        for f in sources:
+            if f in waiting:
+                arrays.append(waiting[f][0])
+                contents.append(waiting[f][1])
+        joined = join(plan, arrays, contents, list(bundles.values()))
+        second += [shifted(m, -f) for f, m in zip(bundles, joined)]
+        held += list(bundles.values())
+    came = list(came.values()) + second + [far]
+    held.append([plan.far])
     away, self_new = call(
         functools.partial(product_kernel, plan, held), "product",
         [table, own, *came], [SMEM] + [VMEM] * (1 + len(came)),
-        [((n_moved, *block), dtype), (block, jnp.float32)],
+        [((len(plan.near_moved), *block), dtype), ((2, *block), jnp.float32)],
         [pltpu.VMEM((slot_count, *block), jnp.float32), pltpu.VMEM((slot_count, *block), dtype)],
     )
     groups = home_groups(plan)

time: 142 us -> 135 us (0.951); the launches traced: 143 us -> 134 us
  waiting for transfers between devices: 82.3 us -> 68.8 us
  starting transfers between devices: 48.1 us -> 53 us
    ppermute x19 -> x20, waiting for transfers between devices: 49 us -> 33.9 us  [shifted(): lax.ppermute(value, 'col', [(i, (i + by) % length) for i in range(length)])]
    ppermute x19 -> x20, starting transfers between devices: 37.2 us -> 43.5 us  [shifted(): lax.ppermute(value, 'col', [(i, (i + by) % length) for i in range(length)])]
    ppermute x6, waiting for transfers between devices: 30.2 us -> 31.8 us  [from_chip(): return lax.ppermute(block, 'row', pairs)]
    pallas_call x8 -> x9, Pallas kernels: 11.3 us -> 11.2 us  [call(): pl.pallas_call(kernel, out_shape=[jax.ShapeDtypeStruct(shape, dtype) for...]
  transfers between devices with their start and end apart: 33 -> 34, of which waited for: 15 -> 18; matrix products, arithmetic and copies ran while one was open for 0% -> 0% of each run, Pallas kernels for 0% -> 0%
where the time goes in v5:
time: 135 us; the launch traced here: 134 us
  waiting for transfers between devices  68.8 us (51%)
  starting transfers between devices  53 us (39%)
  Pallas kernels  11.2 us (8%)
    ppermute x20, starting transfers between devices, shifted(): lax.ppermute(value, 'col', [(i, (i + by) % length) for i in range(length)])  43.5 us
    ppermute x20, waiting for transfers between devices, shifted(): lax.ppermute(value, 'col', [(i, (i + by) % length) for i in range(length)])  33.9 us
    ppermute x6, waiting for transfers between devices, from_chip(): return lax.ppermute(block, 'row', pairs)  31.8 us
    pallas_call x9, Pallas kernels, call(): pl.pallas_call(kernel, out_shape=[jax.ShapeDtypeStruct(shape, dtype) for...  11.2 us
    ppermute x6, starting transfers between devices, from_chip(): return lax.ppermute(block, 'row', pairs)  8.48 us
    ppermute x8, waiting for transfers between devices, from_core(): lax.ppermute(block, 'row', [(i, i ^ 1) for i in range(lax.axis_size('row'...  3.15 us
  transfers between devices with their start and end apart: 34, of which 18 were waited for; matrix products, arithmetic and copies ran while one was open for 0% of the time, Pallas kernels for 0%

profile of v5, /device:TPU:2, one launch (start us, length us, event | category | flops | bytes accessed | tf_op | source)
XLA Modules:
  0.0 134.4 jit_solution(11363142848774473256)
XLA Ops:
  4.0 6.4 %collective-permute-done.1.refs_3_ = bf16[9,128,128]{2,1,0:T(8,128)(2,1)S(1)} collective-permute-done((bf16[9,128,128]{2,1,0:T(8,128)(2,1)S(1)}, bf16[9,128,128]{2,1,0:T(8,128)(2,1)S(1)}, u32[]{:S(2)}, u32[]{:S(2)}) %collective-permute-start.1) | collective-permute-done | bytes 294944 | tf_op jit(solution)/shard_map/ppermute | solution.py:67
  10.3 2.1 %collective-permute-start.3 = (bf16[9,128,128]{2,1,0:T(8,128)(2,1)S(1)}, bf16[9,128,128]{2,1,0:T(8,128)(2,1)S(1)}, u32[]{:S(2)}, u32[]{:S(2)}) collective-permute-start(bf16[9,128,128]{2,1,0:T(8,128)(2,1)S(1)} %keep.1.refs_1_), channel_id=1, source_target_pairs={{0,128},{32,160},{64,192},{96,224},{128,0},{160,32},{192,64},{224,... | collective-permute-start | bytes 884744 | tf_op jit(solution)/shard_map/ppermute | solution.py:67
  13.0 6.5 %collective-permute-done.3.refs_5_ = bf16[9,128,128]{2,1,0:T(8,128)(2,1)S(1)} collective-permute-done((bf16[9,128,128]{2,1,0:T(8,128)(2,1)S(1)}, bf16[9,128,128]{2,1,0:T(8,128)(2,1)S(1)}, u32[]{:S(2)}, u32[]{:S(2)}) %collective-permute-start.3) | collective-permute-done | bytes 294944 | tf_op jit(solution)/shard_map/ppermute | solution.py:67
  22.7 8.8 %collective-permute-start.9 = (bf16[11,128,128]{2,1,0:T(8,128)(2,1)S(1)}, bf16[11,128,128]{2,1,0:T(8,128)(2,1)S(1)}, u32[]{:S(2)}, u32[]{:S(2)}) collective-permute-start(bf16[11,128,128]{2,1,0:T(8,128)(2,1)S(1)} %get-tuple-element.42), channel_id=1, source_target_pairs={{0,30},{1,31},{2,0},{3,1},{4,2},{5,3},{6,4},{7,5},{8,6},{9,7},{10,... | collective-permute-start | bytes 1081352 | tf_op jit(solution)/shard_map/ppermute | solution.py:48
  33.7 6.7 %collective-permute-done.11.refs_14_ = bf16[2,128,128]{2,1,0:T(8,128)(2,1)S(1)} collective-permute-done((bf16[2,128,128]{2,1,0:T(8,128)(2,1)S(1)}, bf16[2,128,128]{2,1,0:T(8,128)(2,1)S(1)}, u32[]{:S(2)}, u32[]{:S(2)}) %collective-permute-start.11) | collective-permute-done | bytes 65568 | tf_op jit(solution)/shard_map/ppermute | solution.py:48
  40.4 4.3 %collective-permute-start.13 = (bf16[10,128,128]{2,1,0:T(8,128)(2,1)S(1)}, bf16[10,128,128]{2,1,0:T(8,128)(2,1)S(1)}, u32[]{:S(2)}, u32[]{:S(2)}) collective-permute-start(bf16[10,128,128]{2,1,0:T(8,128)(2,1)S(1)} %get-tuple-element.48), channel_id=1, source_target_pairs={{0,4},{1,5},{2,6},{3,7},{4,8},{5,9},{6,10},{7,11},{8,12},{9,13},{1... | collective-permute-start | bytes 983048 | tf_op jit(solution)/shard_map/ppermute | solution.py:48
  44.7 2.0 %collective-permute-start.8 = (bf16[12,128,128]{2,1,0:T(8,128)(2,1)S(1)}, bf16[12,128,128]{2,1,0:T(8,128)(2,1)S(1)}, u32[]{:S(2)}, u32[]{:S(2)}) collective-permute-start(bf16[12,128,128]{2,1,0:T(8,128)(2,1)S(1)} %get-tuple-element.41), channel_id=1, source_target_pairs={{0,1},{1,2},{2,3},{3,4},{4,5},{5,6},{6,7},{7,8},{8,9},{9,10},{10,1... | collective-permute-start | bytes 1179656 | tf_op jit(solution)/shard_map/ppermute | solution.py:48
  47.9 6.8 %collective-permute-done.12.refs_0_.refs_6_ = bf16[9,128,128]{2,1,0:T(8,128)(2,1)S(1)} collective-permute-done((bf16[9,128,128]{2,1,0:T(8,128)(2,1)S(1)}, bf16[9,128,128]{2,1,0:T(8,128)(2,1)S(1)}, u32[]{:S(2)}, u32[]{:S(2)}) %collective-permute-start.12) | collective-permute-done | bytes 294944 | tf_op jit(solution)/shard_map/ppermute | solution.py:48
  54.8 3.2 %collective-permute-start.17 = (bf16[10,128,128]{2,1,0:T(8,128)(2,1)S(1)}, bf16[10,128,128]{2,1,0:T(8,128)(2,1)S(1)}, u32[]{:S(2)}, u32[]{:S(2)}) collective-permute-start(bf16[10,128,128]{2,1,0:T(8,128)(2,1)S(1)} %get-tuple-element.55), channel_id=1, source_target_pairs={{0,3},{1,4},{2,5},{3,6},{4,7},{5,8},{6,9},{7,10},{8,11},{9,12},{10... | collective-permute-start | bytes 983048 | tf_op jit(solution)/shard_map/ppermute | solution.py:48
  58.1 1.8 %collective-permute-start.19 = (bf16[4,128,128]{2,1,0:T(8,128)(2,1)S(1)}, bf16[4,128,128]{2,1,0:T(8,128)(2,1)S(1)}, u32[]{:S(2)}, u32[]{:S(2)}) collective-permute-start(bf16[4,128,128]{2,1,0:T(8,128)(2,1)S(1)} %get-tuple-element.57), channel_id=1, source_target_pairs={{0,4},{1,5},{2,6},{3,7},{4,8},{5,9},{6,10},{7,11},{8,12},{9,13},{1... | collective-permute-start | bytes 393224 | tf_op jit(solution)/shard_map/ppermute | solution.py:48
  60.7 5.8 %collective-permute-start.18 = (bf16[5,128,128]{2,1,0:T(8,128)(2,1)S(1)}, bf16[5,128,128]{2,1,0:T(8,128)(2,1)S(1)}, u32[]{:S(2)}, u32[]{:S(2)}) collective-permute-start(bf16[5,128,128]{2,1,0:T(8,128)(2,1)S(1)} %get-tuple-element.56), channel_id=1, source_target_pairs={{0,28},{1,29},{2,30},{3,31},{4,0},{5,1},{6,2},{7,3},{8,4},{9,5},{1... | collective-permute-start | bytes 491528 | tf_op jit(solution)/shard_map/ppermute | solution.py:48
  66.6 2.0 %collective-permute-start.15 = (bf16[5,128,128]{2,1,0:T(8,128)(2,1)S(1)}, bf16[5,128,128]{2,1,0:T(8,128)(2,1)S(1)}, u32[]{:S(2)}, u32[]{:S(2)}) collective-permute-start(bf16[5,128,128]{2,1,0:T(8,128)(2,1)S(1)} %get-tuple-element.50), channel_id=1, source_target_pairs={{0,4},{1,5},{2,6},{3,7},{4,8},{5,9},{6,10},{7,11},{8,12},{9,13},{1... | collective-permute-start | bytes 491528 | tf_op jit(solution)/shard_map/ppermute | solution.py:48
  68.6 4.6 %collective-permute-done.18.refs_12_ = bf16[5,128,128]{2,1,0:T(8,128)(2,1)S(1)} collective-permute-done((bf16[5,128,128]{2,1,0:T(8,128)(2,1)S(1)}, bf16[5,128,128]{2,1,0:T(8,128)(2,1)S(1)}, u32[]{:S(2)}, u32[]{:S(2)}) %collective-permute-start.18) | collective-permute-done | bytes 163872 | tf_op jit(solution)/shard_map/ppermute | solution.py:48
  74.9 6.1 %product.1 = (bf16[14,128,128]{2,1,0:T(8,128)(2,1)S(1)}, f32[2,128,128]{2,1,0:T(8,128)S(1)}) custom-call(s32[4096]{0:T(1024)S(1)} %reshape.3.refs_0_, bf16[16,128,128]{2,1,0:T(8,128)(2,1)S(1)} %bitcast.2, bf16[12,128,128]{2,1,0:T(8,128)(2,1)S(1)} %collective-permute-done.7.refs_0_.refs_2_, bf16[12,128,128]{2,1,0:T(8,128)(2,1)S(1)} %collective-permute-done.8.refs_1_.refs_3_, ...), custom_call_target="tpu_custom_call" | custom-call | tf_op jit(solution)/shard_map/product/pallas_call | solution.py:267
  81.1 2.4 %collective-permute-start.21 = (bf16[14,128,128]{2,1,0:T(8,128)(2,1)S(1)}, bf16[14,128,128]{2,1,0:T(8,128)(2,1)S(1)}, u32[]{:S(2)}, u32[]{:S(2)}) collective-permute-start(bf16[14,128,128]{2,1,0:T(8,128)(2,1)S(1)} %get-tuple-element.60.refs_1_), channel_id=1, source_target_pairs={{0,64},{32,96},{64,128},{96,160},{128,192},{160,224},{192,0},{224,... | collective-permute-start | bytes 1376264 | tf_op jit(solution)/shard_map/ppermute | solution.py:67
  83.5 9.1 %collective-permute-done.21.refs_3_ = bf16[14,128,128]{2,1,0:T(8,128)(2,1)S(1)} collective-permute-done((bf16[14,128,128]{2,1,0:T(8,128)(2,1)S(1)}, bf16[14,128,128]{2,1,0:T(8,128)(2,1)S(1)}, u32[]{:S(2)}, u32[]{:S(2)}) %collective-permute-start.21) | collective-permute-done | bytes 458784 | tf_op jit(solution)/shard_map/ppermute | solution.py:67
  94.6 9.8 %collective-permute-done.23.refs_5_ = bf16[14,128,128]{2,1,0:T(8,128)(2,1)S(1)} collective-permute-done((bf16[14,128,128]{2,1,0:T(8,128)(2,1)S(1)}, bf16[14,128,128]{2,1,0:T(8,128)(2,1)S(1)}, u32[]{:S(2)}, u32[]{:S(2)}) %collective-permute-start.23) | collective-permute-done | bytes 458784 | tf_op jit(solution)/shard_map/ppermute | solution.py:67
  104.5 1.8 %collective-permute-done.24.refs_6_ = bf16[14,128,128]{2,1,0:T(8,128)(2,1)S(1)} collective-permute-done((bf16[14,128,128]{2,1,0:T(8,128)(2,1)S(1)}, bf16[14,128,128]{2,1,0:T(8,128)(2,1)S(1)}, u32[]{:S(2)}, u32[]{:S(2)}) %collective-permute-start.24) | collective-permute-done | bytes 458784 | tf_op jit(solution)/shard_map/ppermute | solution.py:71
  107.9 6.8 %collective-permute-start.27 = (bf16[4,128,128]{2,1,0:T(8,128)(2,1)S(1)}, bf16[4,128,128]{2,1,0:T(8,128)(2,1)S(1)}, u32[]{:S(2)}, u32[]{:S(2)}) collective-permute-start(bf16[4,128,128]{2,1,0:T(8,128)(2,1)S(1)} %get-tuple-element.61), channel_id=1, source_target_pairs={{0,28},{1,29},{2,30},{3,31},{4,0},{5,1},{6,2},{7,3},{8,4},{9,5},{1... | collective-permute-start | bytes 393224 | tf_op jit(solution)/shard_map/ppermute | solution.py:48
  115.3 3.6 %collective-permute-start.29 = (bf16[1,128,128]{2,1,0:T(8,128)(2,1)S(1)}, bf16[1,128,128]{2,1,0:T(8,128)(2,1)S(1)}, u32[]{:S(2)}, u32[]{:S(2)}) collective-permute-start(bf16[1,128,128]{2,1,0:T(8,128)(2,1)S(1)} %get-tuple-element.63), channel_id=1, source_target_pairs={{0,24},{1,25},{2,26},{3,27},{4,28},{5,29},{6,30},{7,31},{8,0},{9,1... | collective-permute-start | bytes 98312 | tf_op jit(solution)/shard_map/ppermute | solution.py:48
  118.9 1.8 %collective-permute-done.29.refs_2_ = bf16[1,128,128]{2,1,0:T(8,128)(2,1)S(1)} collective-permute-done((bf16[1,128,128]{2,1,0:T(8,128)(2,1)S(1)}, bf16[1,128,128]{2,1,0:T(8,128)(2,1)S(1)}, u32[]{:S(2)}, u32[]{:S(2)}) %collective-permute-start.29) | collective-permute-done | bytes 32800 | tf_op jit(solution)/shard_map/ppermute | solution.py:48
  123.5 2.0 %collective-permute-start.32 = (bf16[4,128,128]{2,1,0:T(8,128)(2,1)S(1)}, bf16[4,128,128]{2,1,0:T(8,128)(2,1)S(1)}, u32[]{:S(2)}, u32[]{:S(2)}) collective-permute-start(bf16[4,128,128]{2,1,0:T(8,128)(2,1)S(1)} %get-tuple-element.71), channel_id=1, source_target_pairs={{0,1},{1,2},{2,3},{3,4},{4,5},{5,6},{6,7},{7,8},{8,9},{9,10},{10,1... | collective-permute-start | bytes 393224 | tf_op jit(solution)/shard_map/ppermute | solution.py:48
  125.5 2.9 %collective-permute-done.31.refs_4_ = bf16[4,128,128]{2,1,0:T(8,128)(2,1)S(1)} collective-permute-done((bf16[4,128,128]{2,1,0:T(8,128)(2,1)S(1)}, bf16[4,128,128]{2,1,0:T(8,128)(2,1)S(1)}, u32[]{:S(2)}, u32[]{:S(2)}) %collective-permute-start.31) | collective-permute-done | bytes 131104 | tf_op jit(solution)/shard_map/ppermute | solution.py:48
  128.4 4.6 %collective-permute-done.32.refs_5_ = bf16[4,128,128]{2,1,0:T(8,128)(2,1)S(1)} collective-permute-done((bf16[4,128,128]{2,1,0:T(8,128)(2,1)S(1)}, bf16[4,128,128]{2,1,0:T(8,128)(2,1)S(1)}, u32[]{:S(2)}, u32[]{:S(2)}) %collective-permute-start.32) | collective-permute-done | bytes 131104 | tf_op jit(solution)/shard_map/ppermute | solution.py:48
  (61 shorter events, 22.2 us)
Async XLA Ops:
  1.5 8.8 %collective-permute-start.1 = (bf16[9,128,128]{2,1,0:T(8,128)(2,1)S(1)}, bf16[9,128,128]{2,1,0:T(8,128)(2,1)S(1)}, u32[]{:S(2)}, u32[]{:S(2)}) collective-permute-start(bf16[9,128,128]{2,1,0:T(8,128)(2,1)S(1)} %keep.1.refs_1_), channel_id=1, source_target_pairs={{0,64},{32,96},{64,128},{96,160},{128,192},{160,224},{192,0},{224,... | collective-permute-start | bytes 884744 | tf_op jit(solution)/shard_map/ppermute | solution.py:67
  3.1 9.9 %collective-permute-start.5 = (bf16[9,128,128]{2,1,0:T(8,128)(2,1)S(1)}, bf16[9,128,128]{2,1,0:T(8,128)(2,1)S(1)}, u32[]{:S(2)}, u32[]{:S(2)}) collective-permute-start(bf16[9,128,128]{2,1,0:T(8,128)(2,1)S(1)} %keep.1.refs_1_), channel_id=1, source_target_pairs={{0,192},{32,224},{64,0},{96,32},{128,64},{160,96},{192,128},{224,1... | collective-permute-start | bytes 884744 | tf_op jit(solution)/shard_map/ppermute | solution.py:67
  10.3 9.1 %collective-permute-start.3 = (bf16[9,128,128]{2,1,0:T(8,128)(2,1)S(1)}, bf16[9,128,128]{2,1,0:T(8,128)(2,1)S(1)}, u32[]{:S(2)}, u32[]{:S(2)}) collective-permute-start(bf16[9,128,128]{2,1,0:T(8,128)(2,1)S(1)} %keep.1.refs_1_), channel_id=1, source_target_pairs={{0,128},{32,160},{64,192},{96,224},{128,0},{160,32},{192,64},{224,... | collective-permute-start | bytes 884744 | tf_op jit(solution)/shard_map/ppermute | solution.py:67
  22.7 22.1 %collective-permute-start.9 = (bf16[11,128,128]{2,1,0:T(8,128)(2,1)S(1)}, bf16[11,128,128]{2,1,0:T(8,128)(2,1)S(1)}, u32[]{:S(2)}, u32[]{:S(2)}) collective-permute-start(bf16[11,128,128]{2,1,0:T(8,128)(2,1)S(1)} %get-tuple-element.42), channel_id=1, source_target_pairs={{0,30},{1,31},{2,0},{3,1},{4,2},{5,3},{6,4},{7,5},{8,6},{9,7},{10,... | collective-permute-start | bytes 1081352 | tf_op jit(solution)/shard_map/ppermute | solution.py:48
  31.5 8.9 %collective-permute-start.11 = (bf16[2,128,128]{2,1,0:T(8,128)(2,1)S(1)}, bf16[2,128,128]{2,1,0:T(8,128)(2,1)S(1)}, u32[]{:S(2)}, u32[]{:S(2)}) collective-permute-start(bf16[2,128,128]{2,1,0:T(8,128)(2,1)S(1)} %get-tuple-element.45), channel_id=1, source_target_pairs={{0,16},{1,17},{2,18},{3,19},{4,20},{5,21},{6,22},{7,23},{8,24},{9,... | collective-permute-start | bytes 196616 | tf_op jit(solution)/shard_map/ppermute | solution.py:48
  32.9 15.0 %collective-permute-start.10 = (bf16[11,128,128]{2,1,0:T(8,128)(2,1)S(1)}, bf16[11,128,128]{2,1,0:T(8,128)(2,1)S(1)}, u32[]{:S(2)}, u32[]{:S(2)}) collective-permute-start(bf16[11,128,128]{2,1,0:T(8,128)(2,1)S(1)} %get-tuple-element.43), channel_id=1, source_target_pairs={{0,2},{1,3},{2,4},{3,5},{4,6},{5,7},{6,8},{7,9},{8,10},{9,11},{10,... | collective-permute-start | bytes 1081352 | tf_op jit(solution)/shard_map/ppermute | solution.py:48
  40.4 14.3 %collective-permute-start.13 = (bf16[10,128,128]{2,1,0:T(8,128)(2,1)S(1)}, bf16[10,128,128]{2,1,0:T(8,128)(2,1)S(1)}, u32[]{:S(2)}, u32[]{:S(2)}) collective-permute-start(bf16[10,128,128]{2,1,0:T(8,128)(2,1)S(1)} %get-tuple-element.48), channel_id=1, source_target_pairs={{0,4},{1,5},{2,6},{3,7},{4,8},{5,9},{6,10},{7,11},{8,12},{9,13},{1... | collective-permute-start | bytes 983048 | tf_op jit(solution)/shard_map/ppermute | solution.py:48
  44.7 9.9 %collective-permute-start.12 = (bf16[9,128,128]{2,1,0:T(8,128)(2,1)S(1)}, bf16[9,128,128]{2,1,0:T(8,128)(2,1)S(1)}, u32[]{:S(2)}, u32[]{:S(2)}) collective-permute-start(bf16[9,128,128]{2,1,0:T(8,128)(2,1)S(1)} %get-tuple-element.46), channel_id=1, source_target_pairs={{0,28},{1,29},{2,30},{3,31},{4,0},{5,1},{6,2},{7,3},{8,4},{9,5},{1... | collective-permute-start | bytes 884744 | tf_op jit(solution)/shard_map/ppermute | solution.py:48
  44.7 15.9 %collective-permute-start.7 = (bf16[12,128,128]{2,1,0:T(8,128)(2,1)S(1)}, bf16[12,128,128]{2,1,0:T(8,128)(2,1)S(1)}, u32[]{:S(2)}, u32[]{:S(2)}) collective-permute-start(bf16[12,128,128]{2,1,0:T(8,128)(2,1)S(1)} %get-tuple-element.40), channel_id=1, source_target_pairs={{0,31},{1,0},{2,1},{3,2},{4,3},{5,4},{6,5},{7,6},{8,7},{9,8},{10,9... | collective-permute-start | bytes 1179656 | tf_op jit(solution)/shard_map/ppermute | solution.py:48
  44.7 21.7 %collective-permute-start.8 = (bf16[12,128,128]{2,1,0:T(8,128)(2,1)S(1)}, bf16[12,128,128]{2,1,0:T(8,128)(2,1)S(1)}, u32[]{:S(2)}, u32[]{:S(2)}) collective-permute-start(bf16[12,128,128]{2,1,0:T(8,128)(2,1)S(1)} %get-tuple-element.41), channel_id=1, source_target_pairs={{0,1},{1,2},{2,3},{3,4},{4,5},{5,6},{6,7},{7,8},{8,9},{9,10},{10,1... | collective-permute-start | bytes 1179656 | tf_op jit(solution)/shard_map/ppermute | solution.py:48
  54.7 20.2 %collective-permute-start.16 = (bf16[10,128,128]{2,1,0:T(8,128)(2,1)S(1)}, bf16[10,128,128]{2,1,0:T(8,128)(2,1)S(1)}, u32[]{:S(2)}, u32[]{:S(2)}) collective-permute-start(bf16[10,128,128]{2,1,0:T(8,128)(2,1)S(1)} %get-tuple-element.54), channel_id=1, source_target_pairs={{0,29},{1,30},{2,31},{3,0},{4,1},{5,2},{6,3},{7,4},{8,5},{9,6},{10... | collective-permute-start | bytes 983048 | tf_op jit(solution)/shard_map/ppermute | solution.py:48
  54.8 20.1 %collective-permute-start.17 = (bf16[10,128,128]{2,1,0:T(8,128)(2,1)S(1)}, bf16[10,128,128]{2,1,0:T(8,128)(2,1)S(1)}, u32[]{:S(2)}, u32[]{:S(2)}) collective-permute-start(bf16[10,128,128]{2,1,0:T(8,128)(2,1)S(1)} %get-tuple-element.55), channel_id=1, source_target_pairs={{0,3},{1,4},{2,5},{3,6},{4,7},{5,8},{6,9},{7,10},{8,11},{9,12},{10... | collective-permute-start | bytes 983048 | tf_op jit(solution)/shard_map/ppermute | solution.py:48
  58.1 8.5 %collective-permute-start.19 = (bf16[4,128,128]{2,1,0:T(8,128)(2,1)S(1)}, bf16[4,128,128]{2,1,0:T(8,128)(2,1)S(1)}, u32[]{:S(2)}, u32[]{:S(2)}) collective-permute-start(bf16[4,128,128]{2,1,0:T(8,128)(2,1)S(1)} %get-tuple-element.57), channel_id=1, source_target_pairs={{0,4},{1,5},{2,6},{3,7},{4,8},{5,9},{6,10},{7,11},{8,12},{9,13},{1... | collective-permute-start | bytes 393224 | tf_op jit(solution)/shard_map/ppermute | solution.py:48
  60.7 12.5 %collective-permute-start.18 = (bf16[5,128,128]{2,1,0:T(8,128)(2,1)S(1)}, bf16[5,128,128]{2,1,0:T(8,128)(2,1)S(1)}, u32[]{:S(2)}, u32[]{:S(2)}) collective-permute-start(bf16[5,128,128]{2,1,0:T(8,128)(2,1)S(1)} %get-tuple-element.56), channel_id=1, source_target_pairs={{0,28},{1,29},{2,30},{3,31},{4,0},{5,1},{6,2},{7,3},{8,4},{9,5},{1... | collective-permute-start | bytes 491528 | tf_op jit(solution)/shard_map/ppermute | solution.py:48
  66.5 8.4 %collective-permute-start.14 = (bf16[5,128,128]{2,1,0:T(8,128)(2,1)S(1)}, bf16[5,128,128]{2,1,0:T(8,128)(2,1)S(1)}, u32[]{:S(2)}, u32[]{:S(2)}) collective-permute-start(bf16[5,128,128]{2,1,0:T(8,128)(2,1)S(1)} %get-tuple-element.49), channel_id=1, source_target_pairs={{0,28},{1,29},{2,30},{3,31},{4,0},{5,1},{6,2},{7,3},{8,4},{9,5},{1... | collective-permute-start | bytes 491528 | tf_op jit(solution)/shard_map/ppermute | solution.py:48
  81.1 11.5 %collective-permute-start.21 = (bf16[14,128,128]{2,1,0:T(8,128)(2,1)S(1)}, bf16[14,128,128]{2,1,0:T(8,128)(2,1)S(1)}, u32[]{:S(2)}, u32[]{:S(2)}) collective-permute-start(bf16[14,128,128]{2,1,0:T(8,128)(2,1)S(1)} %get-tuple-element.60.refs_1_), channel_id=1, source_target_pairs={{0,64},{32,96},{64,128},{96,160},{128,192},{160,224},{192,0},{224,... | collective-permute-start | bytes 1376264 | tf_op jit(solution)/shard_map/ppermute | solution.py:67
  83.5 11.2 %collective-permute-start.25 = (bf16[14,128,128]{2,1,0:T(8,128)(2,1)S(1)}, bf16[14,128,128]{2,1,0:T(8,128)(2,1)S(1)}, u32[]{:S(2)}, u32[]{:S(2)}) collective-permute-start(bf16[14,128,128]{2,1,0:T(8,128)(2,1)S(1)} %get-tuple-element.60.refs_1_), channel_id=1, source_target_pairs={{0,192},{32,224},{64,0},{96,32},{128,64},{160,96},{192,128},{224,1... | collective-permute-start | bytes 1376264 | tf_op jit(solution)/shard_map/ppermute | solution.py:67
  92.6 11.8 %collective-permute-start.23 = (bf16[14,128,128]{2,1,0:T(8,128)(2,1)S(1)}, bf16[14,128,128]{2,1,0:T(8,128)(2,1)S(1)}, u32[]{:S(2)}, u32[]{:S(2)}) collective-permute-start(bf16[14,128,128]{2,1,0:T(8,128)(2,1)S(1)} %get-tuple-element.60.refs_1_), channel_id=1, source_target_pairs={{0,128},{32,160},{64,192},{96,224},{128,0},{160,32},{192,64},{224,... | collective-permute-start | bytes 1376264 | tf_op jit(solution)/shard_map/ppermute | solution.py:67
  94.1 10.3 %collective-permute-start.20 = (bf16[14,128,128]{2,1,0:T(8,128)(2,1)S(1)}, bf16[14,128,128]{2,1,0:T(8,128)(2,1)S(1)}, u32[]{:S(2)}, u32[]{:S(2)}) collective-permute-start(bf16[14,128,128]{2,1,0:T(8,128)(2,1)S(1)} %get-tuple-element.60.refs_1_), channel_id=1, source_target_pairs={{0,32},{32,0},{64,96},{96,64},{128,160},{160,128},{192,224},{224,1... | collective-permute-start | bytes 1376264 | tf_op jit(solution)/shard_map/ppermute | solution.py:71
  94.1 10.3 %collective-permute-start.22 = (bf16[14,128,128]{2,1,0:T(8,128)(2,1)S(1)}, bf16[14,128,128]{2,1,0:T(8,128)(2,1)S(1)}, u32[]{:S(2)}, u32[]{:S(2)}) collective-permute-start(bf16[14,128,128]{2,1,0:T(8,128)(2,1)S(1)} %collective-permute-done.21.refs_3_), channel_id=1, source_target_pairs={{0,32},{32,0},{64,96},{96,64},{128,160},{160,128},{192,224},{224,1... | collective-permute-start | bytes 1376264 | tf_op jit(solution)/shard_map/ppermute | solution.py:71
  94.6 9.8 %collective-permute-start.26 = (bf16[14,128,128]{2,1,0:T(8,128)(2,1)S(1)}, bf16[14,128,128]{2,1,0:T(8,128)(2,1)S(1)}, u32[]{:S(2)}, u32[]{:S(2)}) collective-permute-start(bf16[14,128,128]{2,1,0:T(8,128)(2,1)S(1)} %collective-permute-done.25.refs_7_), channel_id=1, source_target_pairs={{0,32},{32,0},{64,96},{96,64},{128,160},{160,128},{192,224},{224,1... | collective-permute-start | bytes 1376264 | tf_op jit(solution)/shard_map/ppermute | solution.py:71
  107.9 14.0 %collective-permute-start.27 = (bf16[4,128,128]{2,1,0:T(8,128)(2,1)S(1)}, bf16[4,128,128]{2,1,0:T(8,128)(2,1)S(1)}, u32[]{:S(2)}, u32[]{:S(2)}) collective-permute-start(bf16[4,128,128]{2,1,0:T(8,128)(2,1)S(1)} %get-tuple-element.61), channel_id=1, source_target_pairs={{0,28},{1,29},{2,30},{3,31},{4,0},{5,1},{6,2},{7,3},{8,4},{9,5},{1... | collective-permute-start | bytes 393224 | tf_op jit(solution)/shard_map/ppermute | solution.py:48
  114.8 8.6 %collective-permute-start.28 = (bf16[4,128,128]{2,1,0:T(8,128)(2,1)S(1)}, bf16[4,128,128]{2,1,0:T(8,128)(2,1)S(1)}, u32[]{:S(2)}, u32[]{:S(2)}) collective-permute-start(bf16[4,128,128]{2,1,0:T(8,128)(2,1)S(1)} %get-tuple-element.62), channel_id=1, source_target_pairs={{0,4},{1,5},{2,6},{3,7},{4,8},{5,9},{6,10},{7,11},{8,12},{9,13},{1... | collective-permute-start | bytes 393224 | tf_op jit(solution)/shard_map/ppermute | solution.py:48
  123.5 9.5 %collective-permute-start.32 = (bf16[4,128,128]{2,1,0:T(8,128)(2,1)S(1)}, bf16[4,128,128]{2,1,0:T(8,128)(2,1)S(1)}, u32[]{:S(2)}, u32[]{:S(2)}) collective-permute-start(bf16[4,128,128]{2,1,0:T(8,128)(2,1)S(1)} %get-tuple-element.71), channel_id=1, source_target_pairs={{0,1},{1,2},{2,3},{3,4},{4,5},{5,6},{6,7},{7,8},{8,9},{9,10},{10,1... | collective-permute-start | bytes 393224 | tf_op jit(solution)/shard_map/ppermute | solution.py:48
  (13 other events, 94.4 us)

commit v6 on v5

--- a/solution.py
+++ b/solution.py
@@ -72,6 +72,15 @@
 
 
 def gather_rows(block):
+    half = block.shape[0] // 2
+    ahead, behind = from_chip(block, 1), from_chip(block, -1)
+    out = []
+    for piece in (block, ahead, from_chip(ahead[:half], 1), from_chip(behind[half:], -1), behind):
+        out += [piece, from_core(piece)]
+    return out
+
+
+def gather_small(block):
     chips = lax.axis_size("row") // 2
     same = [block] + [None] * (chips - 1)
     same[1], same[chips - 1] = from_chip(block, 1), from_chip(block, chips - 1)
@@ -109,6 +118,15 @@
     for s in range(1, plan.slot_count):
         square = square + nt(own[s], own[s])
     out[len(plan.kept)] = square.astype(out.dtype)
+
+
+class Joined:
+    def __init__(self, refs):
+        self.first, self.second = refs
+
+    def __getitem__(self, p):
+        n = self.first.shape[0]
+        return self.first[p] if p < n else self.second[p - n]
 
 
 def pick_kernel(plan, *refs):
@@ -222,7 +240,8 @@
 
 
 def home_kernel(plan, *refs):
-    cols, pieces, outs = refs[0], refs[1:1 + plan.grid_rows], refs[1 + plan.grid_rows:]
+    cols, (*pieces, p0, q0, p1, q1, r0, r1), outs = refs[0], refs[1:11], refs[11:]
+    pieces += [Joined((p0, p1)), Joined((q0, q1)), r0, r1]
     n = plan.slot_count
     my_row, my_col = lax.axis_index("row"), lax.axis_index("col")
     for out, group in zip(outs, home_groups(plan)):
@@ -291,7 +310,7 @@
     groups = pick_groups(plan)
     far, *first, three, minus_three = call(
         functools.partial(pick_kernel, plan), "pick",
-        [table, *gather_rows(kept)], [SMEM] + [ANY] * rows,
+        [table, *gather_small(kept)], [SMEM] + [ANY] * rows,
         [((total_size(plan, g), *block), dtype) for g in groups],
         panel_scratch(n_kept),
     )
@@ -325,7 +344,7 @@
     groups = home_groups(plan)
     homing = call(
         functools.partial(home_kernel, plan), "home",
-        [table, *gather_rows(away)], [SMEM] + [VMEM] * rows,
+        [table, *gather_rows(away)], [SMEM] + [VMEM] * (rows + 2),
         [((len(g), *block), dtype) for g in groups],
     )
     n_long = len(LONG)

time: 135 us -> 131 us (0.970); the launches traced: 134 us -> 129 us
  starting transfers between devices: 53 us -> 49.5 us
  waiting for transfers between devices: 68.8 us -> 65.9 us
    ppermute x20, starting transfers between devices: 43.5 us -> 39.6 us  [shifted(): lax.ppermute(value, 'col', [(i, (i + by) % length) for i in range(length)])]
    ppermute x6 -> x7, waiting for transfers between devices: 31.8 us -> 28.9 us  [from_chip(): return lax.ppermute(block, 'row', pairs)]
    ppermute x6 -> x7, starting transfers between devices: 8.48 us -> 8.9 us  [from_chip(): return lax.ppermute(block, 'row', pairs)]
    ppermute x8 -> x9, waiting for transfers between devices: 3.15 us -> 2.82 us  [from_core(): lax.ppermute(block, 'row', [(i, i ^ 1) for i in range(lax.axis_size('row'...]
  transfers between devices with their start and end apart: 34 -> 36, of which waited for: 18 -> 18; matrix products, arithmetic and copies ran while one was open for 0% -> 0% of each run, Pallas kernels for 0% -> 0%
where the time goes in v6:
time: 131 us; the launch traced here: 129 us
  waiting for transfers between devices  65.9 us (50%)
  starting transfers between devices  49.5 us (38%)
  Pallas kernels  11.8 us (9%)
    ppermute x20, starting transfers between devices, shifted(): lax.ppermute(value, 'col', [(i, (i + by) % length) for i in range(length)])  39.6 us
    ppermute x20, waiting for transfers between devices, shifted(): lax.ppermute(value, 'col', [(i, (i + by) % length) for i in range(length)])  34.2 us
    ppermute x7, waiting for transfers between devices, from_chip(): return lax.ppermute(block, 'row', pairs)  28.9 us
    pallas_call x9, Pallas kernels, call(): pl.pallas_call(kernel, out_shape=[jax.ShapeDtypeStruct(shape, dtype) for...  11.8 us
    ppermute x7, starting transfers between devices, from_chip(): return lax.ppermute(block, 'row', pairs)  8.9 us
    ppermute x9, waiting for transfers between devices, from_core(): lax.ppermute(block, 'row', [(i, i ^ 1) for i in range(lax.axis_size('row'...  2.82 us
  transfers between devices with their start and end apart: 36, of which 18 were waited for; matrix products, arithmetic and copies ran while one was open for 0% of the time, Pallas kernels for 0%

profile of v6, /device:TPU:2, one launch (start us, length us, event | category | flops | bytes accessed | tf_op | source)
XLA Modules:
  0.0 128.7 jit_solution(5610022403140419410)
XLA Ops:
  4.0 6.4 %collective-permute-done.1.refs_3_ = bf16[9,128,128]{2,1,0:T(8,128)(2,1)S(1)} collective-permute-done((bf16[9,128,128]{2,1,0:T(8,128)(2,1)S(1)}, bf16[9,128,128]{2,1,0:T(8,128)(2,1)S(1)}, u32[]{:S(2)}, u32[]{:S(2)}) %collective-permute-start.1) | collective-permute-done | bytes 294944 | tf_op jit(solution)/shard_map/ppermute | solution.py:67
  10.3 2.1 %collective-permute-start.3 = (bf16[9,128,128]{2,1,0:T(8,128)(2,1)S(1)}, bf16[9,128,128]{2,1,0:T(8,128)(2,1)S(1)}, u32[]{:S(2)}, u32[]{:S(2)}) collective-permute-start(bf16[9,128,128]{2,1,0:T(8,128)(2,1)S(1)} %keep.1.refs_1_), channel_id=1, source_target_pairs={{0,128},{32,160},{64,192},{96,224},{128,0},{160,32},{192,64},{224,... | collective-permute-start | bytes 884744 | tf_op jit(solution)/shard_map/ppermute | solution.py:67
  13.0 6.5 %collective-permute-done.3.refs_5_ = bf16[9,128,128]{2,1,0:T(8,128)(2,1)S(1)} collective-permute-done((bf16[9,128,128]{2,1,0:T(8,128)(2,1)S(1)}, bf16[9,128,128]{2,1,0:T(8,128)(2,1)S(1)}, u32[]{:S(2)}, u32[]{:S(2)}) %collective-permute-start.3) | collective-permute-done | bytes 294944 | tf_op jit(solution)/shard_map/ppermute | solution.py:67
  22.7 8.8 %collective-permute-start.9 = (bf16[11,128,128]{2,1,0:T(8,128)(2,1)S(1)}, bf16[11,128,128]{2,1,0:T(8,128)(2,1)S(1)}, u32[]{:S(2)}, u32[]{:S(2)}) collective-permute-start(bf16[11,128,128]{2,1,0:T(8,128)(2,1)S(1)} %get-tuple-element.41), channel_id=1, source_target_pairs={{0,30},{1,31},{2,0},{3,1},{4,2},{5,3},{6,4},{7,5},{8,6},{9,7},{10,... | collective-permute-start | bytes 1081352 | tf_op jit(solution)/shard_map/ppermute | solution.py:48
  33.7 6.7 %collective-permute-done.11.refs_14_ = bf16[2,128,128]{2,1,0:T(8,128)(2,1)S(1)} collective-permute-done((bf16[2,128,128]{2,1,0:T(8,128)(2,1)S(1)}, bf16[2,128,128]{2,1,0:T(8,128)(2,1)S(1)}, u32[]{:S(2)}, u32[]{:S(2)}) %collective-permute-start.11) | collective-permute-done | bytes 65568 | tf_op jit(solution)/shard_map/ppermute | solution.py:48
  40.4 4.3 %collective-permute-start.13 = (bf16[10,128,128]{2,1,0:T(8,128)(2,1)S(1)}, bf16[10,128,128]{2,1,0:T(8,128)(2,1)S(1)}, u32[]{:S(2)}, u32[]{:S(2)}) collective-permute-start(bf16[10,128,128]{2,1,0:T(8,128)(2,1)S(1)} %get-tuple-element.47), channel_id=1, source_target_pairs={{0,4},{1,5},{2,6},{3,7},{4,8},{5,9},{6,10},{7,11},{8,12},{9,13},{1... | collective-permute-start | bytes 983048 | tf_op jit(solution)/shard_map/ppermute | solution.py:48
  44.7 2.0 %collective-permute-start.8 = (bf16[12,128,128]{2,1,0:T(8,128)(2,1)S(1)}, bf16[12,128,128]{2,1,0:T(8,128)(2,1)S(1)}, u32[]{:S(2)}, u32[]{:S(2)}) collective-permute-start(bf16[12,128,128]{2,1,0:T(8,128)(2,1)S(1)} %get-tuple-element.40), channel_id=1, source_target_pairs={{0,1},{1,2},{2,3},{3,4},{4,5},{5,6},{6,7},{7,8},{8,9},{9,10},{10,1... | collective-permute-start | bytes 1179656 | tf_op jit(solution)/shard_map/ppermute | solution.py:48
  47.9 6.8 %collective-permute-done.12.refs_0_.refs_6_ = bf16[9,128,128]{2,1,0:T(8,128)(2,1)S(1)} collective-permute-done((bf16[9,128,128]{2,1,0:T(8,128)(2,1)S(1)}, bf16[9,128,128]{2,1,0:T(8,128)(2,1)S(1)}, u32[]{:S(2)}, u32[]{:S(2)}) %collective-permute-start.12) | collective-permute-done | bytes 294944 | tf_op jit(solution)/shard_map/ppermute | solution.py:48
  54.8 3.2 %collective-permute-start.17 = (bf16[10,128,128]{2,1,0:T(8,128)(2,1)S(1)}, bf16[10,128,128]{2,1,0:T(8,128)(2,1)S(1)}, u32[]{:S(2)}, u32[]{:S(2)}) collective-permute-start(bf16[10,128,128]{2,1,0:T(8,128)(2,1)S(1)} %get-tuple-element.54), channel_id=1, source_target_pairs={{0,3},{1,4},{2,5},{3,6},{4,7},{5,8},{6,9},{7,10},{8,11},{9,12},{10... | collective-permute-start | bytes 983048 | tf_op jit(solution)/shard_map/ppermute | solution.py:48
  58.1 1.8 %collective-permute-start.19 = (bf16[4,128,128]{2,1,0:T(8,128)(2,1)S(1)}, bf16[4,128,128]{2,1,0:T(8,128)(2,1)S(1)}, u32[]{:S(2)}, u32[]{:S(2)}) collective-permute-start(bf16[4,128,128]{2,1,0:T(8,128)(2,1)S(1)} %get-tuple-element.56), channel_id=1, source_target_pairs={{0,4},{1,5},{2,6},{3,7},{4,8},{5,9},{6,10},{7,11},{8,12},{9,13},{1... | collective-permute-start | bytes 393224 | tf_op jit(solution)/shard_map/ppermute | solution.py:48
  60.7 5.8 %collective-permute-start.18 = (bf16[5,128,128]{2,1,0:T(8,128)(2,1)S(1)}, bf16[5,128,128]{2,1,0:T(8,128)(2,1)S(1)}, u32[]{:S(2)}, u32[]{:S(2)}) collective-permute-start(bf16[5,128,128]{2,1,0:T(8,128)(2,1)S(1)} %get-tuple-element.55), channel_id=1, source_target_pairs={{0,28},{1,29},{2,30},{3,31},{4,0},{5,1},{6,2},{7,3},{8,4},{9,5},{1... | collective-permute-start | bytes 491528 | tf_op jit(solution)/shard_map/ppermute | solution.py:48
  66.6 2.0 %collective-permute-start.15 = (bf16[5,128,128]{2,1,0:T(8,128)(2,1)S(1)}, bf16[5,128,128]{2,1,0:T(8,128)(2,1)S(1)}, u32[]{:S(2)}, u32[]{:S(2)}) collective-permute-start(bf16[5,128,128]{2,1,0:T(8,128)(2,1)S(1)} %get-tuple-element.49), channel_id=1, source_target_pairs={{0,4},{1,5},{2,6},{3,7},{4,8},{5,9},{6,10},{7,11},{8,12},{9,13},{1... | collective-permute-start | bytes 491528 | tf_op jit(solution)/shard_map/ppermute | solution.py:48
  68.6 4.6 %collective-permute-done.18.refs_12_ = bf16[5,128,128]{2,1,0:T(8,128)(2,1)S(1)} collective-permute-done((bf16[5,128,128]{2,1,0:T(8,128)(2,1)S(1)}, bf16[5,128,128]{2,1,0:T(8,128)(2,1)S(1)}, u32[]{:S(2)}, u32[]{:S(2)}) %collective-permute-start.18) | collective-permute-done | bytes 163872 | tf_op jit(solution)/shard_map/ppermute | solution.py:48
  74.9 6.8 %product.1 = (bf16[14,128,128]{2,1,0:T(8,128)(2,1)S(1)}, f32[2,128,128]{2,1,0:T(8,128)S(1)}) custom-call(s32[4096]{0:T(1024)S(1)} %reshape.3.refs_0_, bf16[16,128,128]{2,1,0:T(8,128)(2,1)S(1)} %bitcast.2, bf16[12,128,128]{2,1,0:T(8,128)(2,1)S(1)} %collective-permute-done.7.refs_0_.refs_2_, bf16[12,128,128]{2,1,0:T(8,128)(2,1)S(1)} %collective-permute-done.8.refs_1_.refs_3_, ...), custom_call_target="tpu_custom_call" | custom-call | tf_op jit(solution)/shard_map/product/pallas_call | solution.py:286
  81.7 2.1 %collective-permute-start.25 = (bf16[14,128,128]{2,1,0:T(8,128)(2,1)S(1)}, bf16[14,128,128]{2,1,0:T(8,128)(2,1)S(1)}, u32[]{:S(2)}, u32[]{:S(2)}) collective-permute-start(bf16[14,128,128]{2,1,0:T(8,128)(2,1)S(1)} %get-tuple-element.58.refs_1_), channel_id=1, source_target_pairs={{0,192},{32,224},{64,0},{96,32},{128,64},{160,96},{192,128},{224,1... | collective-permute-start | bytes 1376264 | tf_op jit(solution)/shard_map/ppermute | solution.py:67
  84.2 9.7 %collective-permute-done.25.refs_9_ = bf16[14,128,128]{2,1,0:T(8,128)(2,1)S(1)} collective-permute-done((bf16[14,128,128]{2,1,0:T(8,128)(2,1)S(1)}, bf16[14,128,128]{2,1,0:T(8,128)(2,1)S(1)}, u32[]{:S(2)}, u32[]{:S(2)}) %collective-permute-start.25) | collective-permute-done | bytes 458784 | tf_op jit(solution)/shard_map/ppermute | solution.py:67
  96.6 3.4 %collective-permute-done.26.refs_7_ = bf16[7,128,128]{2,1,0:T(8,128)(2,1)S(1)} collective-permute-done((bf16[7,128,128]{2,1,0:T(8,128)(2,1)S(1)}, bf16[7,128,128]{2,1,0:T(8,128)(2,1)S(1)}, u32[]{:S(2)}, u32[]{:S(2)}) %collective-permute-start.26) | collective-permute-done | bytes 229408 | tf_op jit(solution)/shard_map/ppermute | solution.py:67
  100.0 2.7 %collective-permute-done.23.refs_5_ = bf16[7,128,128]{2,1,0:T(8,128)(2,1)S(1)} collective-permute-done((bf16[7,128,128]{2,1,0:T(8,128)(2,1)S(1)}, bf16[7,128,128]{2,1,0:T(8,128)(2,1)S(1)}, u32[]{:S(2)}, u32[]{:S(2)}) %collective-permute-start.23) | collective-permute-done | bytes 229408 | tf_op jit(solution)/shard_map/ppermute | solution.py:67
  105.9 2.4 %collective-permute-start.29 = (bf16[4,128,128]{2,1,0:T(8,128)(2,1)S(1)}, bf16[4,128,128]{2,1,0:T(8,128)(2,1)S(1)}, u32[]{:S(2)}, u32[]{:S(2)}) collective-permute-start(bf16[4,128,128]{2,1,0:T(8,128)(2,1)S(1)} %get-tuple-element.59), channel_id=1, source_target_pairs={{0,28},{1,29},{2,30},{3,31},{4,0},{5,1},{6,2},{7,3},{8,4},{9,5},{1... | collective-permute-start | bytes 393224 | tf_op jit(solution)/shard_map/ppermute | solution.py:48
  109.2 3.2 %collective-permute-start.31 = (bf16[1,128,128]{2,1,0:T(8,128)(2,1)S(1)}, bf16[1,128,128]{2,1,0:T(8,128)(2,1)S(1)}, u32[]{:S(2)}, u32[]{:S(2)}) collective-permute-start(bf16[1,128,128]{2,1,0:T(8,128)(2,1)S(1)} %get-tuple-element.61), channel_id=1, source_target_pairs={{0,24},{1,25},{2,26},{3,27},{4,28},{5,29},{6,30},{7,31},{8,0},{9,1... | collective-permute-start | bytes 98312 | tf_op jit(solution)/shard_map/ppermute | solution.py:48
  112.4 1.8 %collective-permute-done.31.refs_2_ = bf16[1,128,128]{2,1,0:T(8,128)(2,1)S(1)} collective-permute-done((bf16[1,128,128]{2,1,0:T(8,128)(2,1)S(1)}, bf16[1,128,128]{2,1,0:T(8,128)(2,1)S(1)}, u32[]{:S(2)}, u32[]{:S(2)}) %collective-permute-start.31) | collective-permute-done | bytes 32800 | tf_op jit(solution)/shard_map/ppermute | solution.py:48
  114.2 2.9 %collective-permute-done.32.refs_3_ = bf16[2,128,128]{2,1,0:T(8,128)(2,1)S(1)} collective-permute-done((bf16[2,128,128]{2,1,0:T(8,128)(2,1)S(1)}, bf16[2,128,128]{2,1,0:T(8,128)(2,1)S(1)}, u32[]{:S(2)}, u32[]{:S(2)}) %collective-permute-start.32) | collective-permute-done | bytes 65568 | tf_op jit(solution)/shard_map/ppermute | solution.py:48
  119.8 3.6 %collective-permute-done.33.refs_4_ = bf16[4,128,128]{2,1,0:T(8,128)(2,1)S(1)} collective-permute-done((bf16[4,128,128]{2,1,0:T(8,128)(2,1)S(1)}, bf16[4,128,128]{2,1,0:T(8,128)(2,1)S(1)}, u32[]{:S(2)}, u32[]{:S(2)}) %collective-permute-start.33) | collective-permute-done | bytes 131104 | tf_op jit(solution)/shard_map/ppermute | solution.py:48
  123.4 4.1 %collective-permute-done.34.refs_5_ = bf16[4,128,128]{2,1,0:T(8,128)(2,1)S(1)} collective-permute-done((bf16[4,128,128]{2,1,0:T(8,128)(2,1)S(1)}, bf16[4,128,128]{2,1,0:T(8,128)(2,1)S(1)}, u32[]{:S(2)}, u32[]{:S(2)}) %collective-permute-start.34) | collective-permute-done | bytes 131104 | tf_op jit(solution)/shard_map/ppermute | solution.py:48
  (67 shorter events, 24.8 us)
Async XLA Ops:
  1.5 8.8 %collective-permute-start.1 = (bf16[9,128,128]{2,1,0:T(8,128)(2,1)S(1)}, bf16[9,128,128]{2,1,0:T(8,128)(2,1)S(1)}, u32[]{:S(2)}, u32[]{:S(2)}) collective-permute-start(bf16[9,128,128]{2,1,0:T(8,128)(2,1)S(1)} %keep.1.refs_1_), channel_id=1, source_target_pairs={{0,64},{32,96},{64,128},{96,160},{128,192},{160,224},{192,0},{224,... | collective-permute-start | bytes 884744 | tf_op jit(solution)/shard_map/ppermute | solution.py:67
  3.1 9.9 %collective-permute-start.5 = (bf16[9,128,128]{2,1,0:T(8,128)(2,1)S(1)}, bf16[9,128,128]{2,1,0:T(8,128)(2,1)S(1)}, u32[]{:S(2)}, u32[]{:S(2)}) collective-permute-start(bf16[9,128,128]{2,1,0:T(8,128)(2,1)S(1)} %keep.1.refs_1_), channel_id=1, source_target_pairs={{0,192},{32,224},{64,0},{96,32},{128,64},{160,96},{192,128},{224,1... | collective-permute-start | bytes 884744 | tf_op jit(solution)/shard_map/ppermute | solution.py:67
  10.3 9.1 %collective-permute-start.3 = (bf16[9,128,128]{2,1,0:T(8,128)(2,1)S(1)}, bf16[9,128,128]{2,1,0:T(8,128)(2,1)S(1)}, u32[]{:S(2)}, u32[]{:S(2)}) collective-permute-start(bf16[9,128,128]{2,1,0:T(8,128)(2,1)S(1)} %keep.1.refs_1_), channel_id=1, source_target_pairs={{0,128},{32,160},{64,192},{96,224},{128,0},{160,32},{192,64},{224,... | collective-permute-start | bytes 884744 | tf_op jit(solution)/shard_map/ppermute | solution.py:67
  22.7 22.1 %collective-permute-start.9 = (bf16[11,128,128]{2,1,0:T(8,128)(2,1)S(1)}, bf16[11,128,128]{2,1,0:T(8,128)(2,1)S(1)}, u32[]{:S(2)}, u32[]{:S(2)}) collective-permute-start(bf16[11,128,128]{2,1,0:T(8,128)(2,1)S(1)} %get-tuple-element.41), channel_id=1, source_target_pairs={{0,30},{1,31},{2,0},{3,1},{4,2},{5,3},{6,4},{7,5},{8,6},{9,7},{10,... | collective-permute-start | bytes 1081352 | tf_op jit(solution)/shard_map/ppermute | solution.py:48
  31.5 8.9 %collective-permute-start.11 = (bf16[2,128,128]{2,1,0:T(8,128)(2,1)S(1)}, bf16[2,128,128]{2,1,0:T(8,128)(2,1)S(1)}, u32[]{:S(2)}, u32[]{:S(2)}) collective-permute-start(bf16[2,128,128]{2,1,0:T(8,128)(2,1)S(1)} %get-tuple-element.44), channel_id=1, source_target_pairs={{0,16},{1,17},{2,18},{3,19},{4,20},{5,21},{6,22},{7,23},{8,24},{9,... | collective-permute-start | bytes 196616 | tf_op jit(solution)/shard_map/ppermute | solution.py:48
  32.9 15.0 %collective-permute-start.10 = (bf16[11,128,128]{2,1,0:T(8,128)(2,1)S(1)}, bf16[11,128,128]{2,1,0:T(8,128)(2,1)S(1)}, u32[]{:S(2)}, u32[]{:S(2)}) collective-permute-start(bf16[11,128,128]{2,1,0:T(8,128)(2,1)S(1)} %get-tuple-element.42), channel_id=1, source_target_pairs={{0,2},{1,3},{2,4},{3,5},{4,6},{5,7},{6,8},{7,9},{8,10},{9,11},{10,... | collective-permute-start | bytes 1081352 | tf_op jit(solution)/shard_map/ppermute | solution.py:48
  40.4 14.3 %collective-permute-start.13 = (bf16[10,128,128]{2,1,0:T(8,128)(2,1)S(1)}, bf16[10,128,128]{2,1,0:T(8,128)(2,1)S(1)}, u32[]{:S(2)}, u32[]{:S(2)}) collective-permute-start(bf16[10,128,128]{2,1,0:T(8,128)(2,1)S(1)} %get-tuple-element.47), channel_id=1, source_target_pairs={{0,4},{1,5},{2,6},{3,7},{4,8},{5,9},{6,10},{7,11},{8,12},{9,13},{1... | collective-permute-start | bytes 983048 | tf_op jit(solution)/shard_map/ppermute | solution.py:48
  44.7 9.9 %collective-permute-start.12 = (bf16[9,128,128]{2,1,0:T(8,128)(2,1)S(1)}, bf16[9,128,128]{2,1,0:T(8,128)(2,1)S(1)}, u32[]{:S(2)}, u32[]{:S(2)}) collective-permute-start(bf16[9,128,128]{2,1,0:T(8,128)(2,1)S(1)} %get-tuple-element.45), channel_id=1, source_target_pairs={{0,28},{1,29},{2,30},{3,31},{4,0},{5,1},{6,2},{7,3},{8,4},{9,5},{1... | collective-permute-start | bytes 884744 | tf_op jit(solution)/shard_map/ppermute | solution.py:48
  44.7 15.9 %collective-permute-start.7 = (bf16[12,128,128]{2,1,0:T(8,128)(2,1)S(1)}, bf16[12,128,128]{2,1,0:T(8,128)(2,1)S(1)}, u32[]{:S(2)}, u32[]{:S(2)}) collective-permute-start(bf16[12,128,128]{2,1,0:T(8,128)(2,1)S(1)} %get-tuple-element.39), channel_id=1, source_target_pairs={{0,31},{1,0},{2,1},{3,2},{4,3},{5,4},{6,5},{7,6},{8,7},{9,8},{10,9... | collective-permute-start | bytes 1179656 | tf_op jit(solution)/shard_map/ppermute | solution.py:48
  44.7 21.7 %collective-permute-start.8 = (bf16[12,128,128]{2,1,0:T(8,128)(2,1)S(1)}, bf16[12,128,128]{2,1,0:T(8,128)(2,1)S(1)}, u32[]{:S(2)}, u32[]{:S(2)}) collective-permute-start(bf16[12,128,128]{2,1,0:T(8,128)(2,1)S(1)} %get-tuple-element.40), channel_id=1, source_target_pairs={{0,1},{1,2},{2,3},{3,4},{4,5},{5,6},{6,7},{7,8},{8,9},{9,10},{10,1... | collective-permute-start | bytes 1179656 | tf_op jit(solution)/shard_map/ppermute | solution.py:48
  54.7 20.2 %collective-permute-start.16 = (bf16[10,128,128]{2,1,0:T(8,128)(2,1)S(1)}, bf16[10,128,128]{2,1,0:T(8,128)(2,1)S(1)}, u32[]{:S(2)}, u32[]{:S(2)}) collective-permute-start(bf16[10,128,128]{2,1,0:T(8,128)(2,1)S(1)} %get-tuple-element.53), channel_id=1, source_target_pairs={{0,29},{1,30},{2,31},{3,0},{4,1},{5,2},{6,3},{7,4},{8,5},{9,6},{10... | collective-permute-start | bytes 983048 | tf_op jit(solution)/shard_map/ppermute | solution.py:48
  54.8 20.1 %collective-permute-start.17 = (bf16[10,128,128]{2,1,0:T(8,128)(2,1)S(1)}, bf16[10,128,128]{2,1,0:T(8,128)(2,1)S(1)}, u32[]{:S(2)}, u32[]{:S(2)}) collective-permute-start(bf16[10,128,128]{2,1,0:T(8,128)(2,1)S(1)} %get-tuple-element.54), channel_id=1, source_target_pairs={{0,3},{1,4},{2,5},{3,6},{4,7},{5,8},{6,9},{7,10},{8,11},{9,12},{10... | collective-permute-start | bytes 983048 | tf_op jit(solution)/shard_map/ppermute | solution.py:48
  58.1 8.5 %collective-permute-start.19 = (bf16[4,128,128]{2,1,0:T(8,128)(2,1)S(1)}, bf16[4,128,128]{2,1,0:T(8,128)(2,1)S(1)}, u32[]{:S(2)}, u32[]{:S(2)}) collective-permute-start(bf16[4,128,128]{2,1,0:T(8,128)(2,1)S(1)} %get-tuple-element.56), channel_id=1, source_target_pairs={{0,4},{1,5},{2,6},{3,7},{4,8},{5,9},{6,10},{7,11},{8,12},{9,13},{1... | collective-permute-start | bytes 393224 | tf_op jit(solution)/shard_map/ppermute | solution.py:48
  60.7 12.5 %collective-permute-start.18 = (bf16[5,128,128]{2,1,0:T(8,128)(2,1)S(1)}, bf16[5,128,128]{2,1,0:T(8,128)(2,1)S(1)}, u32[]{:S(2)}, u32[]{:S(2)}) collective-permute-start(bf16[5,128,128]{2,1,0:T(8,128)(2,1)S(1)} %get-tuple-element.55), channel_id=1, source_target_pairs={{0,28},{1,29},{2,30},{3,31},{4,0},{5,1},{6,2},{7,3},{8,4},{9,5},{1... | collective-permute-start | bytes 491528 | tf_op jit(solution)/shard_map/ppermute | solution.py:48
  66.5 8.4 %collective-permute-start.14 = (bf16[5,128,128]{2,1,0:T(8,128)(2,1)S(1)}, bf16[5,128,128]{2,1,0:T(8,128)(2,1)S(1)}, u32[]{:S(2)}, u32[]{:S(2)}) collective-permute-start(bf16[5,128,128]{2,1,0:T(8,128)(2,1)S(1)} %get-tuple-element.48), channel_id=1, source_target_pairs={{0,28},{1,29},{2,30},{3,31},{4,0},{5,1},{6,2},{7,3},{8,4},{9,5},{1... | collective-permute-start | bytes 491528 | tf_op jit(solution)/shard_map/ppermute | solution.py:48
  66.6 8.3 %collective-permute-start.15 = (bf16[5,128,128]{2,1,0:T(8,128)(2,1)S(1)}, bf16[5,128,128]{2,1,0:T(8,128)(2,1)S(1)}, u32[]{:S(2)}, u32[]{:S(2)}) collective-permute-start(bf16[5,128,128]{2,1,0:T(8,128)(2,1)S(1)} %get-tuple-element.49), channel_id=1, source_target_pairs={{0,4},{1,5},{2,6},{3,7},{4,8},{5,9},{6,10},{7,11},{8,12},{9,13},{1... | collective-permute-start | bytes 491528 | tf_op jit(solution)/shard_map/ppermute | solution.py:48
  81.7 12.2 %collective-permute-start.25 = (bf16[14,128,128]{2,1,0:T(8,128)(2,1)S(1)}, bf16[14,128,128]{2,1,0:T(8,128)(2,1)S(1)}, u32[]{:S(2)}, u32[]{:S(2)}) collective-permute-start(bf16[14,128,128]{2,1,0:T(8,128)(2,1)S(1)} %get-tuple-element.58.refs_1_), channel_id=1, source_target_pairs={{0,192},{32,224},{64,0},{96,32},{128,64},{160,96},{192,128},{224,1... | collective-permute-start | bytes 1376264 | tf_op jit(solution)/shard_map/ppermute | solution.py:67
  83.7 11.1 %collective-permute-start.21 = (bf16[14,128,128]{2,1,0:T(8,128)(2,1)S(1)}, bf16[14,128,128]{2,1,0:T(8,128)(2,1)S(1)}, u32[]{:S(2)}, u32[]{:S(2)}) collective-permute-start(bf16[14,128,128]{2,1,0:T(8,128)(2,1)S(1)} %get-tuple-element.58.refs_1_), channel_id=1, source_target_pairs={{0,64},{32,96},{64,128},{96,160},{128,192},{160,224},{192,0},{224,... | collective-permute-start | bytes 1376264 | tf_op jit(solution)/shard_map/ppermute | solution.py:67
  84.2 18.5 %collective-permute-start.20 = (bf16[14,128,128]{2,1,0:T(8,128)(2,1)S(1)}, bf16[14,128,128]{2,1,0:T(8,128)(2,1)S(1)}, u32[]{:S(2)}, u32[]{:S(2)}) collective-permute-start(bf16[14,128,128]{2,1,0:T(8,128)(2,1)S(1)} %get-tuple-element.58.refs_1_), channel_id=1, source_target_pairs={{0,32},{32,0},{64,96},{96,64},{128,160},{160,128},{192,224},{224,1... | collective-permute-start | bytes 1376264 | tf_op jit(solution)/shard_map/ppermute | solution.py:71
  105.9 11.3 %collective-permute-start.29 = (bf16[4,128,128]{2,1,0:T(8,128)(2,1)S(1)}, bf16[4,128,128]{2,1,0:T(8,128)(2,1)S(1)}, u32[]{:S(2)}, u32[]{:S(2)}) collective-permute-start(bf16[4,128,128]{2,1,0:T(8,128)(2,1)S(1)} %get-tuple-element.59), channel_id=1, source_target_pairs={{0,28},{1,29},{2,30},{3,31},{4,0},{5,1},{6,2},{7,3},{8,4},{9,5},{1... | collective-permute-start | bytes 393224 | tf_op jit(solution)/shard_map/ppermute | solution.py:48
  108.3 8.8 %collective-permute-start.30 = (bf16[4,128,128]{2,1,0:T(8,128)(2,1)S(1)}, bf16[4,128,128]{2,1,0:T(8,128)(2,1)S(1)}, u32[]{:S(2)}, u32[]{:S(2)}) collective-permute-start(bf16[4,128,128]{2,1,0:T(8,128)(2,1)S(1)} %get-tuple-element.60), channel_id=1, source_target_pairs={{0,4},{1,5},{2,6},{3,7},{4,8},{5,9},{6,10},{7,11},{8,12},{9,13},{1... | collective-permute-start | bytes 393224 | tf_op jit(solution)/shard_map/ppermute | solution.py:48
  108.3 8.8 %collective-permute-start.32 = (bf16[2,128,128]{2,1,0:T(8,128)(2,1)S(1)}, bf16[2,128,128]{2,1,0:T(8,128)(2,1)S(1)}, u32[]{:S(2)}, u32[]{:S(2)}) collective-permute-start(bf16[2,128,128]{2,1,0:T(8,128)(2,1)S(1)} %get-tuple-element.62), channel_id=1, source_target_pairs={{0,8},{1,9},{2,10},{3,11},{4,12},{5,13},{6,14},{7,15},{8,16},{9,17... | collective-permute-start | bytes 196616 | tf_op jit(solution)/shard_map/ppermute | solution.py:48
  118.2 9.3 %collective-permute-start.34 = (bf16[4,128,128]{2,1,0:T(8,128)(2,1)S(1)}, bf16[4,128,128]{2,1,0:T(8,128)(2,1)S(1)}, u32[]{:S(2)}, u32[]{:S(2)}) collective-permute-start(bf16[4,128,128]{2,1,0:T(8,128)(2,1)S(1)} %get-tuple-element.69), channel_id=1, source_target_pairs={{0,1},{1,2},{2,3},{3,4},{4,5},{5,6},{6,7},{7,8},{8,9},{9,10},{10,1... | collective-permute-start | bytes 393224 | tf_op jit(solution)/shard_map/ppermute | solution.py:48
  119.3 8.3 %collective-permute-start.35 = (bf16[4,128,128]{2,1,0:T(8,128)(2,1)S(1)}, bf16[4,128,128]{2,1,0:T(8,128)(2,1)S(1)}, u32[]{:S(2)}, u32[]{:S(2)}) collective-permute-start(bf16[4,128,128]{2,1,0:T(8,128)(2,1)S(1)} %get-tuple-element.70), channel_id=1, source_target_pairs={{0,30},{1,31},{2,0},{3,1},{4,2},{5,3},{6,4},{7,5},{8,6},{9,7},{10,... | collective-permute-start | bytes 393224 | tf_op jit(solution)/shard_map/ppermute | solution.py:48
  (15 other events, 103.1 us)

commit v7 on v6

--- a/solution.py
+++ b/solution.py
@@ -189,54 +189,77 @@
         return self.ref[self.first + p]
 
 
-def product_kernel(plan, held, *refs):
-    cols, own = refs[:2]
+def parts_of(plan, refs, held):
     arrived = {}
-    for ref, group in zip(refs[2:2 + len(held)], held):
+    for ref, group in zip(refs, held):
         for a in group:
             arrived[a] = Part(ref, start_of(plan, group, a))
-    away, self_new, total, half = refs[2 + len(held):]
+    return arrived
+
+
+def add_edges(plan, cols, arrived, strides, left, total, scale):
     n = plan.slot_count
     i = plan.row_id(lax.axis_index("row"), lax.axis_index("col"))
-
-    def add_edges(left, scale):
-        for a in plan.moved:
-            for p, b in enumerate(plan.edges[a]):
-                ta, tb = plan.slot[a], plan.slot[b]
-                k, j = cols[i * n + ta], cols[i * n + tb]
-
-                @pl.when(cols[k * n + plan.slot[b - a]] == j)
-                def _():
-                    edge = arrived[a][p + 1]
-                    total[tb] += scale * nn(left[ta], edge)
-                    total[ta] += scale * nt(left[tb], edge)
-
-    acc = nt(own[0], own[0])
-    for s in range(1, n):
-        acc = acc + nt(own[s], own[s])
-    total[0] = acc
-    half[0] = acc.astype(half.dtype)
+    for a in strides:
+        for p, b in enumerate(plan.edges[a]):
+            ta, tb = plan.slot[a], plan.slot[b]
+            k, j = cols[i * n + ta], cols[i * n + tb]
+
+            @pl.when(cols[k * n + plan.slot[b - a]] == j)
+            def _():
+                edge = arrived[a][p + 1]
+                total[tb] += scale * nn(left[ta], edge)
+                total[ta] += scale * nt(left[tb], edge)
+
+
+def early_kernel(plan, held, *refs):
+    cols, own, base = refs[0], refs[1], refs[-1]
+    arrived = parts_of(plan, refs[2:-1], held)
+    square = nt(own[0], own[0])
+    for s in range(1, plan.slot_count):
+        square = square + nt(own[s], own[s])
+    base[0] = square
     for a in plan.moved:
         t = plan.slot[a]
-        total[t] = nn(own[0], own[t]) + nn(own[t], arrived[a][0])
-    add_edges(own, 1.0)
+        base[t] = nn(own[0], own[t])
+        if a in FIRST:
+            base[t] += nn(own[t], arrived[a][0])
+    add_edges(plan, cols, arrived, [a for a in plan.moved if a in FIRST], own, base, 1.0)
+
+
+def product_kernel(plan, held, *refs):
+    cols, own, base = refs[:3]
+    arrived = parts_of(plan, refs[3:3 + len(held)], held)
+    away, half, far_square, total = refs[3 + len(held):]
+    n = plan.slot_count
+    for a in plan.moved:
+        t = plan.slot[a]
+        total[t] = base[t]
+        if a not in FIRST:
+            total[t] += nn(own[t], arrived[a][0])
+    add_edges(plan, cols, arrived, [a for a in plan.moved if a not in FIRST], own, total, 1.0)
+    half[0] = base[0].astype(half.dtype)
     for t in range(1, n):
         half[t] = total[t].astype(half.dtype)
-    acc = nt(own[0], half[0])
-    for s in range(1, n):
-        acc = acc + nt(own[s], half[s])
-    self_new[0] = 3.0 * total[0] - 2.0 * acc
-    t = plan.slot[plan.far]
-    cube = nn(own[0], half[t]) + nn(own[t], arrived[plan.far][1])
-    self_new[1] = 3.0 * total[t] - 2.0 * cube
+    far_square[...] = total[plan.slot[plan.far]]
     for a in plan.near_moved:
         t = plan.slot[a]
         cube = nn(half[0], own[t]) + nn(half[t], arrived[a][0])
         total[t] = 3.0 * total[t] - 2.0 * cube
-    add_edges(half, -2.0)
+    add_edges(plan, cols, arrived, plan.moved, half, total, -2.0)
     for a in plan.near_moved:
         t = plan.slot[a]
         away[t - 1] = total[t].astype(away.dtype)
+
+
+def late_kernel(plan, own, half, base, far_square, far, self_new):
+    cube = nt(own[0], half[0])
+    for s in range(1, plan.slot_count):
+        cube = cube + nt(own[s], half[s])
+    self_new[0] = 3.0 * base[0] - 2.0 * cube
+    t = plan.slot[plan.far]
+    cube = nn(own[0], half[t]) + nn(own[t], far[1])
+    self_new[1] = 3.0 * far_square[...] - 2.0 * cube
 
 
 def home_kernel(plan, *refs):
@@ -335,11 +358,21 @@
         held += list(bundles.values())
     came = list(came.values()) + second + [far]
     held.append([plan.far])
-    away, self_new = call(
+    n_first = len(FIRST)
+    (base,) = call(
+        functools.partial(early_kernel, plan, held[:n_first]), "early",
+        [table, own, *came[:n_first]], [SMEM] + [VMEM] * (1 + n_first),
+        [((slot_count, *block), jnp.float32)],
+    )
+    away, half, far_square = call(
         functools.partial(product_kernel, plan, held), "product",
-        [table, own, *came], [SMEM] + [VMEM] * (1 + len(came)),
-        [((len(plan.near_moved), *block), dtype), ((2, *block), jnp.float32)],
-        [pltpu.VMEM((slot_count, *block), jnp.float32), pltpu.VMEM((slot_count, *block), dtype)],
+        [table, own, base, *came], [SMEM] + [VMEM] * (2 + len(came)),
+        [((len(plan.near_moved), *block), dtype), ((slot_count, *block), dtype), (block, jnp.float32)],
+        [pltpu.VMEM((slot_count, *block), jnp.float32)],
+    )
+    (self_new,) = call(
+        functools.partial(late_kernel, plan), "late",
+        [own, half, base, far_square, far], [VMEM] * 5, [((2, *block), jnp.float32)],
     )
     groups = home_groups(plan)
     homing = call(

time: 131 us -> 128 us (0.977); the launches traced: 129 us -> 127 us
  waiting for transfers between devices: 65.9 us -> 60.3 us
  starting transfers between devices: 49.5 us -> 52.6 us
    ppermute x20, waiting for transfers between devices: 34.2 us -> 31 us  [shifted(): lax.ppermute(value, 'col', [(i, (i + by) % length) for i in range(length)])]
    ppermute x20, starting transfers between devices: 39.6 us -> 42.7 us  [shifted(): lax.ppermute(value, 'col', [(i, (i + by) % length) for i in range(length)])]
    ppermute x7, waiting for transfers between devices: 28.9 us -> 26.5 us  [from_chip(): return lax.ppermute(block, 'row', pairs)]
    pallas_call x9 -> x11, Pallas kernels: 11.8 us -> 13 us  [call(): pl.pallas_call(kernel, out_shape=[jax.ShapeDtypeStruct(shape, dtype) for...]
  transfers between devices with their start and end apart: 36 -> 36, of which waited for: 18 -> 19; matrix products, arithmetic and copies ran while one was open for 0% -> 0% of each run, Pallas kernels for 0% -> 2%
where the time goes in v7:
time: 128 us; the launch traced here: 127 us
  waiting for transfers between devices  60.3 us (47%)
  starting transfers between devices  52.6 us (41%)
  Pallas kernels  13 us (10%)
  local copies, waits for them, and re-layouts  1.28 us (1%)
    ppermute x20, starting transfers between devices, shifted(): lax.ppermute(value, 'col', [(i, (i + by) % length) for i in range(length)])  42.7 us
    ppermute x20, waiting for transfers between devices, shifted(): lax.ppermute(value, 'col', [(i, (i + by) % length) for i in range(length)])  31 us
    ppermute x7, waiting for transfers between devices, from_chip(): return lax.ppermute(block, 'row', pairs)  26.5 us
    pallas_call x11, Pallas kernels, call(): pl.pallas_call(kernel, out_shape=[jax.ShapeDtypeStruct(shape, dtype) for...  13 us
    ppermute x7, starting transfers between devices, from_chip(): return lax.ppermute(block, 'row', pairs)  8.85 us
    ppermute x9, waiting for transfers between devices, from_core(): lax.ppermute(block, 'row', [(i, i ^ 1) for i in range(lax.axis_size('row'...  2.82 us
  transfers between devices with their start and end apart: 36, of which 19 were waited for; matrix products, arithmetic and copies ran while one was open for 0% of the time, Pallas kernels for 2%

profile of v7, /device:TPU:2, one launch (start us, length us, event | category | flops | bytes accessed | tf_op | source)
XLA Modules:
  0.0 127.3 jit_solution(157482437373167577)
XLA Ops:
  4.0 6.4 %collective-permute-done.1.refs_3_ = bf16[9,128,128]{2,1,0:T(8,128)(2,1)S(1)} collective-permute-done((bf16[9,128,128]{2,1,0:T(8,128)(2,1)S(1)}, bf16[9,128,128]{2,1,0:T(8,128)(2,1)S(1)}, u32[]{:S(2)}, u32[]{:S(2)}) %collective-permute-start.1) | collective-permute-done | bytes 294944 | tf_op jit(solution)/shard_map/ppermute | solution.py:67
  10.3 2.1 %collective-permute-start.3 = (bf16[9,128,128]{2,1,0:T(8,128)(2,1)S(1)}, bf16[9,128,128]{2,1,0:T(8,128)(2,1)S(1)}, u32[]{:S(2)}, u32[]{:S(2)}) collective-permute-start(bf16[9,128,128]{2,1,0:T(8,128)(2,1)S(1)} %keep.1.refs_1_), channel_id=1, source_target_pairs={{0,128},{32,160},{64,192},{96,224},{128,0},{160,32},{192,64},{224,... | collective-permute-start | bytes 884744 | tf_op jit(solution)/shard_map/ppermute | solution.py:67
  13.0 6.5 %collective-permute-done.3.refs_5_ = bf16[9,128,128]{2,1,0:T(8,128)(2,1)S(1)} collective-permute-done((bf16[9,128,128]{2,1,0:T(8,128)(2,1)S(1)}, bf16[9,128,128]{2,1,0:T(8,128)(2,1)S(1)}, u32[]{:S(2)}, u32[]{:S(2)}) %collective-permute-start.3) | collective-permute-done | bytes 294944 | tf_op jit(solution)/shard_map/ppermute | solution.py:67
  22.7 8.8 %collective-permute-start.9 = (bf16[11,128,128]{2,1,0:T(8,128)(2,1)S(1)}, bf16[11,128,128]{2,1,0:T(8,128)(2,1)S(1)}, u32[]{:S(2)}, u32[]{:S(2)}) collective-permute-start(bf16[11,128,128]{2,1,0:T(8,128)(2,1)S(1)} %get-tuple-element.42), channel_id=1, source_target_pairs={{0,30},{1,31},{2,0},{3,1},{4,2},{5,3},{6,4},{7,5},{8,6},{9,7},{10,... | collective-permute-start | bytes 1081352 | tf_op jit(solution)/shard_map/ppermute | solution.py:48
  33.7 6.7 %collective-permute-done.11.refs_15_.far = bf16[2,128,128]{2,1,0:T(8,128)(2,1)S(1)} collective-permute-done((bf16[2,128,128]{2,1,0:T(8,128)(2,1)S(1)}, bf16[2,128,128]{2,1,0:T(8,128)(2,1)S(1)}, u32[]{:S(2)}, u32[]{:S(2)}) %collective-permute-start.11) | collective-permute-done | bytes 65568 | tf_op jit(solution)/shard_map/ppermute | solution.py:48
  40.4 4.3 %collective-permute-start.13 = (bf16[10,128,128]{2,1,0:T(8,128)(2,1)S(1)}, bf16[10,128,128]{2,1,0:T(8,128)(2,1)S(1)}, u32[]{:S(2)}, u32[]{:S(2)}) collective-permute-start(bf16[10,128,128]{2,1,0:T(8,128)(2,1)S(1)} %get-tuple-element.48), channel_id=1, source_target_pairs={{0,4},{1,5},{2,6},{3,7},{4,8},{5,9},{6,10},{7,11},{8,12},{9,13},{1... | collective-permute-start | bytes 983048 | tf_op jit(solution)/shard_map/ppermute | solution.py:48
  44.7 2.0 %collective-permute-start.8 = (bf16[12,128,128]{2,1,0:T(8,128)(2,1)S(1)}, bf16[12,128,128]{2,1,0:T(8,128)(2,1)S(1)}, u32[]{:S(2)}, u32[]{:S(2)}) collective-permute-start(bf16[12,128,128]{2,1,0:T(8,128)(2,1)S(1)} %get-tuple-element.41), channel_id=1, source_target_pairs={{0,1},{1,2},{2,3},{3,4},{4,5},{5,6},{6,7},{7,8},{8,9},{9,10},{10,1... | collective-permute-start | bytes 1179656 | tf_op jit(solution)/shard_map/ppermute | solution.py:48
  47.9 6.8 %collective-permute-done.12.refs_6_.refs_0_.refs_7_ = bf16[9,128,128]{2,1,0:T(8,128)(2,1)S(1)} collective-permute-done((bf16[9,128,128]{2,1,0:T(8,128)(2,1)S(1)}, bf16[9,128,128]{2,1,0:T(8,128)(2,1)S(1)}, u32[]{:S(2)}, u32[]{:S(2)}) %collective-permute-start.12) | collective-permute-done | bytes 294944 | tf_op jit(solution)/shard_map/ppermute | solution.py:48
  54.8 3.2 %collective-permute-start.17 = (bf16[10,128,128]{2,1,0:T(8,128)(2,1)S(1)}, bf16[10,128,128]{2,1,0:T(8,128)(2,1)S(1)}, u32[]{:S(2)}, u32[]{:S(2)}) collective-permute-start(bf16[10,128,128]{2,1,0:T(8,128)(2,1)S(1)} %get-tuple-element.55), channel_id=1, source_target_pairs={{0,3},{1,4},{2,5},{3,6},{4,7},{5,8},{6,9},{7,10},{8,11},{9,12},{10... | collective-permute-start | bytes 983048 | tf_op jit(solution)/shard_map/ppermute | solution.py:48
  58.1 1.8 %collective-permute-start.19 = (bf16[4,128,128]{2,1,0:T(8,128)(2,1)S(1)}, bf16[4,128,128]{2,1,0:T(8,128)(2,1)S(1)}, u32[]{:S(2)}, u32[]{:S(2)}) collective-permute-start(bf16[4,128,128]{2,1,0:T(8,128)(2,1)S(1)} %get-tuple-element.57), channel_id=1, source_target_pairs={{0,4},{1,5},{2,6},{3,7},{4,8},{5,9},{6,10},{7,11},{8,12},{9,13},{1... | collective-permute-start | bytes 393224 | tf_op jit(solution)/shard_map/ppermute | solution.py:48
  60.7 5.8 %collective-permute-start.18 = (bf16[5,128,128]{2,1,0:T(8,128)(2,1)S(1)}, bf16[5,128,128]{2,1,0:T(8,128)(2,1)S(1)}, u32[]{:S(2)}, u32[]{:S(2)}) collective-permute-start(bf16[5,128,128]{2,1,0:T(8,128)(2,1)S(1)} %get-tuple-element.56), channel_id=1, source_target_pairs={{0,28},{1,29},{2,30},{3,31},{4,0},{5,1},{6,2},{7,3},{8,4},{9,5},{1... | collective-permute-start | bytes 491528 | tf_op jit(solution)/shard_map/ppermute | solution.py:48
  66.6 2.0 %collective-permute-start.15 = (bf16[5,128,128]{2,1,0:T(8,128)(2,1)S(1)}, bf16[5,128,128]{2,1,0:T(8,128)(2,1)S(1)}, u32[]{:S(2)}, u32[]{:S(2)}) collective-permute-start(bf16[5,128,128]{2,1,0:T(8,128)(2,1)S(1)} %get-tuple-element.50), channel_id=1, source_target_pairs={{0,4},{1,5},{2,6},{3,7},{4,8},{5,9},{6,10},{7,11},{8,12},{9,13},{1... | collective-permute-start | bytes 491528 | tf_op jit(solution)/shard_map/ppermute | solution.py:48
  68.6 2.4 %early.1.refs_2_.base = f32[16,128,128]{2,1,0:T(8,128)S(1)} custom-call(s32[4096]{0:T(1024)S(1)} %reshape.3.refs_0_, bf16[16,128,128]{2,1,0:T(8,128)(2,1)S(1)} %bitcast.2, bf16[12,128,128]{2,1,0:T(8,128)(2,1)S(1)} %collective-permute-done.7.refs_2_.refs_0_.refs_3_, bf16[12,128,128]{2,1,0:T(8,128)(2,1)S(1)} %collective-permute-done.8.refs_3_.refs_1_.refs_4_, ...), custom_call_target="tpu_custom_call" | custom-call | tf_op jit(solution)/shard_map/early/pallas_call | solution.py:309
  71.0 2.1 %collective-permute-done.18.refs_13_ = bf16[5,128,128]{2,1,0:T(8,128)(2,1)S(1)} collective-permute-done((bf16[5,128,128]{2,1,0:T(8,128)(2,1)S(1)}, bf16[5,128,128]{2,1,0:T(8,128)(2,1)S(1)}, u32[]{:S(2)}, u32[]{:S(2)}) %collective-permute-start.18) | collective-permute-done | bytes 163872 | tf_op jit(solution)/shard_map/ppermute | solution.py:48
  74.9 5.0 %product.1 = (bf16[14,128,128]{2,1,0:T(8,128)(2,1)S(1)}, bf16[16,128,128]{2,1,0:T(8,128)(2,1)S(1)}, f32[128,128]{1,0:T(8,128)S(1)}) custom-call(s32[4096]{0:T(1024)S(1)} %reshape.3.refs_0_, bf16[16,128,128]{2,1,0:T(8,128)(2,1)S(1)} %bitcast.3, f32[16,128,128]{2,1,0:T(8,128)S(1)} %early.1.refs_2_.base, ...), custom_call_target="tpu_custom_call" | custom-call | tf_op jit(solution)/shard_map/product/pallas_call | solution.py:309
  82.0 8.3 %collective-permute-done.25.refs_9_ = bf16[14,128,128]{2,1,0:T(8,128)(2,1)S(1)} collective-permute-done((bf16[14,128,128]{2,1,0:T(8,128)(2,1)S(1)}, bf16[14,128,128]{2,1,0:T(8,128)(2,1)S(1)}, u32[]{:S(2)}, u32[]{:S(2)}) %collective-permute-start.25) | collective-permute-done | bytes 458784 | tf_op jit(solution)/shard_map/ppermute | solution.py:67
  93.1 3.4 %collective-permute-done.26.refs_7_ = bf16[7,128,128]{2,1,0:T(8,128)(2,1)S(1)} collective-permute-done((bf16[7,128,128]{2,1,0:T(8,128)(2,1)S(1)}, bf16[7,128,128]{2,1,0:T(8,128)(2,1)S(1)}, u32[]{:S(2)}, u32[]{:S(2)}) %collective-permute-start.26) | collective-permute-done | bytes 229408 | tf_op jit(solution)/shard_map/ppermute | solution.py:67
  96.5 1.9 %collective-permute-done.23.refs_5_ = bf16[7,128,128]{2,1,0:T(8,128)(2,1)S(1)} collective-permute-done((bf16[7,128,128]{2,1,0:T(8,128)(2,1)S(1)}, bf16[7,128,128]{2,1,0:T(8,128)(2,1)S(1)}, u32[]{:S(2)}, u32[]{:S(2)}) %collective-permute-start.23) | collective-permute-done | bytes 229408 | tf_op jit(solution)/shard_map/ppermute | solution.py:67
  101.5 6.0 %collective-permute-start.29 = (bf16[4,128,128]{2,1,0:T(8,128)(2,1)S(1)}, bf16[4,128,128]{2,1,0:T(8,128)(2,1)S(1)}, u32[]{:S(2)}, u32[]{:S(2)}) collective-permute-start(bf16[4,128,128]{2,1,0:T(8,128)(2,1)S(1)} %get-tuple-element.61), channel_id=1, source_target_pairs={{0,28},{1,29},{2,30},{3,31},{4,0},{5,1},{6,2},{7,3},{8,4},{9,5},{1... | collective-permute-start | bytes 393224 | tf_op jit(solution)/shard_map/ppermute | solution.py:48
  107.5 4.1 %collective-permute-start.31 = (bf16[1,128,128]{2,1,0:T(8,128)(2,1)S(1)}, bf16[1,128,128]{2,1,0:T(8,128)(2,1)S(1)}, u32[]{:S(2)}, u32[]{:S(2)}) collective-permute-start(bf16[1,128,128]{2,1,0:T(8,128)(2,1)S(1)} %get-tuple-element.63), channel_id=1, source_target_pairs={{0,24},{1,25},{2,26},{3,27},{4,28},{5,29},{6,30},{7,31},{8,0},{9,1... | collective-permute-start | bytes 98312 | tf_op jit(solution)/shard_map/ppermute | solution.py:48
  113.5 1.9 %collective-permute-done.32.refs_3_ = bf16[2,128,128]{2,1,0:T(8,128)(2,1)S(1)} collective-permute-done((bf16[2,128,128]{2,1,0:T(8,128)(2,1)S(1)}, bf16[2,128,128]{2,1,0:T(8,128)(2,1)S(1)}, u32[]{:S(2)}, u32[]{:S(2)}) %collective-permute-start.32) | collective-permute-done | bytes 65568 | tf_op jit(solution)/shard_map/ppermute | solution.py:48
  116.4 1.8 %collective-permute-start.34 = (bf16[4,128,128]{2,1,0:T(8,128)(2,1)S(1)}, bf16[4,128,128]{2,1,0:T(8,128)(2,1)S(1)}, u32[]{:S(2)}, u32[]{:S(2)}) collective-permute-start(bf16[4,128,128]{2,1,0:T(8,128)(2,1)S(1)} %get-tuple-element.71), channel_id=1, source_target_pairs={{0,1},{1,2},{2,3},{3,4},{4,5},{5,6},{6,7},{7,8},{8,9},{9,10},{10,1... | collective-permute-start | bytes 393224 | tf_op jit(solution)/shard_map/ppermute | solution.py:48
  118.8 2.4 %collective-permute-done.33.refs_4_ = bf16[4,128,128]{2,1,0:T(8,128)(2,1)S(1)} collective-permute-done((bf16[4,128,128]{2,1,0:T(8,128)(2,1)S(1)}, bf16[4,128,128]{2,1,0:T(8,128)(2,1)S(1)}, u32[]{:S(2)}, u32[]{:S(2)}) %collective-permute-start.33) | collective-permute-done | bytes 131104 | tf_op jit(solution)/shard_map/ppermute | solution.py:48
  121.2 4.7 %collective-permute-done.34.refs_5_ = bf16[4,128,128]{2,1,0:T(8,128)(2,1)S(1)} collective-permute-done((bf16[4,128,128]{2,1,0:T(8,128)(2,1)S(1)}, bf16[4,128,128]{2,1,0:T(8,128)(2,1)S(1)}, u32[]{:S(2)}, u32[]{:S(2)}) %collective-permute-start.34) | collective-permute-done | bytes 131104 | tf_op jit(solution)/shard_map/ppermute | solution.py:48
  (69 shorter events, 26.5 us)
Async XLA Ops:
  1.5 8.8 %collective-permute-start.1 = (bf16[9,128,128]{2,1,0:T(8,128)(2,1)S(1)}, bf16[9,128,128]{2,1,0:T(8,128)(2,1)S(1)}, u32[]{:S(2)}, u32[]{:S(2)}) collective-permute-start(bf16[9,128,128]{2,1,0:T(8,128)(2,1)S(1)} %keep.1.refs_1_), channel_id=1, source_target_pairs={{0,64},{32,96},{64,128},{96,160},{128,192},{160,224},{192,0},{224,... | collective-permute-start | bytes 884744 | tf_op jit(solution)/shard_map/ppermute | solution.py:67
  3.1 9.9 %collective-permute-start.5 = (bf16[9,128,128]{2,1,0:T(8,128)(2,1)S(1)}, bf16[9,128,128]{2,1,0:T(8,128)(2,1)S(1)}, u32[]{:S(2)}, u32[]{:S(2)}) collective-permute-start(bf16[9,128,128]{2,1,0:T(8,128)(2,1)S(1)} %keep.1.refs_1_), channel_id=1, source_target_pairs={{0,192},{32,224},{64,0},{96,32},{128,64},{160,96},{192,128},{224,1... | collective-permute-start | bytes 884744 | tf_op jit(solution)/shard_map/ppermute | solution.py:67
  10.3 9.1 %collective-permute-start.3 = (bf16[9,128,128]{2,1,0:T(8,128)(2,1)S(1)}, bf16[9,128,128]{2,1,0:T(8,128)(2,1)S(1)}, u32[]{:S(2)}, u32[]{:S(2)}) collective-permute-start(bf16[9,128,128]{2,1,0:T(8,128)(2,1)S(1)} %keep.1.refs_1_), channel_id=1, source_target_pairs={{0,128},{32,160},{64,192},{96,224},{128,0},{160,32},{192,64},{224,... | collective-permute-start | bytes 884744 | tf_op jit(solution)/shard_map/ppermute | solution.py:67
  22.7 22.1 %collective-permute-start.9 = (bf16[11,128,128]{2,1,0:T(8,128)(2,1)S(1)}, bf16[11,128,128]{2,1,0:T(8,128)(2,1)S(1)}, u32[]{:S(2)}, u32[]{:S(2)}) collective-permute-start(bf16[11,128,128]{2,1,0:T(8,128)(2,1)S(1)} %get-tuple-element.42), channel_id=1, source_target_pairs={{0,30},{1,31},{2,0},{3,1},{4,2},{5,3},{6,4},{7,5},{8,6},{9,7},{10,... | collective-permute-start | bytes 1081352 | tf_op jit(solution)/shard_map/ppermute | solution.py:48
  31.5 8.9 %collective-permute-start.11 = (bf16[2,128,128]{2,1,0:T(8,128)(2,1)S(1)}, bf16[2,128,128]{2,1,0:T(8,128)(2,1)S(1)}, u32[]{:S(2)}, u32[]{:S(2)}) collective-permute-start(bf16[2,128,128]{2,1,0:T(8,128)(2,1)S(1)} %get-tuple-element.45), channel_id=1, source_target_pairs={{0,16},{1,17},{2,18},{3,19},{4,20},{5,21},{6,22},{7,23},{8,24},{9,... | collective-permute-start | bytes 196616 | tf_op jit(solution)/shard_map/ppermute | solution.py:48
  32.9 15.0 %collective-permute-start.10 = (bf16[11,128,128]{2,1,0:T(8,128)(2,1)S(1)}, bf16[11,128,128]{2,1,0:T(8,128)(2,1)S(1)}, u32[]{:S(2)}, u32[]{:S(2)}) collective-permute-start(bf16[11,128,128]{2,1,0:T(8,128)(2,1)S(1)} %get-tuple-element.43), channel_id=1, source_target_pairs={{0,2},{1,3},{2,4},{3,5},{4,6},{5,7},{6,8},{7,9},{8,10},{9,11},{10,... | collective-permute-start | bytes 1081352 | tf_op jit(solution)/shard_map/ppermute | solution.py:48
  40.4 14.3 %collective-permute-start.13 = (bf16[10,128,128]{2,1,0:T(8,128)(2,1)S(1)}, bf16[10,128,128]{2,1,0:T(8,128)(2,1)S(1)}, u32[]{:S(2)}, u32[]{:S(2)}) collective-permute-start(bf16[10,128,128]{2,1,0:T(8,128)(2,1)S(1)} %get-tuple-element.48), channel_id=1, source_target_pairs={{0,4},{1,5},{2,6},{3,7},{4,8},{5,9},{6,10},{7,11},{8,12},{9,13},{1... | collective-permute-start | bytes 983048 | tf_op jit(solution)/shard_map/ppermute | solution.py:48
  44.7 9.9 %collective-permute-start.12 = (bf16[9,128,128]{2,1,0:T(8,128)(2,1)S(1)}, bf16[9,128,128]{2,1,0:T(8,128)(2,1)S(1)}, u32[]{:S(2)}, u32[]{:S(2)}) collective-permute-start(bf16[9,128,128]{2,1,0:T(8,128)(2,1)S(1)} %get-tuple-element.46), channel_id=1, source_target_pairs={{0,28},{1,29},{2,30},{3,31},{4,0},{5,1},{6,2},{7,3},{8,4},{9,5},{1... | collective-permute-start | bytes 884744 | tf_op jit(solution)/shard_map/ppermute | solution.py:48
  44.7 15.9 %collective-permute-start.7 = (bf16[12,128,128]{2,1,0:T(8,128)(2,1)S(1)}, bf16[12,128,128]{2,1,0:T(8,128)(2,1)S(1)}, u32[]{:S(2)}, u32[]{:S(2)}) collective-permute-start(bf16[12,128,128]{2,1,0:T(8,128)(2,1)S(1)} %get-tuple-element.40), channel_id=1, source_target_pairs={{0,31},{1,0},{2,1},{3,2},{4,3},{5,4},{6,5},{7,6},{8,7},{9,8},{10,9... | collective-permute-start | bytes 1179656 | tf_op jit(solution)/shard_map/ppermute | solution.py:48
  44.7 21.7 %collective-permute-start.8 = (bf16[12,128,128]{2,1,0:T(8,128)(2,1)S(1)}, bf16[12,128,128]{2,1,0:T(8,128)(2,1)S(1)}, u32[]{:S(2)}, u32[]{:S(2)}) collective-permute-start(bf16[12,128,128]{2,1,0:T(8,128)(2,1)S(1)} %get-tuple-element.41), channel_id=1, source_target_pairs={{0,1},{1,2},{2,3},{3,4},{4,5},{5,6},{6,7},{7,8},{8,9},{9,10},{10,1... | collective-permute-start | bytes 1179656 | tf_op jit(solution)/shard_map/ppermute | solution.py:48
  54.7 20.2 %collective-permute-start.16 = (bf16[10,128,128]{2,1,0:T(8,128)(2,1)S(1)}, bf16[10,128,128]{2,1,0:T(8,128)(2,1)S(1)}, u32[]{:S(2)}, u32[]{:S(2)}) collective-permute-start(bf16[10,128,128]{2,1,0:T(8,128)(2,1)S(1)} %get-tuple-element.54), channel_id=1, source_target_pairs={{0,29},{1,30},{2,31},{3,0},{4,1},{5,2},{6,3},{7,4},{8,5},{9,6},{10... | collective-permute-start | bytes 983048 | tf_op jit(solution)/shard_map/ppermute | solution.py:48
  54.8 20.1 %collective-permute-start.17 = (bf16[10,128,128]{2,1,0:T(8,128)(2,1)S(1)}, bf16[10,128,128]{2,1,0:T(8,128)(2,1)S(1)}, u32[]{:S(2)}, u32[]{:S(2)}) collective-permute-start(bf16[10,128,128]{2,1,0:T(8,128)(2,1)S(1)} %get-tuple-element.55), channel_id=1, source_target_pairs={{0,3},{1,4},{2,5},{3,6},{4,7},{5,8},{6,9},{7,10},{8,11},{9,12},{10... | collective-permute-start | bytes 983048 | tf_op jit(solution)/shard_map/ppermute | solution.py:48
  58.1 8.5 %collective-permute-start.19 = (bf16[4,128,128]{2,1,0:T(8,128)(2,1)S(1)}, bf16[4,128,128]{2,1,0:T(8,128)(2,1)S(1)}, u32[]{:S(2)}, u32[]{:S(2)}) collective-permute-start(bf16[4,128,128]{2,1,0:T(8,128)(2,1)S(1)} %get-tuple-element.57), channel_id=1, source_target_pairs={{0,4},{1,5},{2,6},{3,7},{4,8},{5,9},{6,10},{7,11},{8,12},{9,13},{1... | collective-permute-start | bytes 393224 | tf_op jit(solution)/shard_map/ppermute | solution.py:48
  60.7 12.5 %collective-permute-start.18 = (bf16[5,128,128]{2,1,0:T(8,128)(2,1)S(1)}, bf16[5,128,128]{2,1,0:T(8,128)(2,1)S(1)}, u32[]{:S(2)}, u32[]{:S(2)}) collective-permute-start(bf16[5,128,128]{2,1,0:T(8,128)(2,1)S(1)} %get-tuple-element.56), channel_id=1, source_target_pairs={{0,28},{1,29},{2,30},{3,31},{4,0},{5,1},{6,2},{7,3},{8,4},{9,5},{1... | collective-permute-start | bytes 491528 | tf_op jit(solution)/shard_map/ppermute | solution.py:48
  66.5 8.4 %collective-permute-start.14 = (bf16[5,128,128]{2,1,0:T(8,128)(2,1)S(1)}, bf16[5,128,128]{2,1,0:T(8,128)(2,1)S(1)}, u32[]{:S(2)}, u32[]{:S(2)}) collective-permute-start(bf16[5,128,128]{2,1,0:T(8,128)(2,1)S(1)} %get-tuple-element.49), channel_id=1, source_target_pairs={{0,28},{1,29},{2,30},{3,31},{4,0},{5,1},{6,2},{7,3},{8,4},{9,5},{1... | collective-permute-start | bytes 491528 | tf_op jit(solution)/shard_map/ppermute | solution.py:48
  66.6 8.3 %collective-permute-start.15 = (bf16[5,128,128]{2,1,0:T(8,128)(2,1)S(1)}, bf16[5,128,128]{2,1,0:T(8,128)(2,1)S(1)}, u32[]{:S(2)}, u32[]{:S(2)}) collective-permute-start(bf16[5,128,128]{2,1,0:T(8,128)(2,1)S(1)} %get-tuple-element.50), channel_id=1, source_target_pairs={{0,4},{1,5},{2,6},{3,7},{4,8},{5,9},{6,10},{7,11},{8,12},{9,13},{1... | collective-permute-start | bytes 491528 | tf_op jit(solution)/shard_map/ppermute | solution.py:48
  79.9 10.4 %collective-permute-start.25 = (bf16[14,128,128]{2,1,0:T(8,128)(2,1)S(1)}, bf16[14,128,128]{2,1,0:T(8,128)(2,1)S(1)}, u32[]{:S(2)}, u32[]{:S(2)}) collective-permute-start(bf16[14,128,128]{2,1,0:T(8,128)(2,1)S(1)} %get-tuple-element.60.refs_1_), channel_id=1, source_target_pairs={{0,192},{32,224},{64,0},{96,32},{128,64},{160,96},{192,128},{224,1... | collective-permute-start | bytes 1376264 | tf_op jit(solution)/shard_map/ppermute | solution.py:67
  81.6 10.3 %collective-permute-start.21 = (bf16[14,128,128]{2,1,0:T(8,128)(2,1)S(1)}, bf16[14,128,128]{2,1,0:T(8,128)(2,1)S(1)}, u32[]{:S(2)}, u32[]{:S(2)}) collective-permute-start(bf16[14,128,128]{2,1,0:T(8,128)(2,1)S(1)} %get-tuple-element.60.refs_1_), channel_id=1, source_target_pairs={{0,64},{32,96},{64,128},{96,160},{128,192},{160,224},{192,0},{224,... | collective-permute-start | bytes 1376264 | tf_op jit(solution)/shard_map/ppermute | solution.py:67
  82.0 16.4 %collective-permute-start.20 = (bf16[14,128,128]{2,1,0:T(8,128)(2,1)S(1)}, bf16[14,128,128]{2,1,0:T(8,128)(2,1)S(1)}, u32[]{:S(2)}, u32[]{:S(2)}) collective-permute-start(bf16[14,128,128]{2,1,0:T(8,128)(2,1)S(1)} %get-tuple-element.60.refs_1_), channel_id=1, source_target_pairs={{0,32},{32,0},{64,96},{96,64},{128,160},{160,128},{192,224},{224,1... | collective-permute-start | bytes 1376264 | tf_op jit(solution)/shard_map/ppermute | solution.py:71
  101.5 13.9 %collective-permute-start.29 = (bf16[4,128,128]{2,1,0:T(8,128)(2,1)S(1)}, bf16[4,128,128]{2,1,0:T(8,128)(2,1)S(1)}, u32[]{:S(2)}, u32[]{:S(2)}) collective-permute-start(bf16[4,128,128]{2,1,0:T(8,128)(2,1)S(1)} %get-tuple-element.61), channel_id=1, source_target_pairs={{0,28},{1,29},{2,30},{3,31},{4,0},{5,1},{6,2},{7,3},{8,4},{9,5},{1... | collective-permute-start | bytes 393224 | tf_op jit(solution)/shard_map/ppermute | solution.py:48
  107.5 8.6 %collective-permute-start.30 = (bf16[4,128,128]{2,1,0:T(8,128)(2,1)S(1)}, bf16[4,128,128]{2,1,0:T(8,128)(2,1)S(1)}, u32[]{:S(2)}, u32[]{:S(2)}) collective-permute-start(bf16[4,128,128]{2,1,0:T(8,128)(2,1)S(1)} %get-tuple-element.62), channel_id=1, source_target_pairs={{0,4},{1,5},{2,6},{3,7},{4,8},{5,9},{6,10},{7,11},{8,12},{9,13},{1... | collective-permute-start | bytes 393224 | tf_op jit(solution)/shard_map/ppermute | solution.py:48
  107.5 7.9 %collective-permute-start.32 = (bf16[2,128,128]{2,1,0:T(8,128)(2,1)S(1)}, bf16[2,128,128]{2,1,0:T(8,128)(2,1)S(1)}, u32[]{:S(2)}, u32[]{:S(2)}) collective-permute-start(bf16[2,128,128]{2,1,0:T(8,128)(2,1)S(1)} %get-tuple-element.64), channel_id=1, source_target_pairs={{0,8},{1,9},{2,10},{3,11},{4,12},{5,13},{6,14},{7,15},{8,16},{9,17... | collective-permute-start | bytes 196616 | tf_op jit(solution)/shard_map/ppermute | solution.py:48
  116.4 9.5 %collective-permute-start.34 = (bf16[4,128,128]{2,1,0:T(8,128)(2,1)S(1)}, bf16[4,128,128]{2,1,0:T(8,128)(2,1)S(1)}, u32[]{:S(2)}, u32[]{:S(2)}) collective-permute-start(bf16[4,128,128]{2,1,0:T(8,128)(2,1)S(1)} %get-tuple-element.71), channel_id=1, source_target_pairs={{0,1},{1,2},{2,3},{3,4},{4,5},{5,6},{6,7},{7,8},{8,9},{9,10},{10,1... | collective-permute-start | bytes 393224 | tf_op jit(solution)/shard_map/ppermute | solution.py:48
  118.2 7.9 %collective-permute-start.35 = (bf16[4,128,128]{2,1,0:T(8,128)(2,1)S(1)}, bf16[4,128,128]{2,1,0:T(8,128)(2,1)S(1)}, u32[]{:S(2)}, u32[]{:S(2)}) collective-permute-start(bf16[4,128,128]{2,1,0:T(8,128)(2,1)S(1)} %get-tuple-element.72), channel_id=1, source_target_pairs={{0,30},{1,31},{2,0},{3,1},{4,2},{5,3},{6,4},{7,5},{8,6},{9,7},{10,... | collective-permute-start | bytes 393224 | tf_op jit(solution)/shard_map/ppermute | solution.py:48
  (15 other events, 92.7 us)

commit v8 on v7

--- a/solution.py
+++ b/solution.py
@@ -11,7 +11,7 @@
 FIRST = {1: [1, 5], -1: [-1, -5], 2: [2, 6], -2: [-2, -6], 4: [4, 7], -4: [-4, -7]}
 THEN = [({4: [5], -4: [-5]}, (1, -1)), ({3: [3, 7], -3: [-3, -7]}, (4, -4)), ({4: [6], -4: [-6]}, (2, -2))]
 LONG = {4: [4, 5, 3, 6], -4: [-4, -3, -5, -2], 8: [7], -8: [-7, -6]}
-SHORT = [1, -1, 2]
+SHORT = [2, 1, -1]
 
 
 class Plan:

time: 128 us -> 128 us (level)
  transfers between devices with their start and end apart: 36 -> 36, of which waited for: 19 -> 19; matrix products, arithmetic and copies ran while one was open for 0% -> 0% of each run, Pallas kernels for 2% -> 3%
where the time goes in v8:
time: 128 us; the launch traced here: 127 us
  waiting for transfers between devices  60.5 us (47%)
  starting transfers between devices  52.4 us (41%)
  Pallas kernels  13 us (10%)
  local copies, waits for them, and re-layouts  1.28 us (1%)
    ppermute x20, starting transfers between devices, shifted(): lax.ppermute(value, 'col', [(i, (i + by) % length) for i in range(length)])  42.3 us
    ppermute x20, waiting for transfers between devices, shifted(): lax.ppermute(value, 'col', [(i, (i + by) % length) for i in range(length)])  31.1 us
    ppermute x7, waiting for transfers between devices, from_chip(): return lax.ppermute(block, 'row', pairs)  26.6 us
    pallas_call x11, Pallas kernels, call(): pl.pallas_call(kernel, out_shape=[jax.ShapeDtypeStruct(shape, dtype) for...  13 us
    ppermute x7, starting transfers between devices, from_chip(): return lax.ppermute(block, 'row', pairs)  9.04 us
    ppermute x9, waiting for transfers between devices, from_core(): lax.ppermute(block, 'row', [(i, i ^ 1) for i in range(lax.axis_size('row'...  2.83 us
  transfers between devices with their start and end apart: 36, of which 19 were waited for; matrix products, arithmetic and copies ran while one was open for 0% of the time, Pallas kernels for 3%

profile of v8, /device:TPU:2, one launch (start us, length us, event | category | flops | bytes accessed | tf_op | source)
XLA Modules:
  0.0 127.3 jit_solution(17805929709018413651)
XLA Ops:
  4.0 6.4 %collective-permute-done.1.refs_3_ = bf16[9,128,128]{2,1,0:T(8,128)(2,1)S(1)} collective-permute-done((bf16[9,128,128]{2,1,0:T(8,128)(2,1)S(1)}, bf16[9,128,128]{2,1,0:T(8,128)(2,1)S(1)}, u32[]{:S(2)}, u32[]{:S(2)}) %collective-permute-start.1) | collective-permute-done | bytes 294944 | tf_op jit(solution)/shard_map/ppermute | solution.py:67
  10.3 2.1 %collective-permute-start.3 = (bf16[9,128,128]{2,1,0:T(8,128)(2,1)S(1)}, bf16[9,128,128]{2,1,0:T(8,128)(2,1)S(1)}, u32[]{:S(2)}, u32[]{:S(2)}) collective-permute-start(bf16[9,128,128]{2,1,0:T(8,128)(2,1)S(1)} %keep.1.refs_1_), channel_id=1, source_target_pairs={{0,128},{32,160},{64,192},{96,224},{128,0},{160,32},{192,64},{224,... | collective-permute-start | bytes 884744 | tf_op jit(solution)/shard_map/ppermute | solution.py:67
  13.0 6.5 %collective-permute-done.3.refs_5_ = bf16[9,128,128]{2,1,0:T(8,128)(2,1)S(1)} collective-permute-done((bf16[9,128,128]{2,1,0:T(8,128)(2,1)S(1)}, bf16[9,128,128]{2,1,0:T(8,128)(2,1)S(1)}, u32[]{:S(2)}, u32[]{:S(2)}) %collective-permute-start.3) | collective-permute-done | bytes 294944 | tf_op jit(solution)/shard_map/ppermute | solution.py:67
  22.7 8.8 %collective-permute-start.9 = (bf16[11,128,128]{2,1,0:T(8,128)(2,1)S(1)}, bf16[11,128,128]{2,1,0:T(8,128)(2,1)S(1)}, u32[]{:S(2)}, u32[]{:S(2)}) collective-permute-start(bf16[11,128,128]{2,1,0:T(8,128)(2,1)S(1)} %get-tuple-element.42), channel_id=1, source_target_pairs={{0,30},{1,31},{2,0},{3,1},{4,2},{5,3},{6,4},{7,5},{8,6},{9,7},{10,... | collective-permute-start | bytes 1081352 | tf_op jit(solution)/shard_map/ppermute | solution.py:48
  33.7 6.7 %collective-permute-done.11.refs_15_.far = bf16[2,128,128]{2,1,0:T(8,128)(2,1)S(1)} collective-permute-done((bf16[2,128,128]{2,1,0:T(8,128)(2,1)S(1)}, bf16[2,128,128]{2,1,0:T(8,128)(2,1)S(1)}, u32[]{:S(2)}, u32[]{:S(2)}) %collective-permute-start.11) | collective-permute-done | bytes 65568 | tf_op jit(solution)/shard_map/ppermute | solution.py:48
  40.4 4.3 %collective-permute-start.13 = (bf16[10,128,128]{2,1,0:T(8,128)(2,1)S(1)}, bf16[10,128,128]{2,1,0:T(8,128)(2,1)S(1)}, u32[]{:S(2)}, u32[]{:S(2)}) collective-permute-start(bf16[10,128,128]{2,1,0:T(8,128)(2,1)S(1)} %get-tuple-element.48), channel_id=1, source_target_pairs={{0,4},{1,5},{2,6},{3,7},{4,8},{5,9},{6,10},{7,11},{8,12},{9,13},{1... | collective-permute-start | bytes 983048 | tf_op jit(solution)/shard_map/ppermute | solution.py:48
  44.7 2.0 %collective-permute-start.8 = (bf16[12,128,128]{2,1,0:T(8,128)(2,1)S(1)}, bf16[12,128,128]{2,1,0:T(8,128)(2,1)S(1)}, u32[]{:S(2)}, u32[]{:S(2)}) collective-permute-start(bf16[12,128,128]{2,1,0:T(8,128)(2,1)S(1)} %get-tuple-element.41), channel_id=1, source_target_pairs={{0,1},{1,2},{2,3},{3,4},{4,5},{5,6},{6,7},{7,8},{8,9},{9,10},{10,1... | collective-permute-start | bytes 1179656 | tf_op jit(solution)/shard_map/ppermute | solution.py:48
  47.9 6.8 %collective-permute-done.12.refs_6_.refs_0_.refs_7_ = bf16[9,128,128]{2,1,0:T(8,128)(2,1)S(1)} collective-permute-done((bf16[9,128,128]{2,1,0:T(8,128)(2,1)S(1)}, bf16[9,128,128]{2,1,0:T(8,128)(2,1)S(1)}, u32[]{:S(2)}, u32[]{:S(2)}) %collective-permute-start.12) | collective-permute-done | bytes 294944 | tf_op jit(solution)/shard_map/ppermute | solution.py:48
  54.8 3.2 %collective-permute-start.17 = (bf16[10,128,128]{2,1,0:T(8,128)(2,1)S(1)}, bf16[10,128,128]{2,1,0:T(8,128)(2,1)S(1)}, u32[]{:S(2)}, u32[]{:S(2)}) collective-permute-start(bf16[10,128,128]{2,1,0:T(8,128)(2,1)S(1)} %get-tuple-element.55), channel_id=1, source_target_pairs={{0,3},{1,4},{2,5},{3,6},{4,7},{5,8},{6,9},{7,10},{8,11},{9,12},{10... | collective-permute-start | bytes 983048 | tf_op jit(solution)/shard_map/ppermute | solution.py:48
  58.1 1.8 %collective-permute-start.19 = (bf16[4,128,128]{2,1,0:T(8,128)(2,1)S(1)}, bf16[4,128,128]{2,1,0:T(8,128)(2,1)S(1)}, u32[]{:S(2)}, u32[]{:S(2)}) collective-permute-start(bf16[4,128,128]{2,1,0:T(8,128)(2,1)S(1)} %get-tuple-element.57), channel_id=1, source_target_pairs={{0,4},{1,5},{2,6},{3,7},{4,8},{5,9},{6,10},{7,11},{8,12},{9,13},{1... | collective-permute-start | bytes 393224 | tf_op jit(solution)/shard_map/ppermute | solution.py:48
  60.7 5.8 %collective-permute-start.18 = (bf16[5,128,128]{2,1,0:T(8,128)(2,1)S(1)}, bf16[5,128,128]{2,1,0:T(8,128)(2,1)S(1)}, u32[]{:S(2)}, u32[]{:S(2)}) collective-permute-start(bf16[5,128,128]{2,1,0:T(8,128)(2,1)S(1)} %get-tuple-element.56), channel_id=1, source_target_pairs={{0,28},{1,29},{2,30},{3,31},{4,0},{5,1},{6,2},{7,3},{8,4},{9,5},{1... | collective-permute-start | bytes 491528 | tf_op jit(solution)/shard_map/ppermute | solution.py:48
  66.6 2.0 %collective-permute-start.15 = (bf16[5,128,128]{2,1,0:T(8,128)(2,1)S(1)}, bf16[5,128,128]{2,1,0:T(8,128)(2,1)S(1)}, u32[]{:S(2)}, u32[]{:S(2)}) collective-permute-start(bf16[5,128,128]{2,1,0:T(8,128)(2,1)S(1)} %get-tuple-element.50), channel_id=1, source_target_pairs={{0,4},{1,5},{2,6},{3,7},{4,8},{5,9},{6,10},{7,11},{8,12},{9,13},{1... | collective-permute-start | bytes 491528 | tf_op jit(solution)/shard_map/ppermute | solution.py:48
  68.6 2.8 %early.1.refs_2_.base = f32[16,128,128]{2,1,0:T(8,128)S(1)} custom-call(s32[4096]{0:T(1024)S(1)} %reshape.3.refs_0_, bf16[16,128,128]{2,1,0:T(8,128)(2,1)S(1)} %bitcast.2, bf16[12,128,128]{2,1,0:T(8,128)(2,1)S(1)} %collective-permute-done.7.refs_2_.refs_0_.refs_3_, bf16[12,128,128]{2,1,0:T(8,128)(2,1)S(1)} %collective-permute-done.8.refs_3_.refs_1_.refs_4_, ...), custom_call_target="tpu_custom_call" | custom-call | tf_op jit(solution)/shard_map/early/pallas_call | solution.py:309
  74.9 4.7 %product.1 = (bf16[14,128,128]{2,1,0:T(8,128)(2,1)S(1)}, bf16[16,128,128]{2,1,0:T(8,128)(2,1)S(1)}, f32[128,128]{1,0:T(8,128)S(1)}) custom-call(s32[4096]{0:T(1024)S(1)} %reshape.3.refs_0_, bf16[16,128,128]{2,1,0:T(8,128)(2,1)S(1)} %bitcast.3, f32[16,128,128]{2,1,0:T(8,128)S(1)} %early.1.refs_2_.base, ...), custom_call_target="tpu_custom_call" | custom-call | tf_op jit(solution)/shard_map/product/pallas_call | solution.py:309
  79.6 2.3 %collective-permute-start.25 = (bf16[14,128,128]{2,1,0:T(8,128)(2,1)S(1)}, bf16[14,128,128]{2,1,0:T(8,128)(2,1)S(1)}, u32[]{:S(2)}, u32[]{:S(2)}) collective-permute-start(bf16[14,128,128]{2,1,0:T(8,128)(2,1)S(1)} %get-tuple-element.60.refs_1_), channel_id=1, source_target_pairs={{0,192},{32,224},{64,0},{96,32},{128,64},{160,96},{192,128},{224,1... | collective-permute-start | bytes 1376264 | tf_op jit(solution)/shard_map/ppermute | solution.py:67
  81.9 9.6 %collective-permute-done.25.refs_9_ = bf16[14,128,128]{2,1,0:T(8,128)(2,1)S(1)} collective-permute-done((bf16[14,128,128]{2,1,0:T(8,128)(2,1)S(1)}, bf16[14,128,128]{2,1,0:T(8,128)(2,1)S(1)}, u32[]{:S(2)}, u32[]{:S(2)}) %collective-permute-start.25) | collective-permute-done | bytes 458784 | tf_op jit(solution)/shard_map/ppermute | solution.py:67
  94.3 3.4 %collective-permute-done.26.refs_7_ = bf16[7,128,128]{2,1,0:T(8,128)(2,1)S(1)} collective-permute-done((bf16[7,128,128]{2,1,0:T(8,128)(2,1)S(1)}, bf16[7,128,128]{2,1,0:T(8,128)(2,1)S(1)}, u32[]{:S(2)}, u32[]{:S(2)}) %collective-permute-start.26) | collective-permute-done | bytes 229408 | tf_op jit(solution)/shard_map/ppermute | solution.py:67
  101.5 3.4 %collective-permute-start.29 = (bf16[4,128,128]{2,1,0:T(8,128)(2,1)S(1)}, bf16[4,128,128]{2,1,0:T(8,128)(2,1)S(1)}, u32[]{:S(2)}, u32[]{:S(2)}) collective-permute-start(bf16[4,128,128]{2,1,0:T(8,128)(2,1)S(1)} %get-tuple-element.61), channel_id=1, source_target_pairs={{0,28},{1,29},{2,30},{3,31},{4,0},{5,1},{6,2},{7,3},{8,4},{9,5},{1... | collective-permute-start | bytes 393224 | tf_op jit(solution)/shard_map/ppermute | solution.py:48
  106.7 2.4 %collective-permute-start.31 = (bf16[1,128,128]{2,1,0:T(8,128)(2,1)S(1)}, bf16[1,128,128]{2,1,0:T(8,128)(2,1)S(1)}, u32[]{:S(2)}, u32[]{:S(2)}) collective-permute-start(bf16[1,128,128]{2,1,0:T(8,128)(2,1)S(1)} %get-tuple-element.63), channel_id=1, source_target_pairs={{0,24},{1,25},{2,26},{3,27},{4,28},{5,29},{6,30},{7,31},{8,0},{9,1... | collective-permute-start | bytes 98312 | tf_op jit(solution)/shard_map/ppermute | solution.py:48
  109.1 2.4 %collective-permute-done.31.refs_2_ = bf16[1,128,128]{2,1,0:T(8,128)(2,1)S(1)} collective-permute-done((bf16[1,128,128]{2,1,0:T(8,128)(2,1)S(1)}, bf16[1,128,128]{2,1,0:T(8,128)(2,1)S(1)}, u32[]{:S(2)}, u32[]{:S(2)}) %collective-permute-start.31) | collective-permute-done | bytes 32800 | tf_op jit(solution)/shard_map/ppermute | solution.py:48
  111.5 2.7 %collective-permute-done.32.refs_3_ = bf16[2,128,128]{2,1,0:T(8,128)(2,1)S(1)} collective-permute-done((bf16[2,128,128]{2,1,0:T(8,128)(2,1)S(1)}, bf16[2,128,128]{2,1,0:T(8,128)(2,1)S(1)}, u32[]{:S(2)}, u32[]{:S(2)}) %collective-permute-start.32) | collective-permute-done | bytes 65568 | tf_op jit(solution)/shard_map/ppermute | solution.py:48
  114.4 3.4 %collective-permute-start.34 = (bf16[4,128,128]{2,1,0:T(8,128)(2,1)S(1)}, bf16[4,128,128]{2,1,0:T(8,128)(2,1)S(1)}, u32[]{:S(2)}, u32[]{:S(2)}) collective-permute-start(bf16[4,128,128]{2,1,0:T(8,128)(2,1)S(1)} %get-tuple-element.71), channel_id=1, source_target_pairs={{0,31},{1,0},{2,1},{3,2},{4,3},{5,4},{6,5},{7,6},{8,7},{9,8},{10,9... | collective-permute-start | bytes 393224 | tf_op jit(solution)/shard_map/ppermute | solution.py:48
  119.1 2.6 %collective-permute-done.33.refs_4_ = bf16[4,128,128]{2,1,0:T(8,128)(2,1)S(1)} collective-permute-done((bf16[4,128,128]{2,1,0:T(8,128)(2,1)S(1)}, bf16[4,128,128]{2,1,0:T(8,128)(2,1)S(1)}, u32[]{:S(2)}, u32[]{:S(2)}) %collective-permute-start.33) | collective-permute-done | bytes 131104 | tf_op jit(solution)/shard_map/ppermute | solution.py:48
  122.8 3.3 %collective-permute-done.35.refs_6_ = bf16[4,128,128]{2,1,0:T(8,128)(2,1)S(1)} collective-permute-done((bf16[4,128,128]{2,1,0:T(8,128)(2,1)S(1)}, bf16[4,128,128]{2,1,0:T(8,128)(2,1)S(1)}, u32[]{:S(2)}, u32[]{:S(2)}) %collective-permute-start.35) | collective-permute-done | bytes 131104 | tf_op jit(solution)/shard_map/ppermute | solution.py:48
  (69 shorter events, 27.6 us)
Async XLA Ops:
  1.5 8.8 %collective-permute-start.1 = (bf16[9,128,128]{2,1,0:T(8,128)(2,1)S(1)}, bf16[9,128,128]{2,1,0:T(8,128)(2,1)S(1)}, u32[]{:S(2)}, u32[]{:S(2)}) collective-permute-start(bf16[9,128,128]{2,1,0:T(8,128)(2,1)S(1)} %keep.1.refs_1_), channel_id=1, source_target_pairs={{0,64},{32,96},{64,128},{96,160},{128,192},{160,224},{192,0},{224,... | collective-permute-start | bytes 884744 | tf_op jit(solution)/shard_map/ppermute | solution.py:67
  3.1 9.9 %collective-permute-start.5 = (bf16[9,128,128]{2,1,0:T(8,128)(2,1)S(1)}, bf16[9,128,128]{2,1,0:T(8,128)(2,1)S(1)}, u32[]{:S(2)}, u32[]{:S(2)}) collective-permute-start(bf16[9,128,128]{2,1,0:T(8,128)(2,1)S(1)} %keep.1.refs_1_), channel_id=1, source_target_pairs={{0,192},{32,224},{64,0},{96,32},{128,64},{160,96},{192,128},{224,1... | collective-permute-start | bytes 884744 | tf_op jit(solution)/shard_map/ppermute | solution.py:67
  10.3 9.1 %collective-permute-start.3 = (bf16[9,128,128]{2,1,0:T(8,128)(2,1)S(1)}, bf16[9,128,128]{2,1,0:T(8,128)(2,1)S(1)}, u32[]{:S(2)}, u32[]{:S(2)}) collective-permute-start(bf16[9,128,128]{2,1,0:T(8,128)(2,1)S(1)} %keep.1.refs_1_), channel_id=1, source_target_pairs={{0,128},{32,160},{64,192},{96,224},{128,0},{160,32},{192,64},{224,... | collective-permute-start | bytes 884744 | tf_op jit(solution)/shard_map/ppermute | solution.py:67
  22.7 22.1 %collective-permute-start.9 = (bf16[11,128,128]{2,1,0:T(8,128)(2,1)S(1)}, bf16[11,128,128]{2,1,0:T(8,128)(2,1)S(1)}, u32[]{:S(2)}, u32[]{:S(2)}) collective-permute-start(bf16[11,128,128]{2,1,0:T(8,128)(2,1)S(1)} %get-tuple-element.42), channel_id=1, source_target_pairs={{0,30},{1,31},{2,0},{3,1},{4,2},{5,3},{6,4},{7,5},{8,6},{9,7},{10,... | collective-permute-start | bytes 1081352 | tf_op jit(solution)/shard_map/ppermute | solution.py:48
  31.5 8.9 %collective-permute-start.11 = (bf16[2,128,128]{2,1,0:T(8,128)(2,1)S(1)}, bf16[2,128,128]{2,1,0:T(8,128)(2,1)S(1)}, u32[]{:S(2)}, u32[]{:S(2)}) collective-permute-start(bf16[2,128,128]{2,1,0:T(8,128)(2,1)S(1)} %get-tuple-element.45), channel_id=1, source_target_pairs={{0,16},{1,17},{2,18},{3,19},{4,20},{5,21},{6,22},{7,23},{8,24},{9,... | collective-permute-start | bytes 196616 | tf_op jit(solution)/shard_map/ppermute | solution.py:48
  32.9 15.0 %collective-permute-start.10 = (bf16[11,128,128]{2,1,0:T(8,128)(2,1)S(1)}, bf16[11,128,128]{2,1,0:T(8,128)(2,1)S(1)}, u32[]{:S(2)}, u32[]{:S(2)}) collective-permute-start(bf16[11,128,128]{2,1,0:T(8,128)(2,1)S(1)} %get-tuple-element.43), channel_id=1, source_target_pairs={{0,2},{1,3},{2,4},{3,5},{4,6},{5,7},{6,8},{7,9},{8,10},{9,11},{10,... | collective-permute-start | bytes 1081352 | tf_op jit(solution)/shard_map/ppermute | solution.py:48
  40.4 14.3 %collective-permute-start.13 = (bf16[10,128,128]{2,1,0:T(8,128)(2,1)S(1)}, bf16[10,128,128]{2,1,0:T(8,128)(2,1)S(1)}, u32[]{:S(2)}, u32[]{:S(2)}) collective-permute-start(bf16[10,128,128]{2,1,0:T(8,128)(2,1)S(1)} %get-tuple-element.48), channel_id=1, source_target_pairs={{0,4},{1,5},{2,6},{3,7},{4,8},{5,9},{6,10},{7,11},{8,12},{9,13},{1... | collective-permute-start | bytes 983048 | tf_op jit(solution)/shard_map/ppermute | solution.py:48
  44.7 9.9 %collective-permute-start.12 = (bf16[9,128,128]{2,1,0:T(8,128)(2,1)S(1)}, bf16[9,128,128]{2,1,0:T(8,128)(2,1)S(1)}, u32[]{:S(2)}, u32[]{:S(2)}) collective-permute-start(bf16[9,128,128]{2,1,0:T(8,128)(2,1)S(1)} %get-tuple-element.46), channel_id=1, source_target_pairs={{0,28},{1,29},{2,30},{3,31},{4,0},{5,1},{6,2},{7,3},{8,4},{9,5},{1... | collective-permute-start | bytes 884744 | tf_op jit(solution)/shard_map/ppermute | solution.py:48
  44.7 15.9 %collective-permute-start.7 = (bf16[12,128,128]{2,1,0:T(8,128)(2,1)S(1)}, bf16[12,128,128]{2,1,0:T(8,128)(2,1)S(1)}, u32[]{:S(2)}, u32[]{:S(2)}) collective-permute-start(bf16[12,128,128]{2,1,0:T(8,128)(2,1)S(1)} %get-tuple-element.40), channel_id=1, source_target_pairs={{0,31},{1,0},{2,1},{3,2},{4,3},{5,4},{6,5},{7,6},{8,7},{9,8},{10,9... | collective-permute-start | bytes 1179656 | tf_op jit(solution)/shard_map/ppermute | solution.py:48
  44.7 21.7 %collective-permute-start.8 = (bf16[12,128,128]{2,1,0:T(8,128)(2,1)S(1)}, bf16[12,128,128]{2,1,0:T(8,128)(2,1)S(1)}, u32[]{:S(2)}, u32[]{:S(2)}) collective-permute-start(bf16[12,128,128]{2,1,0:T(8,128)(2,1)S(1)} %get-tuple-element.41), channel_id=1, source_target_pairs={{0,1},{1,2},{2,3},{3,4},{4,5},{5,6},{6,7},{7,8},{8,9},{9,10},{10,1... | collective-permute-start | bytes 1179656 | tf_op jit(solution)/shard_map/ppermute | solution.py:48
  54.7 20.2 %collective-permute-start.16 = (bf16[10,128,128]{2,1,0:T(8,128)(2,1)S(1)}, bf16[10,128,128]{2,1,0:T(8,128)(2,1)S(1)}, u32[]{:S(2)}, u32[]{:S(2)}) collective-permute-start(bf16[10,128,128]{2,1,0:T(8,128)(2,1)S(1)} %get-tuple-element.54), channel_id=1, source_target_pairs={{0,29},{1,30},{2,31},{3,0},{4,1},{5,2},{6,3},{7,4},{8,5},{9,6},{10... | collective-permute-start | bytes 983048 | tf_op jit(solution)/shard_map/ppermute | solution.py:48
  54.8 20.1 %collective-permute-start.17 = (bf16[10,128,128]{2,1,0:T(8,128)(2,1)S(1)}, bf16[10,128,128]{2,1,0:T(8,128)(2,1)S(1)}, u32[]{:S(2)}, u32[]{:S(2)}) collective-permute-start(bf16[10,128,128]{2,1,0:T(8,128)(2,1)S(1)} %get-tuple-element.55), channel_id=1, source_target_pairs={{0,3},{1,4},{2,5},{3,6},{4,7},{5,8},{6,9},{7,10},{8,11},{9,12},{10... | collective-permute-start | bytes 983048 | tf_op jit(solution)/shard_map/ppermute | solution.py:48
  58.1 8.5 %collective-permute-start.19 = (bf16[4,128,128]{2,1,0:T(8,128)(2,1)S(1)}, bf16[4,128,128]{2,1,0:T(8,128)(2,1)S(1)}, u32[]{:S(2)}, u32[]{:S(2)}) collective-permute-start(bf16[4,128,128]{2,1,0:T(8,128)(2,1)S(1)} %get-tuple-element.57), channel_id=1, source_target_pairs={{0,4},{1,5},{2,6},{3,7},{4,8},{5,9},{6,10},{7,11},{8,12},{9,13},{1... | collective-permute-start | bytes 393224 | tf_op jit(solution)/shard_map/ppermute | solution.py:48
  60.7 12.5 %collective-permute-start.18 = (bf16[5,128,128]{2,1,0:T(8,128)(2,1)S(1)}, bf16[5,128,128]{2,1,0:T(8,128)(2,1)S(1)}, u32[]{:S(2)}, u32[]{:S(2)}) collective-permute-start(bf16[5,128,128]{2,1,0:T(8,128)(2,1)S(1)} %get-tuple-element.56), channel_id=1, source_target_pairs={{0,28},{1,29},{2,30},{3,31},{4,0},{5,1},{6,2},{7,3},{8,4},{9,5},{1... | collective-permute-start | bytes 491528 | tf_op jit(solution)/shard_map/ppermute | solution.py:48
  66.5 8.4 %collective-permute-start.14 = (bf16[5,128,128]{2,1,0:T(8,128)(2,1)S(1)}, bf16[5,128,128]{2,1,0:T(8,128)(2,1)S(1)}, u32[]{:S(2)}, u32[]{:S(2)}) collective-permute-start(bf16[5,128,128]{2,1,0:T(8,128)(2,1)S(1)} %get-tuple-element.49), channel_id=1, source_target_pairs={{0,28},{1,29},{2,30},{3,31},{4,0},{5,1},{6,2},{7,3},{8,4},{9,5},{1... | collective-permute-start | bytes 491528 | tf_op jit(solution)/shard_map/ppermute | solution.py:48
  66.6 8.3 %collective-permute-start.15 = (bf16[5,128,128]{2,1,0:T(8,128)(2,1)S(1)}, bf16[5,128,128]{2,1,0:T(8,128)(2,1)S(1)}, u32[]{:S(2)}, u32[]{:S(2)}) collective-permute-start(bf16[5,128,128]{2,1,0:T(8,128)(2,1)S(1)} %get-tuple-element.50), channel_id=1, source_target_pairs={{0,4},{1,5},{2,6},{3,7},{4,8},{5,9},{6,10},{7,11},{8,12},{9,13},{1... | collective-permute-start | bytes 491528 | tf_op jit(solution)/shard_map/ppermute | solution.py:48
  79.6 11.9 %collective-permute-start.25 = (bf16[14,128,128]{2,1,0:T(8,128)(2,1)S(1)}, bf16[14,128,128]{2,1,0:T(8,128)(2,1)S(1)}, u32[]{:S(2)}, u32[]{:S(2)}) collective-permute-start(bf16[14,128,128]{2,1,0:T(8,128)(2,1)S(1)} %get-tuple-element.60.refs_1_), channel_id=1, source_target_pairs={{0,192},{32,224},{64,0},{96,32},{128,64},{160,96},{192,128},{224,1... | collective-permute-start | bytes 1376264 | tf_op jit(solution)/shard_map/ppermute | solution.py:67
  81.9 10.0 %collective-permute-start.21 = (bf16[14,128,128]{2,1,0:T(8,128)(2,1)S(1)}, bf16[14,128,128]{2,1,0:T(8,128)(2,1)S(1)}, u32[]{:S(2)}, u32[]{:S(2)}) collective-permute-start(bf16[14,128,128]{2,1,0:T(8,128)(2,1)S(1)} %get-tuple-element.60.refs_1_), channel_id=1, source_target_pairs={{0,64},{32,96},{64,128},{96,160},{128,192},{160,224},{192,0},{224,... | collective-permute-start | bytes 1376264 | tf_op jit(solution)/shard_map/ppermute | solution.py:67
  81.9 16.5 %collective-permute-start.20 = (bf16[14,128,128]{2,1,0:T(8,128)(2,1)S(1)}, bf16[14,128,128]{2,1,0:T(8,128)(2,1)S(1)}, u32[]{:S(2)}, u32[]{:S(2)}) collective-permute-start(bf16[14,128,128]{2,1,0:T(8,128)(2,1)S(1)} %get-tuple-element.60.refs_1_), channel_id=1, source_target_pairs={{0,32},{32,0},{64,96},{96,64},{128,160},{160,128},{192,224},{224,1... | collective-permute-start | bytes 1376264 | tf_op jit(solution)/shard_map/ppermute | solution.py:71
  101.5 12.7 %collective-permute-start.29 = (bf16[4,128,128]{2,1,0:T(8,128)(2,1)S(1)}, bf16[4,128,128]{2,1,0:T(8,128)(2,1)S(1)}, u32[]{:S(2)}, u32[]{:S(2)}) collective-permute-start(bf16[4,128,128]{2,1,0:T(8,128)(2,1)S(1)} %get-tuple-element.61), channel_id=1, source_target_pairs={{0,28},{1,29},{2,30},{3,31},{4,0},{5,1},{6,2},{7,3},{8,4},{9,5},{1... | collective-permute-start | bytes 393224 | tf_op jit(solution)/shard_map/ppermute | solution.py:48
  105.0 9.3 %collective-permute-start.30 = (bf16[4,128,128]{2,1,0:T(8,128)(2,1)S(1)}, bf16[4,128,128]{2,1,0:T(8,128)(2,1)S(1)}, u32[]{:S(2)}, u32[]{:S(2)}) collective-permute-start(bf16[4,128,128]{2,1,0:T(8,128)(2,1)S(1)} %get-tuple-element.62), channel_id=1, source_target_pairs={{0,4},{1,5},{2,6},{3,7},{4,8},{5,9},{6,10},{7,11},{8,12},{9,13},{1... | collective-permute-start | bytes 393224 | tf_op jit(solution)/shard_map/ppermute | solution.py:48
  105.0 9.3 %collective-permute-start.32 = (bf16[2,128,128]{2,1,0:T(8,128)(2,1)S(1)}, bf16[2,128,128]{2,1,0:T(8,128)(2,1)S(1)}, u32[]{:S(2)}, u32[]{:S(2)}) collective-permute-start(bf16[2,128,128]{2,1,0:T(8,128)(2,1)S(1)} %get-tuple-element.64), channel_id=1, source_target_pairs={{0,8},{1,9},{2,10},{3,11},{4,12},{5,13},{6,14},{7,15},{8,16},{9,17... | collective-permute-start | bytes 196616 | tf_op jit(solution)/shard_map/ppermute | solution.py:48
  114.4 8.4 %collective-permute-start.34 = (bf16[4,128,128]{2,1,0:T(8,128)(2,1)S(1)}, bf16[4,128,128]{2,1,0:T(8,128)(2,1)S(1)}, u32[]{:S(2)}, u32[]{:S(2)}) collective-permute-start(bf16[4,128,128]{2,1,0:T(8,128)(2,1)S(1)} %get-tuple-element.71), channel_id=1, source_target_pairs={{0,31},{1,0},{2,1},{3,2},{4,3},{5,4},{6,5},{7,6},{8,7},{9,8},{10,9... | collective-permute-start | bytes 393224 | tf_op jit(solution)/shard_map/ppermute | solution.py:48
  117.8 8.3 %collective-permute-start.35 = (bf16[4,128,128]{2,1,0:T(8,128)(2,1)S(1)}, bf16[4,128,128]{2,1,0:T(8,128)(2,1)S(1)}, u32[]{:S(2)}, u32[]{:S(2)}) collective-permute-start(bf16[4,128,128]{2,1,0:T(8,128)(2,1)S(1)} %get-tuple-element.72), channel_id=1, source_target_pairs={{0,1},{1,2},{2,3},{3,4},{4,5},{5,6},{6,7},{7,8},{8,9},{9,10},{10,1... | collective-permute-start | bytes 393224 | tf_op jit(solution)/shard_map/ppermute | solution.py:48
  (15 other events, 91.8 us)
